TPU v7x, 128 devices: a whole 4x4x4 slice. The times are simulated.
128 devices in a mesh: group: 8 (over y, core), ingroup: 16 (over z, x).
Axes of the slice: x: 4, y: 4, z: 4, core: 2. Of those that a mesh axis runs over, the one named last changes fastest.
Arguments:
- context: bfloat16 [2048, 8192], P('group', 'ingroup'), may hold values from -6 to 6
- out_proj: bfloat16 [8192, 7168], P('ingroup'), may hold values from -0.0625 to 0.0625
- residual: bfloat16 [2048, 7168], P(('group', 'ingroup')), may hold values from -6 to 6
- norm_gain: float32 [7168], replicated, may hold values from 0.25 to 1.75
- expert_ids: int32 [2048, 8], P(('group', 'ingroup')), may hold values from 0 to 31, as said below
- gates: bfloat16 [2048, 8], P(('group', 'ingroup')), may hold values from 0.099609375 to 1
- gate_proj: bfloat16 [128, 7168, 256], P(('group', 'ingroup')), may hold values from -0.0625 to 0.0625
- up_proj: bfloat16 [128, 7168, 256], P(('group', 'ingroup')), may hold values from -0.0625 to 0.0625
- down_proj: bfloat16 [128, 256, 7168], P(('group', 'ingroup')), may hold values from -0.1875 to 0.1875
Outputs:
- layer_out: bfloat16 [2048, 7168], P(('group', 'ingroup'))
Inputs may be any that keep to these rules, and one draw needn't show every extreme that they name: `expert_ids`: each row names 8 different experts, all of them in at most 4 expert groups, expert e lying in group e // 4.
All inputs are finite; a program needn't handle non-finite values.
Results may differ from a plain program's by a relative error of at most 0.012.
Values may be sent and summed in bfloat16 or wider, within the bound.
No kernel may reach another device: no remote copies, remote signals or barrier semaphores. Data moves between devices by JAX's collectives and lax.ppermute only.
A program may use at most 128 MiB of HBM per device.

v0:
```python
import jax
import jax.numpy as jnp
from jax import lax
from jax.sharding import PartitionSpec as P

TOPK = 8
SLICES = 4


def slice_output(arrived, gate_block, up_block, down_block):
    shape_in = arrived.shape
    flat_rows = arrived.reshape(-1, shape_in[-1])
    gate_part = jnp.dot(flat_rows, gate_block, preferred_element_type=jnp.float32)
    up_part = jnp.dot(flat_rows, up_block, preferred_element_type=jnp.float32)
    activated = (jax.nn.silu(gate_part) * up_part).astype(jnp.bfloat16)
    partial_out = jnp.dot(activated, down_block, preferred_element_type=jnp.float32).astype(
        jnp.bfloat16
    )
    return partial_out.reshape(shape_in[0], shape_in[1], down_block.shape[1])


def local(context, out_proj, residual, norm_gain, expert_ids, gates, gate_proj, up_proj, down_proj):
    group_count = lax.axis_size("group")
    member_count = lax.axis_size("ingroup")
    rows_here = residual.shape[0]
    model_width = residual.shape[1]
    local_experts = member_count // SLICES
    expert_total = group_count * local_experts
    capacity = min(rows_here, max(2, rows_here * TOPK * 5 // (4 * expert_total)))
    attended = lax.psum_scatter(
        jnp.dot(context, out_proj, preferred_element_type=jnp.float32),
        "ingroup",
        scatter_dimension=0,
        tiled=True,
    )
    hidden = (residual.astype(jnp.float32) + attended).astype(jnp.bfloat16)
    hidden_wide = hidden.astype(jnp.float32)
    inverse = lax.rsqrt(jnp.mean(hidden_wide * hidden_wide, axis=1, keepdims=True) + 1e-06)
    normed = (hidden_wide * inverse * norm_gain).astype(jnp.bfloat16)
    expert_iota = jnp.arange(expert_total, dtype=jnp.int32)
    matches = expert_ids[:, :, None] == expert_iota[None, None, :]
    picked = jnp.any(matches, axis=1)
    weighted = jnp.sum(
        jnp.where(matches, gates.astype(jnp.float32)[:, :, None], jnp.float32(0)), axis=1
    )
    gate_block = gate_proj[0]
    up_block = up_proj[0]
    down_block = down_proj[0]
    capacity_iota = jnp.arange(capacity, dtype=jnp.int32)
    picked_grid = picked.reshape(rows_here, group_count, local_experts)
    touched = jnp.any(picked_grid, axis=2).astype(jnp.int32)
    placed_at = jnp.cumsum(touched, axis=0) - touched
    slot_iota = jnp.arange(rows_here, dtype=jnp.int32)
    selector = (touched.T[:, None, :] > 0) & (placed_at.T[:, None, :] == slot_iota[None, :, None])
    selector_half = selector.astype(jnp.bfloat16)
    outgoing = jnp.einsum(
        "gst,td->gsd", selector_half, normed, preferred_element_type=jnp.float32
    ).astype(jnp.bfloat16)
    gate_grid = weighted.reshape(rows_here, group_count, local_experts).astype(jnp.bfloat16)
    outgoing_gates = jnp.einsum(
        "gst,tgl->gsl", selector_half, gate_grid, preferred_element_type=jnp.float32
    ).astype(jnp.bfloat16)
    arrived_rows, arrived_gates = (
        lax.all_to_all(outgoing, "group", split_axis=0, concat_axis=0, tiled=True),
        lax.all_to_all(outgoing_gates, "group", split_axis=0, concat_axis=0, tiled=True),
    )
    wanted = (arrived_gates > 0).astype(jnp.int32)
    relay_rank = jnp.cumsum(wanted, axis=1) - wanted
    relay_admit = (wanted > 0) & (relay_rank < capacity)
    admit_order = relay_admit.transpose(2, 0, 1)
    rank_order = relay_rank.transpose(2, 0, 1)
    placing = admit_order[:, :, None, :] & (
        rank_order[:, :, None, :] == capacity_iota[None, None, :, None]
    )
    placing_half = placing.astype(jnp.bfloat16)
    expert_rows = jnp.einsum(
        "lgcs,gsd->lgcd", placing_half, arrived_rows, preferred_element_type=jnp.float32
    ).astype(jnp.bfloat16)
    expert_rows = expert_rows.reshape(local_experts, group_count * capacity, model_width)
    dispatch = jnp.broadcast_to(
        expert_rows[:, None], (local_experts, SLICES, group_count * capacity, model_width)
    )
    dispatch = dispatch.reshape(member_count, group_count * capacity, model_width)
    returned = lax.all_to_all(
        slice_output(
            lax.all_to_all(dispatch, "ingroup", split_axis=0, concat_axis=0, tiled=True),
            gate_block,
            up_block,
            down_block,
        ),
        "ingroup",
        split_axis=0,
        concat_axis=0,
        tiled=True,
    )
    returned = returned.reshape(local_experts, SLICES, group_count, capacity, model_width)
    scaled = placing_half * arrived_gates.transpose(2, 0, 1)[:, :, None, :]
    group_out = jnp.einsum("lgcs,lugcd->gsd", scaled, returned, preferred_element_type=jnp.float32)
    back_home = lax.all_to_all(group_out, "group", split_axis=0, concat_axis=0, tiled=True)
    group_iota = jnp.arange(group_count, dtype=jnp.int32)
    fetched = back_home[group_iota[:, None], placed_at.T]
    mixture = jnp.sum(jnp.where(touched.T[:, :, None] > 0, fetched, jnp.float32(0)), axis=0)
    return (hidden_wide + mixture).astype(jnp.bfloat16)


def solution(mesh):
    in_specs = (
        P("group", "ingroup"),
        P("ingroup", None),
        P(("group", "ingroup"), None),
        P(),
        P(("group", "ingroup"), None),
        P(("group", "ingroup"), None),
        P(("group", "ingroup"), None, None),
        P(("group", "ingroup"), None, None),
        P(("group", "ingroup"), None, None),
    )
    out_specs = P(("group", "ingroup"), None)
    return jax.shard_map(local, mesh=mesh, in_specs=in_specs, out_specs=out_specs, check_vma=False)
```

profile of v0, /device:TPU:0, one launch (start us, length us, event | category | flops | bytes accessed | tf_op | source)
XLA Modules:
  0.0 460.6 jit_solution(12581569985303994943)
XLA Ops:
  6.5 0.9 copy-done
  7.5 8.1 %fusion.53 = f32[256,7168]{1,0:T(8,128)} fusion(bf16[256,512]{1,0:T(8,128)(2,1)S(1)} %copy-done, bf16[512,7168]{1,0:T(8,128)(2,1)} %param.10), kind=kOutput, calls=%fused_computation.66 | convolution fusion | flops 1879048192 | bytes 14942208 | tf_op jit(solution)/shard_map/dot_general | solution.py:31
  15.7 0.7 copy-done.5
  16.4 0.1 fusion.36
  16.8 0.1 select_reduce_fusion.1
  17.2 0.7 convolution_convert_fusion.3
  17.9 4.6 all-to-all-start
  22.5 78.9 %reduce-scatter.2.cloned.1.call-done = f32[16,7168]{1,0:T(8,128)} async-done(((f32[256,7168]{1,0:T(8,128)}), f32[16,7168]{1,0:T(8,128)}) %reduce-scatter.2.cloned.1.call-update) | async-done | bytes 458768 | tf_op jit(solution)/shard_map/reduce_scatter | solution.py:30
  101.4 1.2 fusion.21
  102.6 1.9 convolution_convert_fusion.2
  104.6 4.3 all-to-all-start.1
  108.9 0.1 copy.65
  109.0 0.7 fusion.52
  109.7 0.1 copy.66
  109.9 23.4 %all-to-all-done.1 = bf16[8,16,7168]{2,1,0:T(8,128)(2,1)S(1)} async-done(((bf16[8,16,7168]{2,1,0:T(8,128)(2,1)}), bf16[8,16,7168]{2,1,0:T(8,128)(2,1)S(1)}, u32[]{:S(2)}, u32[]{:S(2)}) %all-to-all-start.1) | async-done | bytes 1835040 | tf_op jit(solution)/shard_map/all_to_all | solution.py:64
  133.3 1.1 fusion
  134.4 2.0 copy.67
  136.4 2.1 copy.68
  138.5 2.9 broadcast_in_dim.32
  141.3 109.1 %all_to_all.25 = bf16[16,40,7168]{2,1,0:T(8,128)(2,1)S(1)} all-to-all(bf16[16,40,7168]{2,1,0:T(8,128)(2,1)S(1)} %bitcast.62), channel_id=1, replica_groups=mesh['group'=8,'ingroup'=16] {'ingroup'}, dimensions={0} | all-to-all | bytes 18350080 | tf_op jit(solution)/shard_map/all_to_all | solution.py:86
  250.4 3.5 copy-done.2
  253.9 2.5 fusion.5
  256.5 18.9 %convolution_convert_fusion = bf16[640,7168]{1,0:T(8,128)(2,1)} fusion(bf16[1,256,7168]{2,1,0:T(8,128)(2,1)} %param.17, bf16[640,7168]{1,0:T(8,128)(2,1)} %bitcast.60, bf16[1,7168,256]{2,1,0:T(8,128)(2,1)} %param.16, f32[640,256]{1,0:T(8,128)S(1)} %fusion.5), kind=kOutput, calls=%fused_computation.2 | convolution fusion | flops 4703191040 | bytes 26345472 | tf_op jit(solution)/shard_map/dot_general | solution.py:16
  275.4 108.5 %all_to_all.26 = bf16[16,40,7168]{2,1,0:T(8,128)(2,1)S(1)} all-to-all(bf16[16,40,7168]{2,1,0:T(8,128)(2,1)} %bitcast.61), channel_id=1, replica_groups=mesh['group'=8,'ingroup'=16] {'ingroup'}, dimensions={0} | all-to-all | bytes 18350080 | tf_op jit(solution)/shard_map/all_to_all | solution.py:84
  383.9 3.4 convert_reduce_fusion
  387.3 3.4 copy.74
  390.7 4.0 convolution_bitcast_fusion
  394.7 4.5 all-to-all-start.4
  399.3 43.9 %all-to-all-done.4 = f32[8,16,7168]{2,1,0:T(8,128)} async-done(((f32[8,16,7168]{2,1,0:T(8,128)}), f32[8,16,7168]{2,1,0:T(8,128)}, u32[]{:S(2)}, u32[]{:S(2)}) %all-to-all-start.4) | async-done | bytes 3670048 | tf_op jit(solution)/shard_map/all_to_all | solution.py:99
  443.2 7.3 %gather_fusion = f32[128,7168]{1,0:T(8,128)} fusion(f32[8,16,7168]{2,1,0:T(8,128)} %all-to-all-done.4, s32[128]{0:T(128)S(1)} %reshape.44), kind=kCustom, calls=%fused_computation | custom fusion | bytes 7341056 | tf_op jit(solution)/shard_map/gather | solution.py:101
  450.5 2.4 select_reduce_fusion
  453.0 0.7 fusion.24
  (34 shorter events, 0.9 us)
Async XLA Ops:
  6.5 1.0 copy-start
  6.5 94.9 %reduce-scatter.2.cloned.1.call-start = ((), (), s32[]{:S(2)}) async-start(), calls=%async_computation.6 | async-start | bytes 7798784 | tf_op jit(solution)/shard_map/reduce_scatter | solution.py:30
  15.6 0.7 copy-start.5
  15.6 1.1 copy-start.6
  15.6 85.8 %copy-start.3 = (bf16[16,7168]{1,0:T(8,128)(2,1)S(1)}, bf16[16,7168]{1,0:T(8,128)(2,1)}, u32[]{:S(2)}) copy-start(bf16[16,7168]{1,0:T(8,128)(2,1)} %param.11) | copy-start | bytes 688132
  15.6 87.0 %copy-start.4 = (f32[7168]{0:T(1024)S(1)}, f32[7168]{0:T(1024)}, u32[]{:S(2)}) copy-start(f32[7168]{0:T(1024)} %param.12) | copy-start | bytes 86020
  17.9 86.6 %all-to-all-start = ((bf16[8,16,4]{1,2,0:T(4,128)(2,1)}), bf16[8,16,4]{1,2,0:T(4,128)(2,1)S(1)}, u32[]{:S(2)}, u32[]{:S(2)}) async-start(bf16[8,16,4]{1,2,0:T(4,128)(2,1)} %convolution_convert_fusion.3), calls=%async_computation.1 | async-start | bytes 16384 | tf_op jit(solution)/shard_map/all_to_all | solution.py:65
  104.6 28.7 %all-to-all-start.1 = ((bf16[8,16,7168]{2,1,0:T(8,128)(2,1)}), bf16[8,16,7168]{2,1,0:T(8,128)(2,1)S(1)}, u32[]{:S(2)}, u32[]{:S(2)}) async-start(bf16[8,16,7168]{2,1,0:T(8,128)(2,1)} %convolution_convert_fusion.2), calls=%async_computation.2 | async-start | bytes 3670016 | tf_op jit(solution)/shard_map/all_to_all | solution.py:64
  141.3 112.6 %copy-start.7 = (bf16[1,7168,256]{2,1,0:T(8,128)(2,1)S(1)}, bf16[1,7168,256]{2,1,0:T(8,128)(2,1)}, u32[]{:S(2)}) copy-start(bf16[1,7168,256]{2,1,0:T(8,128)(2,1)} %param.15) | copy-start | bytes 11010052
  250.4 3.5 copy-start.2
  394.7 48.6 %all-to-all-start.4 = ((f32[8,16,7168]{2,1,0:T(8,128)}), f32[8,16,7168]{2,1,0:T(8,128)}, u32[]{:S(2)}, u32[]{:S(2)}) async-start(f32[8,16,7168]{2,1,0:T(8,128)} %convolution_bitcast_fusion), calls=%async_computation.5 | async-start | bytes 7340032 | tf_op jit(solution)/shard_map/all_to_all | solution.py:99
  443.2 10.5 %copy-start.1 = (bf16[256,512]{1,0:T(8,128)(2,1)S(1)}, bf16[256,512]{1,0:T(8,128)(2,1)}, u32[]{:S(2)}) copy-start(bf16[256,512]{1,0:T(8,128)(2,1)} %param.9) | copy-start | bytes 786436
Sparse Core Ops, SparseCore 0:
  15.8 85.6 reduce-scatter.1
where the time goes:
time: 462 us; the launch traced here: 461 us
  blocking collectives  218 us (47%)
  waiting for transfers between devices  146 us (32%)
  matrix products  37.3 us (8%)
  local copies, waits for them, and re-layouts  23.8 us (5%)
  between operations  13.5 us (3%)
  starting transfers between devices  13.4 us (3%)
  other arithmetic  8.83 us (2%)
    all_to_all x1, blocking collectives, local(): lax.all_to_all(dispatch, 'ingroup', split_axis=0, concat_axis=0, tiled=True)  109 us
    all_to_all x1, blocking collectives, local(): lax.all_to_all(slice_output(lax.all_to_all(dispatch, 'ingroup', split_axi...  108 us
    reduce_scatter x1, waiting for transfers between devices, local(): lax.psum_scatter(jnp.dot(context, out_proj, preferred_element_type=jnp.fl...  78.9 us
    all_to_all x1, waiting for transfers between devices, local(): lax.all_to_all(group_out, 'group', split_axis=0, concat_axis=0, tiled=True)  43.9 us
    all_to_all x1, waiting for transfers between devices, local(): lax.all_to_all(outgoing, 'group', split_axis=0, concat_axis=0, tiled=True)  23.4 us
    dot_general x1, matrix products, slice_output(): jnp.dot(activated, down_block, preferred_element_type=jnp.float32)  18.9 us
  transfers between devices with their start and end apart: 4, of which 3 were waited for; matrix products, arithmetic and copies ran while one was open for 1% of the time, Pallas kernels for 0%

commit v1 on v0

v1 whole, which is shorter than its diff:
```python
import jax
import jax.numpy as jnp
from jax import lax
from jax.sharding import Mesh
from jax.sharding import PartitionSpec as P

TOPK = 8
SLICES = 4
F32 = jnp.float32
BF16 = jnp.bfloat16


def shift(value, axis, amount):
    size = lax.axis_size(axis)
    return lax.ppermute(value, axis, [(i, (i + amount) % size) for i in range(size)])


def exchange(value, axes):
    return lax.all_to_all(value, axes, split_axis=0, concat_axis=0, tiled=True)


def local(context, out_proj, residual, norm_gain, expert_ids, gates, gate_proj, up_proj, down_proj):
    ny, nc, nz, nx = (lax.axis_size(a) for a in ("y", "c", "z", "x"))
    rows_here, width = residual.shape
    quarter = width // nx
    experts_total = ny * nc * nz
    capacity = min(rows_here, max(2, rows_here * TOPK * 5 // (4 * experts_total)))
    x = lax.axis_index("x")
    c = lax.axis_index("c")

    def cut(k):
        at = lax.rem(x + k, nx) * quarter
        gate_up = jnp.concatenate(
            [
                lax.dynamic_slice(gate_proj[0], (at, 0), (quarter, gate_proj.shape[2])),
                lax.dynamic_slice(up_proj[0], (at, 0), (quarter, up_proj.shape[2])),
            ],
            axis=1,
        )
        down = lax.dynamic_slice(down_proj[0], (0, at), (down_proj.shape[1], quarter))
        return gate_up, down

    pieces = [cut(k) for k in range(nx)]
    gate_up_by = [p[0] if k == 0 else shift(p[0], "x", k) for k, p in enumerate(pieces)]
    down_by = [p[1] if k == 0 else shift(p[1], "x", k) for k, p in enumerate(pieces)]

    meta = jnp.concatenate([expert_ids.astype(BF16), gates], axis=1)
    meta = jnp.pad(meta, ((0, 0), (0, 128 - meta.shape[1])))
    res_out = residual.reshape(rows_here, nx, quarter).transpose(1, 0, 2)
    res_out = jnp.concatenate([res_out, jnp.broadcast_to(meta[None], (nx,) + meta.shape)], axis=2)
    res_in = exchange(res_out, "x").reshape(nx * rows_here, quarter + 128)
    res_quarter = res_in[:, :quarter]
    meta_own = res_in[:, quarter:]
    meta_all = jnp.concatenate([meta_own, shift(meta_own, "c", 1)], axis=0)
    tokens = nc * nx * rows_here
    ids = meta_all[:, :TOPK].astype(jnp.int32)
    gate_vals = meta_all[:, TOPK : 2 * TOPK].astype(F32)

    places = ny * nz
    place = jnp.arange(places, dtype=jnp.int32)
    expert_of = ((place // nz) * nc + c) * nz + lax.rem(place, nz)
    matches = ids[:, :, None] == expert_of[None, None, :]
    picked = jnp.any(matches, axis=1).astype(jnp.int32)
    weighted = jnp.sum(jnp.where(matches, gate_vals[:, :, None], F32(0)), axis=1)
    by_device = picked.reshape(nc * nx, rows_here, places)
    ranking = jnp.cumsum(by_device, axis=1) - by_device
    admitted = (by_device > 0) & (ranking < capacity)
    device_iota = jnp.arange(nc * nx, dtype=jnp.int32)[:, None, None]
    slot = jnp.where(admitted, device_iota * capacity + ranking, -1).reshape(tokens, places)
    slots = nc * nx * capacity
    slot_iota = jnp.arange(slots, dtype=jnp.int32)
    chosen = slot.T[:, None, :] == slot_iota[None, :, None]
    selector = chosen.astype(BF16).reshape(places * slots, tokens)
    scaled = jnp.where(chosen, weighted.T[:, None, :], F32(0)).astype(BF16)
    scaled = scaled.reshape(places * slots, tokens)

    part = jnp.dot(context, out_proj, preferred_element_type=F32).astype(BF16)
    part = exchange(part.reshape(nz, nx * rows_here, width), "z")
    part = jnp.sum(part.astype(F32), axis=0).astype(BF16)
    part = part.reshape(nx * rows_here, nx, quarter).transpose(1, 0, 2)
    part = exchange(part, "x")
    attended = jnp.sum(part.astype(F32), axis=0)
    hidden = (res_quarter.astype(F32) + attended).astype(BF16)
    hidden_wide = hidden.astype(F32)
    square = jnp.sum(hidden_wide * hidden_wide, axis=1, keepdims=True)
    square = square + shift(square, "x", 1) + shift(square, "x", 2) + shift(square, "x", 3)
    inverse = lax.rsqrt(square / width + 1e-06)
    gain = lax.dynamic_slice(norm_gain, (x * quarter,), (quarter,))
    normed = (hidden_wide * inverse * gain[None, :]).astype(BF16)

    normed_all = jnp.concatenate([normed, shift(normed, "c", 1)], axis=0)
    outgoing = jnp.dot(selector, normed_all, preferred_element_type=F32).astype(BF16)
    arrived = exchange(outgoing.reshape(places, slots, quarter), ("y", "z"))
    arrived = arrived.reshape(places * slots, quarter)

    total = None
    for k in (2, 1, 3, 0):
        piece = jnp.dot(arrived, gate_up_by[k], preferred_element_type=F32)
        if k:
            piece = shift(piece.astype(BF16), "x", -k).astype(F32)
        total = piece if total is None else total + piece
    hid = total.shape[1] // 2
    activated = (jax.nn.silu(total[:, :hid]) * total[:, hid:]).astype(BF16)
    result = None
    for k in range(nx):
        block = activated if k == 0 else shift(activated, "x", k)
        piece = jnp.dot(block, down_by[k], preferred_element_type=F32)
        result = piece if result is None else result + piece

    returned = exchange(result.astype(BF16).reshape(places, slots, quarter), ("y", "z"))
    returned = returned.reshape(places * slots, quarter)
    mixture = lax.dot_general(
        scaled, returned, (((0,), (0,)), ((), ())), preferred_element_type=F32
    )
    half = tokens // nc
    mixture = mixture[:half] + shift(mixture[half:], "c", 1)
    out = (hidden_wide + mixture).astype(BF16)
    out = exchange(out.reshape(nx, rows_here, quarter), "x")
    return out.transpose(1, 0, 2).reshape(rows_here, width)


def solution(mesh):
    y = 4
    grid = Mesh(mesh.devices.reshape(y, 2, 4, 4), ("y", "c", "z", "x"))
    group, member = ("y", "c"), ("z", "x")
    owner = group + member
    in_specs = (
        P(group, member),
        P(member, None),
        P(owner, None),
        P(),
        P(owner, None),
        P(owner, None),
        P(owner, None, None),
        P(owner, None, None),
        P(owner, None, None),
    )
    return jax.shard_map(
        local, mesh=grid, in_specs=in_specs, out_specs=P(owner, None), check_vma=False
    )
```

time: 462 us -> 326 us (0.71)
  blocking collectives: 218 us -> 9.27 us
  waiting for transfers between devices: 146 us -> 229 us
  starting transfers between devices: 13.4 us -> 43.5 us
  between operations: 13.5 us -> 0.45 us
  matrix products: 37.3 us -> 24.3 us
  local copies, waits for them, and re-layouts: 23.8 us -> 11 us
    all_to_all x2 -> x1, blocking collectives: 218 us -> 9.27 us  [exchange(): return lax.all_to_all(value, axes, split_axis=0, concat_axis=0, tiled=True)]
    ppermute x0 -> x18, waiting for transfers between devices: none -> 143 us  [shift(): lax.ppermute(value, axis, [(i, (i + amount) % size) for i in range(size)])]
    reduce_scatter x1 -> x0, waiting for transfers between devices: 78.9 us -> none  [local(): lax.psum_scatter(jnp.dot(context, out_proj, preferred_element_type=jnp.fl...]
    all_to_all x3 -> x5, waiting for transfers between devices: 67.3 us -> 85.5 us  [exchange(): return lax.all_to_all(value, axes, split_axis=0, concat_axis=0, tiled=True)]
    ppermute x0 -> x18, starting transfers between devices: none -> 18 us  [shift(): lax.ppermute(value, axis, [(i, (i + amount) % size) for i in range(size)])]
    dot_general x7 -> x11, matrix products: 37.3 us -> 24.3 us  [the longest x4 10 us: local(): piece = jnp.dot(arrived, gate_up_by[k], preferred_element_type=F32)]
    all_to_all x3 -> x5, starting transfers between devices: 13.4 us -> 25.5 us  [exchange(): return lax.all_to_all(value, axes, split_axis=0, concat_axis=0, tiled=True)]
    unnamed x18, local copies, waits for them, and re-layouts: 8.63 us -> 1.17 us
  transfers between devices with their start and end apart: 4 -> 23, of which waited for: 3 -> 15; matrix products, arithmetic and copies ran while one was open for 1% -> 9% of each run, Pallas kernels for 0% -> 0%
where the time goes in v1:
time: 326 us; the launch traced here: 325 us
  waiting for transfers between devices  229 us (70%)
  starting transfers between devices  43.5 us (13%)
  matrix products  24.3 us (7%)
  local copies, waits for them, and re-layouts  11 us (3%)
  blocking collectives  9.27 us (3%)
  other arithmetic  7.99 us (2%)
    ppermute x18, waiting for transfers between devices, shift(): lax.ppermute(value, axis, [(i, (i + amount) % size) for i in range(size)])  143 us
    all_to_all x5, waiting for transfers between devices, exchange(): return lax.all_to_all(value, axes, split_axis=0, concat_axis=0, tiled=True)  85.5 us
    all_to_all x5, starting transfers between devices, exchange(): return lax.all_to_all(value, axes, split_axis=0, concat_axis=0, tiled=True)  25.5 us
    ppermute x18, starting transfers between devices, shift(): lax.ppermute(value, axis, [(i, (i + amount) % size) for i in range(size)])  18 us
    dot_general x4, matrix products, local(): piece = jnp.dot(arrived, gate_up_by[k], preferred_element_type=F32)  10 us
    all_to_all x1, blocking collectives, exchange(): return lax.all_to_all(value, axes, split_axis=0, concat_axis=0, tiled=True)  9.27 us
    dot_general x1, matrix products, local(): part = jnp.dot(context, out_proj, preferred_element_type=F32).astype(BF16)  7.01 us
  transfers between devices with their start and end apart: 23, of which 15 were waited for; matrix products, arithmetic and copies ran while one was open for 9% of the time, Pallas kernels for 0%

profile of v1, /device:TPU:0, one launch (start us, length us, event | category | flops | bytes accessed | tf_op | source)
XLA Modules:
  0.0 325.3 jit_solution(120596896749609046)
XLA Ops:
  1.0 7.0 %convolution_convert_fusion = bf16[256,7168]{1,0:T(8,128)(2,1)} fusion(bf16[256,512]{1,0:T(8,128)(2,1)S(1)} %copy-done, bf16[512,7168]{1,0:T(8,128)(2,1)} %param.10), kind=kOutput, calls=%fused_computation | convolution fusion | flops 1880883200 | bytes 11272192 | tf_op jit(solution)/shard_map/dot_general | solution.py:77
  8.0 5.5 %all-to-all-start.1 = ((bf16[4,64,7168]{2,1,0:T(8,128)(2,1)}), bf16[4,64,7168]{2,1,0:T(8,128)(2,1)}, u32[]{:S(2)}, u32[]{:S(2)}) async-start(bf16[4,64,7168]{2,1,0:T(8,128)(2,1)} %bitcast.71), calls=%async_computation.1 | async-start | bytes 7340032 | tf_op jit(solution)/shard_map/all_to_all | solution.py:19
  14.6 42.6 %all-to-all-done.1 = bf16[4,64,7168]{2,1,0:T(8,128)(2,1)} async-done(((bf16[4,64,7168]{2,1,0:T(8,128)(2,1)}), bf16[4,64,7168]{2,1,0:T(8,128)(2,1)}, u32[]{:S(2)}, u32[]{:S(2)}) %all-to-all-start.1) | async-done | bytes 3670048 | tf_op jit(solution)/shard_map/all_to_all | solution.py:19
  57.2 4.3 %all-to-all-start = ((bf16[4,16,1920]{2,1,0:T(8,128)(2,1)}), bf16[4,16,1920]{2,1,0:T(8,128)(2,1)S(1)}, u32[]{:S(2)}, u32[]{:S(2)}) async-start(bf16[4,16,1920]{2,1,0:T(8,128)(2,1)} %copy.57), calls=%async_computation | async-start | bytes 491520 | tf_op jit(solution)/shard_map/all_to_all | solution.py:19
  61.5 2.8 reduce_sum.39
  66.0 2.1 all-to-all-done
  68.1 3.5 %all-to-all-start.2 = ((bf16[4,64,1792]{2,1,0:T(8,128)(2,1)}), bf16[4,64,1792]{2,1,0:T(8,128)(2,1)S(1)}, u32[]{:S(2)}, u32[]{:S(2)}) async-start(bf16[4,64,1792]{2,1,0:T(8,128)(2,1)} %copy.58), calls=%async_computation.2 | async-start | bytes 1835008 | tf_op jit(solution)/shard_map/all_to_all | solution.py:19
  73.2 10.0 %all-to-all-done.2 = bf16[4,64,1792]{2,1,0:T(8,128)(2,1)S(1)} async-done(((bf16[4,64,1792]{2,1,0:T(8,128)(2,1)}), bf16[4,64,1792]{2,1,0:T(8,128)(2,1)S(1)}, u32[]{:S(2)}, u32[]{:S(2)}) %all-to-all-start.2) | async-done | bytes 917536 | tf_op jit(solution)/shard_map/all_to_all | solution.py:19
  84.2 2.7 collective-permute-start.3
  87.1 1.6 collective-permute-done.2
  88.7 2.9 collective-permute-done.1
  93.3 2.2 convolution_convert_fusion.1
  95.5 5.2 %all-to-all-start.3 = ((bf16[16,40,1792]{2,1,0:T(8,128)(2,1)}), bf16[16,40,1792]{2,1,0:T(8,128)(2,1)S(1)}, u32[]{:S(2)}, u32[]{:S(2)}) async-start(bf16[16,40,1792]{2,1,0:T(8,128)(2,1)} %bitcast.9), calls=%async_computation.3 | async-start | bytes 4587520 | tf_op jit(solution)/shard_map/all_to_all | solution.py:19
  100.7 4.9 %dynamic-slice_bitcast_fusion.9 = (bf16[1792,256]{1,0:T(8,128)(2,1)S(1)}, bf16[1792,256]{1,0:T(8,128)(2,1)S(1)}, bf16[1792,256]{1,0:T(8,128)(2,1)}, bf16[1792,25...) fusion(bf16[1,7168,256]{2,1,0:T(8,128)(2,1)} %param.16, ...), kind=kLoop, calls=%fused_computation.28 | loop fusion | bytes 14680080 | tf_op jit(solution)/shard_map/dynamic_slice | solution.py:36
  107.3 2.0 collective-permute-start.7
  110.7 38.1 %collective-permute-done.9 = bf16[1792,512]{1,0:T(8,128)(2,1)} collective-permute-done((bf16[1792,512]{1,0:T(8,128)(2,1)S(1)}, bf16[1792,512]{1,0:T(8,128)(2,1)}, u32[]{:S(2)}, u32[]{:S(2)}) %collective-permute-start.9) | collective-permute-done | bytes 1835040 | tf_op jit(solution)/shard_map/ppermute | solution.py:15
  148.9 2.8 convolution_convert_fusion.2
  151.8 39.2 %collective-permute-done.7 = bf16[1792,512]{1,0:T(8,128)(2,1)} collective-permute-done((bf16[1792,512]{1,0:T(8,128)(2,1)}, bf16[1792,512]{1,0:T(8,128)(2,1)}, u32[]{:S(2)}, u32[]{:S(2)}) %collective-permute-start.7) | collective-permute-done | bytes 1835040 | tf_op jit(solution)/shard_map/ppermute | solution.py:15
  191.0 2.8 convolution_convert_fusion.3
  194.1 3.0 convolution_convert_fusion.4
  197.5 1.9 collective-permute-start.12
  199.4 2.7 collective-permute-start.16
  203.5 15.5 %collective-permute-done.10 = bf16[640,512]{1,0:T(8,128)(2,1)S(1)} collective-permute-done((bf16[640,512]{1,0:T(8,128)(2,1)S(1)}, bf16[640,512]{1,0:T(8,128)(2,1)S(1)}, u32[]{:S(2)}, u32[]{:S(2)}) %collective-permute-start.10) | collective-permute-done | bytes 655392 | tf_op jit(solution)/shard_map/ppermute | solution.py:15
  219.0 2.4 collective-permute-done.8
  221.9 7.3 %collective-permute-start.15 = (bf16[640,256]{1,0:T(8,128)(2,1)S(1)}, bf16[640,256]{1,0:T(8,128)(2,1)S(1)}, u32[]{:S(2)}, u32[]{:S(2)}) collective-permute-start(bf16[640,256]{1,0:T(8,128)(2,1)S(1)} %fusion.7), channel_id=1, source_target_pairs={{0,3},{1,0},{2,1},{3,2},{4,7},{5,4},{6,5},{7,6},{8,11},{9,8},{10,9... | collective-permute-start | bytes 983048 | tf_op jit(solution)/shard_map/ppermute | solution.py:15
  229.9 28.4 %collective-permute-done.12 = bf16[256,1792]{1,0:T(8,128)(2,1)S(1)} collective-permute-done((bf16[256,1792]{1,0:T(8,128)(2,1)S(1)}, bf16[256,1792]{1,0:T(8,128)(2,1)S(1)}, u32[]{:S(2)}, u32[]{:S(2)}) %collective-permute-start.12) | collective-permute-done | bytes 917536 | tf_op jit(solution)/shard_map/ppermute | solution.py:15
  258.3 12.9 %collective-permute-done.11 = bf16[640,256]{1,0:T(8,128)(2,1)S(1)} collective-permute-done((bf16[640,256]{1,0:T(8,128)(2,1)S(1)}, bf16[640,256]{1,0:T(8,128)(2,1)S(1)}, u32[]{:S(2)}, u32[]{:S(2)}) %collective-permute-start.11) | collective-permute-done | bytes 327712 | tf_op jit(solution)/shard_map/ppermute | solution.py:15
  272.8 2.2 add_convert_fusion
  275.0 6.9 %all-to-all-start.4 = ((bf16[16,40,1792]{2,1,0:T(8,128)(2,1)}), bf16[16,40,1792]{2,1,0:T(8,128)(2,1)S(1)}, u32[]{:S(2)}, u32[]{:S(2)}) async-start(bf16[16,40,1792]{2,1,0:T(8,128)(2,1)} %bitcast.70), calls=%async_computation.4 | async-start | bytes 4587520 | tf_op jit(solution)/shard_map/all_to_all | solution.py:19
  282.1 30.7 %all-to-all-done.4 = bf16[16,40,1792]{2,1,0:T(8,128)(2,1)S(1)} async-done(((bf16[16,40,1792]{2,1,0:T(8,128)(2,1)}), bf16[16,40,1792]{2,1,0:T(8,128)(2,1)S(1)}, u32[]{:S(2)}, u32[]{:S(2)}) %all-to-all-start.4) | async-done | bytes 2293792 | tf_op jit(solution)/shard_map/all_to_all | solution.py:19
  313.5 1.8 collective-permute-done.17
  315.3 9.3 %all_to_all.30 = bf16[4,16,1792]{2,1,0:T(8,128)(2,1)S(1)} all-to-all(bf16[4,16,1792]{2,1,0:T(8,128)(2,1)S(1)} %bitcast.81), channel_id=1, replica_groups=mesh['y'=4,'c'=2,'z'=4,'x'=4] {'x'}, dimensions={0} | all-to-all | bytes 458752 | tf_op jit(solution)/shard_map/all_to_all | solution.py:19
  (87 shorter events, 17.5 us)
Async XLA Ops:
  0.0 1.0 copy-start
  8.0 5.5 %copy-start.6 = (s32[16,8]{0,1:T(8,128)S(1)}, s32[16,8]{0,1:T(8,128)}, u32[]{:S(2)}) copy-start(s32[16,8]{0,1:T(8,128)} %param.13) | copy-start | bytes 1540
  8.0 5.5 %copy-start.7 = (bf16[16,8]{0,1:T(8,128)(2,1)S(1)}, bf16[16,8]{0,1:T(8,128)(2,1)}, u32[]{:S(2)}) copy-start(bf16[16,8]{0,1:T(8,128)(2,1)} %param.14) | copy-start | bytes 772
  8.0 5.6 %copy-start.5 = (bf16[16,7168]{1,0:T(8,128)(2,1)S(1)}, bf16[16,7168]{1,0:T(8,128)(2,1)}, u32[]{:S(2)}) copy-start(bf16[16,7168]{1,0:T(8,128)(2,1)} %param.11) | copy-start | bytes 688132
  8.0 49.3 %all-to-all-start.1 = ((bf16[4,64,7168]{2,1,0:T(8,128)(2,1)}), bf16[4,64,7168]{2,1,0:T(8,128)(2,1)}, u32[]{:S(2)}, u32[]{:S(2)}) async-start(bf16[4,64,7168]{2,1,0:T(8,128)(2,1)} %bitcast.71), calls=%async_computation.1 | async-start | bytes 7340032 | tf_op jit(solution)/shard_map/all_to_all | solution.py:19
  57.2 10.9 %all-to-all-start = ((bf16[4,16,1920]{2,1,0:T(8,128)(2,1)}), bf16[4,16,1920]{2,1,0:T(8,128)(2,1)S(1)}, u32[]{:S(2)}, u32[]{:S(2)}) async-start(bf16[4,16,1920]{2,1,0:T(8,128)(2,1)} %copy.57), calls=%async_computation | async-start | bytes 491520 | tf_op jit(solution)/shard_map/all_to_all | solution.py:19
  68.1 15.1 %all-to-all-start.2 = ((bf16[4,64,1792]{2,1,0:T(8,128)(2,1)}), bf16[4,64,1792]{2,1,0:T(8,128)(2,1)S(1)}, u32[]{:S(2)}, u32[]{:S(2)}) async-start(bf16[4,64,1792]{2,1,0:T(8,128)(2,1)} %copy.58), calls=%async_computation.2 | async-start | bytes 1835008 | tf_op jit(solution)/shard_map/all_to_all | solution.py:19
  71.8 1.3 collective-permute-start
  83.5 5.1 %collective-permute-start.2 = (f32[64,1]{0,1:T(1,128)S(1)}, f32[64,1]{0,1:T(1,128)S(1)}, u32[]{:S(2)}, u32[]{:S(2)}) collective-permute-start(f32[64,1]{0,1:T(1,128)S(1)} %bitcast.83), channel_id=1, source_target_pairs={{0,2},{1,3},{2,0},{3,1},{4,6},{5,7},{6,4},{7,5},{8,10},{9,11},{10,... | collective-permute-start | bytes 776 | tf_op jit(solution)/shard_map/ppermute | solution.py:15
  84.2 4.5 %collective-permute-start.3 = (f32[64,1]{0,1:T(1,128)S(1)}, f32[64,1]{0,1:T(1,128)S(1)}, u32[]{:S(2)}, u32[]{:S(2)}) collective-permute-start(f32[64,1]{0,1:T(1,128)S(1)} %bitcast.84), channel_id=1, source_target_pairs={{0,3},{1,0},{2,1},{3,2},{4,7},{5,4},{6,5},{7,6},{8,11},{9,8},{10,9... | collective-permute-start | bytes 776 | tf_op jit(solution)/shard_map/ppermute | solution.py:15
  86.9 4.8 %collective-permute-start.1 = (f32[64,1]{0,1:T(1,128)S(1)}, f32[64,1]{0,1:T(1,128)S(1)}, u32[]{:S(2)}, u32[]{:S(2)}) collective-permute-start(f32[64,1]{0,1:T(1,128)S(1)} %bitcast.85), channel_id=1, source_target_pairs={{0,1},{1,2},{2,3},{3,0},{4,5},{5,6},{6,7},{7,4},{8,9},{9,10},{10,1... | collective-permute-start | bytes 776 | tf_op jit(solution)/shard_map/ppermute | solution.py:15
  91.7 1.6 collective-permute-start.4
  95.5 53.4 %all-to-all-start.3 = ((bf16[16,40,1792]{2,1,0:T(8,128)(2,1)}), bf16[16,40,1792]{2,1,0:T(8,128)(2,1)S(1)}, u32[]{:S(2)}, u32[]{:S(2)}) async-start(bf16[16,40,1792]{2,1,0:T(8,128)(2,1)} %bitcast.9), calls=%async_computation.3 | async-start | bytes 4587520 | tf_op jit(solution)/shard_map/all_to_all | solution.py:19
  105.8 43.1 %collective-permute-start.9 = (bf16[1792,512]{1,0:T(8,128)(2,1)S(1)}, bf16[1792,512]{1,0:T(8,128)(2,1)}, u32[]{:S(2)}, u32[]{:S(2)}) collective-permute-start(bf16[1792,512]{1,0:T(8,128)(2,1)S(1)} %pad_maximum_fusion.2), channel_id=1, source_target_pairs={{0,3},{1,0},{2,1},{3,2},{4,7},{5,4},{6,5},{7,6},{8,11},{9,8},{10,9... | collective-permute-start | bytes 5505032 | tf_op jit(solution)/shard_map/ppermute | solution.py:15
  107.3 83.7 %collective-permute-start.7 = (bf16[1792,512]{1,0:T(8,128)(2,1)}, bf16[1792,512]{1,0:T(8,128)(2,1)}, u32[]{:S(2)}, u32[]{:S(2)}) collective-permute-start(bf16[1792,512]{1,0:T(8,128)(2,1)} %pad_maximum_fusion.1), channel_id=1, source_target_pairs={{0,1},{1,2},{2,3},{3,0},{4,5},{5,6},{6,7},{7,4},{8,9},{9,10},{10,1... | collective-permute-start | bytes 5505032 | tf_op jit(solution)/shard_map/ppermute | solution.py:15
  110.7 83.4 %collective-permute-start.5 = (bf16[1792,512]{1,0:T(8,128)(2,1)}, bf16[1792,512]{1,0:T(8,128)(2,1)}, u32[]{:S(2)}, u32[]{:S(2)}) collective-permute-start(bf16[1792,512]{1,0:T(8,128)(2,1)} %pad_maximum_fusion), channel_id=1, source_target_pairs={{0,2},{1,3},{2,0},{3,1},{4,6},{5,7},{6,4},{7,5},{8,10},{9,11},{10,... | collective-permute-start | bytes 5505032 | tf_op jit(solution)/shard_map/ppermute | solution.py:15
  151.7 67.3 %collective-permute-start.10 = (bf16[640,512]{1,0:T(8,128)(2,1)S(1)}, bf16[640,512]{1,0:T(8,128)(2,1)S(1)}, u32[]{:S(2)}, u32[]{:S(2)}) collective-permute-start(bf16[640,512]{1,0:T(8,128)(2,1)S(1)} %convolution_convert_fusion.2), channel_id=1, source_target_pairs={{0,1},{1,2},{2,3},{3,0},{4,5},{5,6},{6,7},{7,4},{8,9},{9,10},{10,1... | collective-permute-start | bytes 1966088 | tf_op jit(solution)/shard_map/ppermute | solution.py:15
  193.8 3.4 %copy-start.2 = (bf16[1,256,7168]{2,1,0:T(8,128)(2,1)S(1)}, bf16[1,256,7168]{2,1,0:T(8,128)(2,1)}, u32[]{:S(2)}) copy-start(bf16[1,256,7168]{2,1,0:T(8,128)(2,1)} %param.17) | copy-start | bytes 11010052
  193.9 27.5 %collective-permute-start.8 = (bf16[640,512]{1,0:T(8,128)(2,1)S(1)}, bf16[640,512]{1,0:T(8,128)(2,1)S(1)}, u32[]{:S(2)}, u32[]{:S(2)}) collective-permute-start(bf16[640,512]{1,0:T(8,128)(2,1)S(1)} %convolution_convert_fusion.3), channel_id=1, source_target_pairs={{0,3},{1,0},{2,1},{3,2},{4,7},{5,4},{6,5},{7,6},{8,11},{9,8},{10,9... | collective-permute-start | bytes 1966088 | tf_op jit(solution)/shard_map/ppermute | solution.py:15
  197.1 5.0 %copy-start.3 = (bf16[1792,256]{1,0:T(8,128)(2,1)S(1)}, bf16[1792,256]{1,0:T(8,128)(2,1)}, u32[]{:S(2)}) copy-start(bf16[1792,256]{1,0:T(8,128)(2,1)} %get-tuple-element.16) | copy-start | bytes 2752516
  197.1 5.0 %copy-start.4 = (bf16[1792,256]{1,0:T(8,128)(2,1)S(1)}, bf16[1792,256]{1,0:T(8,128)(2,1)}, u32[]{:S(2)}) copy-start(bf16[1792,256]{1,0:T(8,128)(2,1)} %get-tuple-element.21) | copy-start | bytes 2752516
  197.1 24.2 %collective-permute-start.6 = (bf16[640,512]{1,0:T(8,128)(2,1)S(1)}, bf16[640,512]{1,0:T(8,128)(2,1)S(1)}, u32[]{:S(2)}, u32[]{:S(2)}) collective-permute-start(bf16[640,512]{1,0:T(8,128)(2,1)S(1)} %convolution_convert_fusion.4), channel_id=1, source_target_pairs={{0,2},{1,3},{2,0},{3,1},{4,6},{5,7},{6,4},{7,5},{8,10},{9,11},{10,... | collective-permute-start | bytes 1966088 | tf_op jit(solution)/shard_map/ppermute | solution.py:15
  197.5 60.8 %collective-permute-start.12 = (bf16[256,1792]{1,0:T(8,128)(2,1)S(1)}, bf16[256,1792]{1,0:T(8,128)(2,1)S(1)}, u32[]{:S(2)}, u32[]{:S(2)}) collective-permute-start(bf16[256,1792]{1,0:T(8,128)(2,1)S(1)} %get-tuple-element.7), channel_id=1, source_target_pairs={{0,1},{1,2},{2,3},{3,0},{4,5},{5,6},{6,7},{7,4},{8,9},{9,10},{10,1... | collective-permute-start | bytes 2752520 | tf_op jit(solution)/shard_map/ppermute | solution.py:15
  199.4 73.4 %collective-permute-start.16 = (bf16[256,1792]{1,0:T(8,128)(2,1)S(1)}, bf16[256,1792]{1,0:T(8,128)(2,1)S(1)}, u32[]{:S(2)}, u32[]{:S(2)}) collective-permute-start(bf16[256,1792]{1,0:T(8,128)(2,1)S(1)} %get-tuple-element.8), channel_id=1, source_target_pairs={{0,3},{1,0},{2,1},{3,2},{4,7},{5,4},{6,5},{7,6},{8,11},{9,8},{10,9... | collective-permute-start | bytes 2752520 | tf_op jit(solution)/shard_map/ppermute | solution.py:15
  219.0 53.0 %collective-permute-start.14 = (bf16[256,1792]{1,0:T(8,128)(2,1)S(1)}, bf16[256,1792]{1,0:T(8,128)(2,1)S(1)}, u32[]{:S(2)}, u32[]{:S(2)}) collective-permute-start(bf16[256,1792]{1,0:T(8,128)(2,1)S(1)} %get-tuple-element.9), channel_id=1, source_target_pairs={{0,2},{1,3},{2,0},{3,1},{4,6},{5,7},{6,4},{7,5},{8,10},{9,11},{10,... | collective-permute-start | bytes 2752520 | tf_op jit(solution)/shard_map/ppermute | solution.py:15
  221.9 50.9 %collective-permute-start.15 = (bf16[640,256]{1,0:T(8,128)(2,1)S(1)}, bf16[640,256]{1,0:T(8,128)(2,1)S(1)}, u32[]{:S(2)}, u32[]{:S(2)}) collective-permute-start(bf16[640,256]{1,0:T(8,128)(2,1)S(1)} %fusion.7), channel_id=1, source_target_pairs={{0,3},{1,0},{2,1},{3,2},{4,7},{5,4},{6,5},{7,6},{8,11},{9,8},{10,9... | collective-permute-start | bytes 983048 | tf_op jit(solution)/shard_map/ppermute | solution.py:15
  229.1 42.1 %collective-permute-start.11 = (bf16[640,256]{1,0:T(8,128)(2,1)S(1)}, bf16[640,256]{1,0:T(8,128)(2,1)S(1)}, u32[]{:S(2)}, u32[]{:S(2)}) collective-permute-start(bf16[640,256]{1,0:T(8,128)(2,1)S(1)} %fusion.7), channel_id=1, source_target_pairs={{0,1},{1,2},{2,3},{3,0},{4,5},{5,6},{6,7},{7,4},{8,9},{9,10},{10,1... | collective-permute-start | bytes 983048 | tf_op jit(solution)/shard_map/ppermute | solution.py:15
  258.3 13.7 %collective-permute-start.13 = (bf16[640,256]{1,0:T(8,128)(2,1)S(1)}, bf16[640,256]{1,0:T(8,128)(2,1)S(1)}, u32[]{:S(2)}, u32[]{:S(2)}) collective-permute-start(bf16[640,256]{1,0:T(8,128)(2,1)S(1)} %fusion.7), channel_id=1, source_target_pairs={{0,2},{1,3},{2,0},{3,1},{4,6},{5,7},{6,4},{7,5},{8,10},{9,11},{10,... | collective-permute-start | bytes 983048 | tf_op jit(solution)/shard_map/ppermute | solution.py:15
  275.0 37.7 %all-to-all-start.4 = ((bf16[16,40,1792]{2,1,0:T(8,128)(2,1)}), bf16[16,40,1792]{2,1,0:T(8,128)(2,1)S(1)}, u32[]{:S(2)}, u32[]{:S(2)}) async-start(bf16[16,40,1792]{2,1,0:T(8,128)(2,1)} %bitcast.70), calls=%async_computation.4 | async-start | bytes 4587520 | tf_op jit(solution)/shard_map/all_to_all | solution.py:19
  312.8 12.5 %copy-start.1 = (bf16[256,512]{1,0:T(8,128)(2,1)S(1)}, bf16[256,512]{1,0:T(8,128)(2,1)}, u32[]{:S(2)}) copy-start(bf16[256,512]{1,0:T(8,128)(2,1)} %param.9) | copy-start | bytes 786436
  313.4 1.9 collective-permute-start.17

commit v2 on v1

v2 whole, which is shorter than its diff:
```python
import jax
import jax.numpy as jnp
from jax import lax
from jax.experimental import pallas as pl
from jax.experimental.pallas import tpu as pltpu
from jax.sharding import Mesh
from jax.sharding import PartitionSpec as P

TOPK = 8
F32 = jnp.float32
BF16 = jnp.bfloat16


def shift(value, axis, amount):
    size = lax.axis_size(axis)
    return lax.ppermute(value, axis, [(i, (i + amount) % size) for i in range(size)])


def exchange(value, axes):
    return lax.all_to_all(value, axes, split_axis=0, concat_axis=0, tiled=True)


def mate_of(c, x):
    return x ^ 1 if c == 0 else x ^ 3


def twin_of(c, x):
    return x ^ 3 if c == 0 else x ^ 1


def from_places(value, source):
    pairs = []
    for c in range(2):
        for x in range(4):
            sc, sx = source(c, x)
            pairs.append((sc * 4 + sx, c * 4 + x))
    return lax.ppermute(value, ("c", "x"), pairs)


def project_body(mine_ref, a_ref, b_ref, r_ref, o_ref, acc_ref):
    own = r_ref.shape[0]
    acc_ref[...] = jnp.dot(a_ref[...], b_ref[...], preferred_element_type=F32)
    here = pl.ds(pl.multiple_of(mine_ref[0] * own, own), own)
    acc_ref[here, :] += r_ref[...].astype(F32)
    o_ref[0] = acc_ref[...].astype(BF16)


def project(mine, context, weight, residual, blocks):
    rows, depth = context.shape
    own, width = residual.shape
    cut = width // blocks
    halves = 2
    step = cut // halves
    return pl.pallas_call(
        project_body,
        out_shape=jax.ShapeDtypeStruct((blocks, rows, cut), BF16),
        grid_spec=pltpu.PrefetchScalarGridSpec(
            num_scalar_prefetch=1,
            grid=(blocks, halves),
            in_specs=[
                pl.BlockSpec((rows, depth), lambda q, j, m: (0, 0)),
                pl.BlockSpec((depth, step), lambda q, j, m: (0, q * halves + j)),
                pl.BlockSpec((own, step), lambda q, j, m: (0, q * halves + j)),
            ],
            out_specs=pl.BlockSpec((1, rows, step), lambda q, j, m: (q, 0, j)),
            scratch_shapes=[pltpu.VMEM((rows, step), F32)],
        ),
        compiler_params=pltpu.CompilerParams(vmem_limit_bytes=56 << 20),
        cost_estimate=pl.CostEstimate(
            flops=2 * rows * depth * width,
            bytes_accessed=2 * (rows * depth + depth * width + rows * width),
            transcendentals=0,
        ),
    )(mine, context, weight, residual)


def first_body(a_ref, gain_ref, w_ref, g_ref, s_ref, o_ref, acc_ref, sq_ref):
    step = pl.program_id(0)

    @pl.when(step == 0)
    def _():
        acc_ref[...] = jnp.zeros_like(acc_ref)
        sq_ref[...] = jnp.zeros_like(sq_ref)

    wide = a_ref[...].astype(F32)
    squares = wide * wide
    lanes = sq_ref.shape[1]
    partial = squares[:, :lanes]
    for i in range(1, squares.shape[1] // lanes):
        partial += squares[:, i * lanes : (i + 1) * lanes]
    sq_ref[...] += partial
    gained = (wide * gain_ref[...]).astype(BF16)
    g_ref[...] = gained
    acc_ref[...] += jnp.dot(gained, w_ref[...], preferred_element_type=F32)

    @pl.when(step == pl.num_programs(0) - 1)
    def _():
        o_ref[...] = acc_ref[...].astype(BF16)
        s_ref[...] = jnp.sum(sq_ref[...], axis=1, keepdims=True)


def first_product(arrived, gain, weight):
    rows, depth = arrived.shape
    cols = weight.shape[1]
    step = 512
    return pl.pallas_call(
        first_body,
        out_shape=(
            jax.ShapeDtypeStruct((rows, depth), BF16),
            jax.ShapeDtypeStruct((rows, 1), F32),
            jax.ShapeDtypeStruct((rows, cols), BF16),
        ),
        grid=(depth // step,),
        in_specs=[
            pl.BlockSpec((rows, step), lambda k: (0, k)),
            pl.BlockSpec((1, step), lambda k: (0, k)),
            pl.BlockSpec((step, cols), lambda k: (k, 0)),
        ],
        out_specs=(
            pl.BlockSpec((rows, step), lambda k: (0, k)),
            pl.BlockSpec((rows, 1), lambda k: (0, 0)),
            pl.BlockSpec((rows, cols), lambda k: (0, 0)),
        ),
        scratch_shapes=[pltpu.VMEM((rows, cols), F32), pltpu.VMEM((rows, 128), F32)],
        compiler_params=pltpu.CompilerParams(vmem_limit_bytes=24 << 20),
        cost_estimate=pl.CostEstimate(
            flops=2 * rows * depth * cols,
            bytes_accessed=2 * (2 * rows * depth + depth * cols + rows * cols),
            transcendentals=0,
        ),
    )(arrived, gain[None, :], weight)


def pack_body(at_ref, g_ref, u_ref, o_ref):
    h = g_ref.shape[2]
    o_ref[:, :h] = g_ref[0]
    o_ref[:, h:] = u_ref[0]


def pack(at, gate, up):
    deep, h = gate.shape[1:]
    cut = deep // 4
    steps = at.shape[0]
    return pl.pallas_call(
        pack_body,
        out_shape=jax.ShapeDtypeStruct((steps * cut, 2 * h), BF16),
        grid_spec=pltpu.PrefetchScalarGridSpec(
            num_scalar_prefetch=1,
            grid=(steps,),
            in_specs=[
                pl.BlockSpec((1, cut, h), lambda i, at: (0, at[i], 0)),
                pl.BlockSpec((1, cut, h), lambda i, at: (0, at[i], 0)),
            ],
            out_specs=pl.BlockSpec((cut, 2 * h), lambda i, at: (i, 0)),
        ),
        compiler_params=pltpu.CompilerParams(vmem_limit_bytes=56 << 20),
        cost_estimate=pl.CostEstimate(
            flops=0, bytes_accessed=8 * steps * cut * h, transcendentals=0
        ),
    )(at, gate, up)


def local(context, out_proj, residual, norm_gain, expert_ids, gates, gate_proj, up_proj, down_proj):
    ny, nc, nz, nx = (lax.axis_size(a) for a in ("y", "c", "z", "x"))
    rows_here, width = residual.shape
    quarter = width // nx
    experts_total = ny * nc * nz
    capacity = min(rows_here, max(2, rows_here * TOPK * 5 // (4 * experts_total)))
    x = lax.axis_index("x")
    c = lax.axis_index("c")
    mate = jnp.where(c == 0, x ^ 1, x ^ 3)
    twin = jnp.where(c == 0, x ^ 3, x ^ 1)
    tokens_core = nx * rows_here
    tokens = nc * tokens_core

    mine = lax.axis_index("z") * nx + x
    part = project(mine[None].astype(jnp.int32), context, out_proj, residual, nx)

    meta = jnp.concatenate([expert_ids.astype(BF16), gates], axis=1)
    meta = jnp.pad(meta, ((0, 0), (0, 128 - meta.shape[1])))
    came = [meta] + [shift(meta, "x", k) for k in range(1, nx)]
    part, came = lax.optimization_barrier((part, came))
    part = exchange(part.reshape(nx * nz, tokens_core, quarter), ("x", "z"))
    ring = [came[(nx - m) % nx] for m in range(nx)]
    ring = jnp.concatenate(ring + ring[:-1], axis=0)
    meta_own = lax.dynamic_slice(
        ring, (lax.rem(nx - x, nx) * rows_here, jnp.int32(0)), (tokens_core, meta.shape[1])
    )
    meta_all = jnp.concatenate([meta_own, shift(meta_own, "c", 1)], axis=0)
    ids = meta_all[:, :TOPK].astype(jnp.int32)
    gate_vals = meta_all[:, TOPK : 2 * TOPK].astype(F32)

    places = ny * nz
    place = jnp.arange(places, dtype=jnp.int32)
    expert_of = ((place // nz) * nc + c) * nz + lax.rem(place, nz)
    matches = ids[:, :, None] == expert_of[None, None, :]
    picked = jnp.any(matches, axis=1).astype(jnp.int32)
    weighted = jnp.sum(jnp.where(matches, gate_vals[:, :, None], F32(0)), axis=1)
    by_device = picked.reshape(nc * nx, rows_here, places)
    ranking = jnp.cumsum(by_device, axis=1) - by_device
    admitted = (by_device > 0) & (ranking < capacity)
    device_iota = jnp.arange(nc * nx, dtype=jnp.int32)[:, None, None]
    slot = jnp.where(admitted, device_iota * capacity + ranking, -1).reshape(tokens, places)
    slots = nc * nx * capacity
    slot_iota = jnp.arange(slots, dtype=jnp.int32)
    chosen = slot.T[:, None, :] == slot_iota[None, :, None]
    selector = chosen.astype(BF16).reshape(places * slots, tokens)
    scaled = jnp.where(chosen, weighted.T[:, None, :], F32(0)).astype(BF16)
    scaled = scaled.reshape(places * slots, tokens)
    kept = pack(jnp.stack([x, twin]).astype(jnp.int32), gate_proj, up_proj)
    given = pack(jnp.stack([mate, x ^ 2]).astype(jnp.int32), gate_proj, up_proj)

    def cut_down(k):
        at = lax.rem(x + k, nx) * quarter
        return lax.dynamic_slice(down_proj[0], (0, at), (down_proj.shape[1], quarter))

    down_cut = [cut_down(k) for k in range(nx)]
    selector, scaled, part, kept, given, down_cut = lax.optimization_barrier(
        (selector, scaled, part, kept, given, down_cut)
    )

    hidden = jnp.sum(part.astype(F32), axis=0).astype(BF16)
    hidden_wide = hidden.astype(F32)

    twin_own = from_places(hidden, lambda c, x: (c, twin_of(c, x)))
    near_other = from_places(hidden, lambda c, x: (1 - c, x))
    twin_other = from_places(hidden, lambda c, x: (1 - c, twin_of(c, x)))
    rows = jnp.concatenate(
        [
            jnp.concatenate([hidden, near_other], axis=0),
            jnp.concatenate([twin_own, twin_other], axis=0),
        ],
        axis=1,
    )
    outgoing = jnp.dot(selector, rows, preferred_element_type=F32).astype(BF16)
    arrived = exchange(outgoing.reshape(places, slots, 2 * quarter), ("y", "z"))
    arrived = arrived.reshape(places * slots, 2 * quarter)

    taken = from_places(given, lambda c, x: (c, mate_of(c, x)))
    down_by = [down_cut[0]] + [shift(down_cut[k], "x", k) for k in range(1, nx)]
    arrived, taken, down_by = lax.optimization_barrier((arrived, taken, down_by))

    gain = jnp.concatenate(
        [lax.dynamic_slice(norm_gain, (q * quarter,), (quarter,)) for q in (x, twin)]
    )
    to_mate = lambda value: from_places(value, lambda c, x: (c, mate_of(c, x)))
    gained, square, theirs = first_product(arrived, gain, taken)
    came_back = to_mate(theirs)
    inverse = lax.rsqrt((square + to_mate(square)) / width + 1e-06)
    total = jnp.dot(gained, kept, preferred_element_type=F32) + came_back.astype(F32)
    total = total * inverse
    hid = total.shape[1] // 2
    activated = (jax.nn.silu(total[:, :hid]) * total[:, hid:]).astype(BF16)
    result = None
    for k in (0, 1, 3, 2):
        block = activated if k == 0 else shift(activated, "x", k)
        piece = jnp.dot(block, down_by[k], preferred_element_type=F32)
        result = piece if result is None else result + piece

    returned = exchange(result.astype(BF16).reshape(places, slots, quarter), ("y", "z"))
    returned = returned.reshape(places * slots, quarter)
    mixture = lax.dot_general(
        scaled, returned, (((0,), (0,)), ((), ())), preferred_element_type=F32
    )
    mixture = mixture[:tokens_core] + shift(mixture[tokens_core:], "c", 1)
    out = (hidden_wide + mixture).astype(BF16)
    out = exchange(out.reshape(nx, rows_here, quarter), "x")
    return out.transpose(1, 0, 2).reshape(rows_here, width)


def solution(mesh):
    grid = Mesh(mesh.devices.reshape(4, 2, 4, 4), ("y", "c", "z", "x"))
    group, member = ("y", "c"), ("z", "x")
    owner = group + member
    in_specs = (
        P(group, member),
        P(member, None),
        P(owner, None),
        P(),
        P(owner, None),
        P(owner, None),
        P(owner, None, None),
        P(owner, None, None),
        P(owner, None, None),
    )
    return jax.shard_map(
        local, mesh=grid, in_specs=in_specs, out_specs=P(owner, None), check_vma=False
    )
```

time: 326 us -> 268 us (0.82)
  waiting for transfers between devices: 229 us -> 145 us
  blocking collectives: 9.27 us -> 46.7 us
  Pallas kernels: 0 us -> 24.9 us
  starting transfers between devices: 43.5 us -> 27.8 us
  matrix products: 24.3 us -> 10.9 us
  local copies, waits for them, and re-layouts: 11 us -> 5.27 us
    ppermute x18 -> x11, waiting for transfers between devices: 143 us -> 90.6 us  [shift(): lax.ppermute(value, axis, [(i, (i + amount) % size) for i in range(size)])]
    all_to_all x5 -> x2, waiting for transfers between devices: 85.5 us -> 34 us  [exchange(): return lax.all_to_all(value, axes, split_axis=0, concat_axis=0, tiled=True)]
    all_to_all x1 -> x2, blocking collectives: 9.27 us -> 46.7 us  [exchange(): return lax.all_to_all(value, axes, split_axis=0, concat_axis=0, tiled=True)]
    pallas_call x0 -> x4, Pallas kernels: none -> 24.9 us  [the longest x1 8.96 us: project(): pl.pallas_call(project_body, out_shape=jax.ShapeDtypeStruct((blocks, rows...]
    ppermute x0 -> x6, waiting for transfers between devices: none -> 20.6 us  [from_places(): return lax.ppermute(value, ('c', 'x'), pairs)]
    dot_general x6 -> x2, matrix products: 19.2 us -> 5.99 us  [the longest x1 3.47 us: local(): outgoing = jnp.dot(selector, rows, preferred_element_type=F32).astype(BF16)]
    all_to_all x5 -> x2, starting transfers between devices: 25.5 us -> 12.6 us  [exchange(): return lax.all_to_all(value, axes, split_axis=0, concat_axis=0, tiled=True)]
    ppermute x18 -> x11, starting transfers between devices: 18 us -> 12.4 us  [shift(): lax.ppermute(value, axis, [(i, (i + amount) % size) for i in range(size)])]
  transfers between devices with their start and end apart: 23 -> 19, of which waited for: 15 -> 9; matrix products, arithmetic and copies ran while one was open for 9% -> 3% of each run, Pallas kernels for 0% -> 6%
where the time goes in v2:
time: 268 us; the launch traced here: 267 us
  waiting for transfers between devices  145 us (54%)
  blocking collectives  46.7 us (17%)
  starting transfers between devices  27.8 us (10%)
  Pallas kernels  24.9 us (9%)
  matrix products  10.9 us (4%)
  other arithmetic  6.29 us (2%)
  local copies, waits for them, and re-layouts  5.27 us (2%)
    ppermute x11, waiting for transfers between devices, shift(): lax.ppermute(value, axis, [(i, (i + amount) % size) for i in range(size)])  90.6 us
    all_to_all x2, blocking collectives, exchange(): return lax.all_to_all(value, axes, split_axis=0, concat_axis=0, tiled=True)  46.7 us
    all_to_all x2, waiting for transfers between devices, exchange(): return lax.all_to_all(value, axes, split_axis=0, concat_axis=0, tiled=True)  34 us
    ppermute x6, waiting for transfers between devices, from_places(): return lax.ppermute(value, ('c', 'x'), pairs)  20.6 us
    all_to_all x2, starting transfers between devices, exchange(): return lax.all_to_all(value, axes, split_axis=0, concat_axis=0, tiled=True)  12.6 us
    ppermute x11, starting transfers between devices, shift(): lax.ppermute(value, axis, [(i, (i + amount) % size) for i in range(size)])  12.4 us
    pallas_call x1, Pallas kernels, project(): pl.pallas_call(project_body, out_shape=jax.ShapeDtypeStruct((blocks, rows...  8.96 us
    pallas_call x2, Pallas kernels, pack(): pl.pallas_call(pack_body, out_shape=jax.ShapeDtypeStruct((steps * cut, 2...  8.22 us
  transfers between devices with their start and end apart: 19, of which 9 were waited for; matrix products, arithmetic and copies ran while one was open for 3% of the time, Pallas kernels for 6%

profile of v2, /device:TPU:0, one launch (start us, length us, event | category | flops | bytes accessed | tf_op | source)
XLA Modules:
  0.0 267.4 jit_solution(17143479520691192158)
XLA Ops:
  1.4 2.8 %collective-permute-start.2 = (bf16[16,128]{0,1:T(8,128)(2,1)S(1)}, bf16[16,128]{0,1:T(8,128)(2,1)S(1)}, u32[]{:S(2)}, u32[]{:S(2)}) collective-permute-start(bf16[16,128]{0,1:T(8,128)(2,1)S(1)} %fusion.15), channel_id=1, source_target_pairs={{0,3},{1,0},{2,1},{3,2},{4,7},{5,4},{6,5},{7,6},{8,11},{9,8},{10,9... | collective-permute-start | bytes 12296 | tf_op jit(solution)/shard_map/ppermute | solution.py:16
  4.2 0.8 collective-permute-start.1
  5.0 0.9 collective-permute-start
  5.9 9.0 %shard_map.91 = bf16[4,256,1792]{2,1,0:T(8,128)(2,1)} custom-call(s32[1]{0:T(128)} %bitcast.mine_ref, bf16[256,512]{1,0:T(8,128)(2,1)} %a_ref.1, bf16[512,7168]{1,0:T(8,128)(2,1)} %b_ref.1, bf16[16,7168]{1,0:T(8,128)(2,1)} %r_ref.1), custom_call_target="tpu_custom_call" | custom-call | flops 1879048192 | bytes 11272192 | tf_op jit(solution)/shard_map/pallas_call | solution.py:54
  14.9 7.3 %all-to-all-start = ((bf16[16,64,1792]{2,1,0:T(8,128)(2,1)}), bf16[16,64,1792]{2,1,0:T(8,128)(2,1)}, u32[]{:S(2)}, u32[]{:S(2)}) async-start(bf16[16,64,1792]{2,1,0:T(8,128)(2,1)} %bitcast.54), calls=%async_computation | async-start | bytes 7340032 | tf_op jit(solution)/shard_map/all_to_all | solution.py:20
  22.9 3.6 %dynamic-slice_bitcast_fusion = (bf16[256,1792]{1,0:T(8,128)(2,1)}, bf16[256,1792]{1,0:T(8,128)(2,1)}, bf16[256,1792]{1,0:T(8,128)(2,1)S(1)}, bf16[256,1792]{1,0:T(8,128)(2,1)}) fusion(bf16[1,256,7168]{2,1,0:T(8,128)(2,1)} %param.17, s32[]{:T(128)S(6)} %select_n.61, s32[]{:T(128)S(6)} %select_n.59, s32[]{:T(128)S(6)} %select_n.58, s32[]{:T(128)S(6)} %select_n.60), kind=kLoop, calls=%fused_computation.10 | loop fusion | bytes 7340048 | tf_op jit(solution)/shard_map/dynamic_slice | solution.py:215
  27.0 4.1 %shard_map.92 = bf16[3584,512]{1,0:T(8,128)(2,1)} custom-call(s32[2]{0:T(128)} %get-tuple-element.59.at_ref, bf16[1,7168,256]{2,1,0:T(8,128)(2,1)} %g_ref.3, bf16[1,7168,256]{2,1,0:T(8,128)(2,1)} %u_ref.3), custom_call_target="tpu_custom_call" | custom-call | bytes 7340032 | tf_op jit(solution)/shard_map/pallas_call | solution.py:144
  31.2 4.1 %shard_map.93 = bf16[3584,512]{1,0:T(8,128)(2,1)} custom-call(s32[2]{0:T(128)} %get-tuple-element.60.at_ref, bf16[1,7168,256]{2,1,0:T(8,128)(2,1)} %g_ref.3, bf16[1,7168,256]{2,1,0:T(8,128)(2,1)} %u_ref.3), custom_call_target="tpu_custom_call" | custom-call | bytes 7340032 | tf_op jit(solution)/shard_map/pallas_call | solution.py:144
  36.9 34.0 %all-to-all-done = bf16[16,64,1792]{2,1,0:T(8,128)(2,1)} async-done(((bf16[16,64,1792]{2,1,0:T(8,128)(2,1)}), bf16[16,64,1792]{2,1,0:T(8,128)(2,1)}, u32[]{:S(2)}, u32[]{:S(2)}) %all-to-all-start) | async-done | bytes 3670048 | tf_op jit(solution)/shard_map/all_to_all | solution.py:20
  70.9 2.6 reduce_sum.22
  74.1 7.9 %collective-permute-done.6 = bf16[64,1792]{1,0:T(8,128)(2,1)S(1)} collective-permute-done((bf16[64,1792]{1,0:T(8,128)(2,1)S(1)}, bf16[64,1792]{1,0:T(8,128)(2,1)S(1)}, u32[]{:S(2)}, u32[]{:S(2)}) %collective-permute-start.6) | collective-permute-done | bytes 229408 | tf_op jit(solution)/shard_map/ppermute | solution.py:37
  82.6 3.5 %convolution_convert_fusion = bf16[640,3584]{1,0:T(8,128)(2,1)} fusion(bf16[640,128]{1,0:T(8,128)(2,1)S(1)} %fusion.11, bf16[64,1792]{1,0:T(8,128)(2,1)S(1)} %collective-permute-done.6, bf16[64,1792]{1,0:T(8,128)(2,1)S(1)} %collective-permute-done.5, bf16[64,1792]{1,0:T(8,128)(2,1)S(1)} %collective-permute-done.4, bf16[64,1792]{1,0:T(8,128)(2,1)S(1)} %reduce_sum.22), kind=kOutput, calls=%fused_computation | convolution fusion | flops 593166336 | bytes 5668864 | tf_op jit(solution)/shard_map/dot_general | solution.py:235
  86.1 5.3 %all-to-all-start.1 = ((bf16[16,40,3584]{2,1,0:T(8,128)(2,1)}), bf16[16,40,3584]{2,1,0:T(8,128)(2,1)}, u32[]{:S(2)}, u32[]{:S(2)}) async-start(bf16[16,40,3584]{2,1,0:T(8,128)(2,1)} %bitcast.53), calls=%async_computation.1 | async-start | bytes 9175040 | tf_op jit(solution)/shard_map/all_to_all | solution.py:20
  91.5 2.0 collective-permute-start.8
  93.5 1.0 collective-permute-start.9
  94.5 1.7 collective-permute-start.10
  96.3 64.0 %collective-permute-done.8 = bf16[256,1792]{1,0:T(8,128)(2,1)S(1)} collective-permute-done((bf16[256,1792]{1,0:T(8,128)(2,1)}, bf16[256,1792]{1,0:T(8,128)(2,1)S(1)}, u32[]{:S(2)}, u32[]{:S(2)}) %collective-permute-start.8) | collective-permute-done | bytes 917536 | tf_op jit(solution)/shard_map/ppermute | solution.py:16
  160.4 11.8 %collective-permute-done.9 = bf16[256,1792]{1,0:T(8,128)(2,1)} collective-permute-done((bf16[256,1792]{1,0:T(8,128)(2,1)}, bf16[256,1792]{1,0:T(8,128)(2,1)}, u32[]{:S(2)}, u32[]{:S(2)}) %collective-permute-start.9) | collective-permute-done | bytes 917536 | tf_op jit(solution)/shard_map/ppermute | solution.py:16
  172.2 1.8 collective-permute-done.10
  174.0 7.7 %shard_map.94 = (bf16[640,3584]{1,0:T(8,128)(2,1)S(1)}, f32[640,1]{1,0:T(8,128)S(1)}, bf16[640,512]{1,0:T(8,128)(2,1)S(1)}) custom-call(bf16[640,3584]{1,0:T(8,128)(2,1)} %bitcast.15.a_ref, f32[1,3584]{1,0:T(1,128)S(1)} %broadcast_in_dim.50.gain_ref, bf16[3584,512]{1,0:T(8,128)(2,1)} %collective-permute-done.7.w_ref), custom_call_target="tpu_custom_call" | custom-call | flops 2348810240 | bytes 13500416 | tf_op jit(solution)/shard_map/pallas_call | solution.py:106
  181.8 2.0 collective-permute-start.12
  183.9 12.1 %collective-permute-done.12 = f32[640,1]{1,0:T(8,128)S(1)} collective-permute-done((f32[640,1]{1,0:T(8,128)S(1)}, f32[640,1]{1,0:T(8,128)S(1)}, u32[]{:S(2)}, u32[]{:S(2)}) %collective-permute-start.12) | collective-permute-done | bytes 2592 | tf_op jit(solution)/shard_map/ppermute | solution.py:37
  196.1 2.5 add_multiply_fusion
  198.9 1.0 collective-permute-start.15
  199.9 1.7 collective-permute-start.14
  202.7 11.1 %collective-permute-done.13 = bf16[640,256]{1,0:T(8,128)(2,1)S(1)} collective-permute-done((bf16[640,256]{1,0:T(8,128)(2,1)S(1)}, bf16[640,256]{1,0:T(8,128)(2,1)S(1)}, u32[]{:S(2)}, u32[]{:S(2)}) %collective-permute-start.13) | collective-permute-done | bytes 327712 | tf_op jit(solution)/shard_map/ppermute | solution.py:16
  213.8 0.8 fusion.25
  214.6 0.8 fusion.26
  215.4 2.1 add_convert_fusion
  217.4 35.8 %all_to_all.20 = bf16[16,40,1792]{2,1,0:T(8,128)(2,1)S(1)} all-to-all(bf16[16,40,1792]{2,1,0:T(8,128)(2,1)S(1)} %bitcast.56), channel_id=1, replica_groups=mesh['y'=4,'c'=2,'z'=4,'x'=4] {'y','z'}, dimensions={0} | all-to-all | bytes 4587520 | tf_op jit(solution)/shard_map/all_to_all | solution.py:20
  254.0 1.8 collective-permute-done.16
  255.8 10.9 %all_to_all.21 = bf16[4,16,1792]{2,1,0:T(8,128)(2,1)S(1)} all-to-all(bf16[4,16,1792]{2,1,0:T(8,128)(2,1)S(1)} %bitcast.58), channel_id=1, replica_groups=mesh['y'=4,'c'=2,'z'=4,'x'=4] {'x'}, dimensions={0} | all-to-all | bytes 458752 | tf_op jit(solution)/shard_map/all_to_all | solution.py:20
  (56 shorter events, 8.6 us)
Async XLA Ops:
  1.4 13.5 %collective-permute-start.2 = (bf16[16,128]{0,1:T(8,128)(2,1)S(1)}, bf16[16,128]{0,1:T(8,128)(2,1)S(1)}, u32[]{:S(2)}, u32[]{:S(2)}) collective-permute-start(bf16[16,128]{0,1:T(8,128)(2,1)S(1)} %fusion.15), channel_id=1, source_target_pairs={{0,3},{1,0},{2,1},{3,2},{4,7},{5,4},{6,5},{7,6},{8,11},{9,8},{10,9... | collective-permute-start | bytes 12296 | tf_op jit(solution)/shard_map/ppermute | solution.py:16
  4.2 10.7 %collective-permute-start.1 = (bf16[16,128]{0,1:T(8,128)(2,1)S(1)}, bf16[16,128]{0,1:T(8,128)(2,1)S(1)}, u32[]{:S(2)}, u32[]{:S(2)}) collective-permute-start(bf16[16,128]{0,1:T(8,128)(2,1)S(1)} %fusion.15), channel_id=1, source_target_pairs={{0,2},{1,3},{2,0},{3,1},{4,6},{5,7},{6,4},{7,5},{8,10},{9,11},{10,... | collective-permute-start | bytes 12296 | tf_op jit(solution)/shard_map/ppermute | solution.py:16
  5.0 9.9 %collective-permute-start = (bf16[16,128]{0,1:T(8,128)(2,1)S(1)}, bf16[16,128]{0,1:T(8,128)(2,1)S(1)}, u32[]{:S(2)}, u32[]{:S(2)}) collective-permute-start(bf16[16,128]{0,1:T(8,128)(2,1)S(1)} %fusion.15), channel_id=1, source_target_pairs={{0,1},{1,2},{2,3},{3,0},{4,5},{5,6},{6,7},{7,4},{8,9},{9,10},{10,1... | collective-permute-start | bytes 12296 | tf_op jit(solution)/shard_map/ppermute | solution.py:16
  14.9 56.0 %all-to-all-start = ((bf16[16,64,1792]{2,1,0:T(8,128)(2,1)}), bf16[16,64,1792]{2,1,0:T(8,128)(2,1)}, u32[]{:S(2)}, u32[]{:S(2)}) async-start(bf16[16,64,1792]{2,1,0:T(8,128)(2,1)} %bitcast.54), calls=%async_computation | async-start | bytes 7340032 | tf_op jit(solution)/shard_map/all_to_all | solution.py:20
  26.7 8.5 %collective-permute-start.3 = (bf16[64,128]{0,1:T(8,128)(2,1)S(1)}, bf16[64,128]{0,1:T(8,128)(2,1)S(1)}, u32[]{:S(2)}, u32[]{:S(2)}) collective-permute-start(bf16[64,128]{0,1:T(8,128)(2,1)S(1)} %constant_dynamic-slice_fusion), channel_id=1, source_target_pairs={{0,16},{16,0},{1,17},{17,1},{2,18},{18,2},{3,19},{19,3},{4,20},{20... | collective-permute-start | bytes 49160 | tf_op jit(solution)/shard_map/ppermute | solution.py:16
  73.5 8.6 %collective-permute-start.6 = (bf16[64,1792]{1,0:T(8,128)(2,1)S(1)}, bf16[64,1792]{1,0:T(8,128)(2,1)S(1)}, u32[]{:S(2)}, u32[]{:S(2)}) collective-permute-start(bf16[64,1792]{1,0:T(8,128)(2,1)S(1)} %reduce_sum.22), channel_id=1, source_target_pairs={{19,0},{18,1},{17,2},{16,3},{1,16},{0,17},{3,18},{2,19},{23,4},{22... | collective-permute-start | bytes 688136 | tf_op jit(solution)/shard_map/ppermute | solution.py:37
  73.5 9.1 %collective-permute-start.5 = (bf16[64,1792]{1,0:T(8,128)(2,1)S(1)}, bf16[64,1792]{1,0:T(8,128)(2,1)S(1)}, u32[]{:S(2)}, u32[]{:S(2)}) collective-permute-start(bf16[64,1792]{1,0:T(8,128)(2,1)S(1)} %reduce_sum.22), channel_id=1, source_target_pairs={{3,0},{2,1},{1,2},{0,3},{17,16},{16,17},{19,18},{18,19},{7,4},{6,5... | collective-permute-start | bytes 688136 | tf_op jit(solution)/shard_map/ppermute | solution.py:37
  73.6 9.0 %collective-permute-start.4 = (bf16[64,1792]{1,0:T(8,128)(2,1)S(1)}, bf16[64,1792]{1,0:T(8,128)(2,1)S(1)}, u32[]{:S(2)}, u32[]{:S(2)}) collective-permute-start(bf16[64,1792]{1,0:T(8,128)(2,1)S(1)} %reduce_sum.22), channel_id=1, source_target_pairs={{16,0},{17,1},{18,2},{19,3},{0,16},{1,17},{2,18},{3,19},{20,4},{21... | collective-permute-start | bytes 688136 | tf_op jit(solution)/shard_map/ppermute | solution.py:37
  86.1 10.1 %copy-start.1 = (f32[7168]{0:T(1024)S(1)}, f32[7168]{0:T(1024)}, u32[]{:S(2)}) copy-start(f32[7168]{0:T(1024)} %param.12) | copy-start | bytes 86020
  86.1 87.9 %all-to-all-start.1 = ((bf16[16,40,3584]{2,1,0:T(8,128)(2,1)}), bf16[16,40,3584]{2,1,0:T(8,128)(2,1)}, u32[]{:S(2)}, u32[]{:S(2)}) async-start(bf16[16,40,3584]{2,1,0:T(8,128)(2,1)} %bitcast.53), calls=%async_computation.1 | async-start | bytes 9175040 | tf_op jit(solution)/shard_map/all_to_all | solution.py:20
  91.4 82.6 %collective-permute-start.7 = (bf16[3584,512]{1,0:T(8,128)(2,1)}, bf16[3584,512]{1,0:T(8,128)(2,1)}, u32[]{:S(2)}, u32[]{:S(2)}) collective-permute-start(bf16[3584,512]{1,0:T(8,128)(2,1)} %shard_map.93), channel_id=1, source_target_pairs={{1,0},{0,1},{3,2},{2,3},{19,16},{18,17},{17,18},{16,19},{5,4},{4,5... | collective-permute-start | bytes 11010056 | tf_op jit(solution)/shard_map/ppermute | solution.py:37
  91.5 68.8 %collective-permute-start.8 = (bf16[256,1792]{1,0:T(8,128)(2,1)}, bf16[256,1792]{1,0:T(8,128)(2,1)S(1)}, u32[]{:S(2)}, u32[]{:S(2)}) collective-permute-start(bf16[256,1792]{1,0:T(8,128)(2,1)} %get-tuple-element.38), channel_id=1, source_target_pairs={{0,1},{1,2},{2,3},{3,0},{4,5},{5,6},{6,7},{7,4},{8,9},{9,10},{10,1... | collective-permute-start | bytes 2752520 | tf_op jit(solution)/shard_map/ppermute | solution.py:16
  93.5 78.7 %collective-permute-start.9 = (bf16[256,1792]{1,0:T(8,128)(2,1)}, bf16[256,1792]{1,0:T(8,128)(2,1)}, u32[]{:S(2)}, u32[]{:S(2)}) collective-permute-start(bf16[256,1792]{1,0:T(8,128)(2,1)} %get-tuple-element.39), channel_id=1, source_target_pairs={{0,2},{1,3},{2,0},{3,1},{4,6},{5,7},{6,4},{7,5},{8,10},{9,11},{10,... | collective-permute-start | bytes 2752520 | tf_op jit(solution)/shard_map/ppermute | solution.py:16
  94.5 79.5 %collective-permute-start.10 = (bf16[256,1792]{1,0:T(8,128)(2,1)}, bf16[256,1792]{1,0:T(8,128)(2,1)S(1)}, u32[]{:S(2)}, u32[]{:S(2)}) collective-permute-start(bf16[256,1792]{1,0:T(8,128)(2,1)} %get-tuple-element.40), channel_id=1, source_target_pairs={{0,3},{1,0},{2,1},{3,2},{4,7},{5,4},{6,5},{7,6},{8,11},{9,8},{10,9... | collective-permute-start | bytes 2752520 | tf_op jit(solution)/shard_map/ppermute | solution.py:16
  174.0 22.1 %copy-start = (bf16[3584,512]{1,0:T(8,128)(2,1)S(1)}, bf16[3584,512]{1,0:T(8,128)(2,1)}, u32[]{:S(2)}) copy-start(bf16[3584,512]{1,0:T(8,128)(2,1)} %shard_map.92) | copy-start | bytes 11010052
  181.8 14.4 %collective-permute-start.11 = (bf16[640,512]{1,0:T(8,128)(2,1)S(1)}, bf16[640,512]{1,0:T(8,128)(2,1)S(1)}, u32[]{:S(2)}, u32[]{:S(2)}) collective-permute-start(bf16[640,512]{1,0:T(8,128)(2,1)S(1)} %get-tuple-element.45), channel_id=1, source_target_pairs={{1,0},{0,1},{3,2},{2,3},{19,16},{18,17},{17,18},{16,19},{5,4},{4,5... | collective-permute-start | bytes 1966088 | tf_op jit(solution)/shard_map/ppermute | solution.py:37
  181.8 14.1 %collective-permute-start.12 = (f32[640,1]{1,0:T(8,128)S(1)}, f32[640,1]{1,0:T(8,128)S(1)}, u32[]{:S(2)}, u32[]{:S(2)}) collective-permute-start(f32[640,1]{1,0:T(8,128)S(1)} %get-tuple-element.46), channel_id=1, source_target_pairs={{1,0},{0,1},{3,2},{2,3},{19,16},{18,17},{17,18},{16,19},{5,4},{4,5... | collective-permute-start | bytes 7688 | tf_op jit(solution)/shard_map/ppermute | solution.py:37
  198.9 16.5 %collective-permute-start.15 = (bf16[640,256]{1,0:T(8,128)(2,1)S(1)}, bf16[640,256]{1,0:T(8,128)(2,1)S(1)}, u32[]{:S(2)}, u32[]{:S(2)}) collective-permute-start(bf16[640,256]{1,0:T(8,128)(2,1)S(1)} %fusion.7), channel_id=1, source_target_pairs={{0,2},{1,3},{2,0},{3,1},{4,6},{5,7},{6,4},{7,5},{8,10},{9,11},{10,... | collective-permute-start | bytes 983048 | tf_op jit(solution)/shard_map/ppermute | solution.py:16
  199.9 14.7 %collective-permute-start.14 = (bf16[640,256]{1,0:T(8,128)(2,1)S(1)}, bf16[640,256]{1,0:T(8,128)(2,1)S(1)}, u32[]{:S(2)}, u32[]{:S(2)}) collective-permute-start(bf16[640,256]{1,0:T(8,128)(2,1)S(1)} %fusion.7), channel_id=1, source_target_pairs={{0,3},{1,0},{2,1},{3,2},{4,7},{5,4},{6,5},{7,6},{8,11},{9,8},{10,9... | collective-permute-start | bytes 983048 | tf_op jit(solution)/shard_map/ppermute | solution.py:16
  201.6 12.2 %collective-permute-start.13 = (bf16[640,256]{1,0:T(8,128)(2,1)S(1)}, bf16[640,256]{1,0:T(8,128)(2,1)S(1)}, u32[]{:S(2)}, u32[]{:S(2)}) collective-permute-start(bf16[640,256]{1,0:T(8,128)(2,1)S(1)} %fusion.7), channel_id=1, source_target_pairs={{0,1},{1,2},{2,3},{3,0},{4,5},{5,6},{6,7},{7,4},{8,9},{9,10},{10,1... | collective-permute-start | bytes 983048 | tf_op jit(solution)/shard_map/ppermute | solution.py:16
  253.9 1.9 collective-permute-start.16

commit v3 on v2

--- a/solution.py
+++ b/solution.py
@@ -49,7 +49,7 @@
     rows, depth = context.shape
     own, width = residual.shape
     cut = width // blocks
-    halves = 2
+    halves = 1
     step = cut // halves
     return pl.pallas_call(
         project_body,
@@ -74,35 +74,28 @@
     )(mine, context, weight, residual)
 
 
-def first_body(a_ref, gain_ref, w_ref, g_ref, s_ref, o_ref, acc_ref, sq_ref):
-    step = pl.program_id(0)
-
-    @pl.when(step == 0)
-    def _():
-        acc_ref[...] = jnp.zeros_like(acc_ref)
-        sq_ref[...] = jnp.zeros_like(sq_ref)
-
-    wide = a_ref[...].astype(F32)
-    squares = wide * wide
-    lanes = sq_ref.shape[1]
-    partial = squares[:, :lanes]
-    for i in range(1, squares.shape[1] // lanes):
-        partial += squares[:, i * lanes : (i + 1) * lanes]
-    sq_ref[...] += partial
-    gained = (wide * gain_ref[...]).astype(BF16)
-    g_ref[...] = gained
-    acc_ref[...] += jnp.dot(gained, w_ref[...], preferred_element_type=F32)
-
-    @pl.when(step == pl.num_programs(0) - 1)
-    def _():
-        o_ref[...] = acc_ref[...].astype(BF16)
-        s_ref[...] = jnp.sum(sq_ref[...], axis=1, keepdims=True)
+def first_body(a_ref, gain_ref, w_ref, g_ref, s_ref, o_ref):
+    depth = a_ref.shape[1]
+    step = depth // 7
+    total = None
+    squares = None
+    for at in range(0, depth, step):
+        wide = a_ref[:, at : at + step].astype(F32)
+        for i in range(0, step, 128):
+            part = wide[:, i : i + 128]
+            squares = part * part if squares is None else squares + part * part
+        gained = (wide * gain_ref[:, at : at + step]).astype(BF16)
+        g_ref[:, at : at + step] = gained
+        piece = jnp.dot(gained, w_ref[at : at + step, :], preferred_element_type=F32)
+        total = piece if total is None else total + piece
+    o_ref[...] = total.astype(BF16)
+    s_ref[...] = jnp.sum(squares, axis=1, keepdims=True)
 
 
 def first_product(arrived, gain, weight):
     rows, depth = arrived.shape
     cols = weight.shape[1]
-    step = 512
+    whole = pl.BlockSpec(memory_space=pltpu.VMEM)
     return pl.pallas_call(
         first_body,
         out_shape=(
@@ -110,19 +103,9 @@
             jax.ShapeDtypeStruct((rows, 1), F32),
             jax.ShapeDtypeStruct((rows, cols), BF16),
         ),
-        grid=(depth // step,),
-        in_specs=[
-            pl.BlockSpec((rows, step), lambda k: (0, k)),
-            pl.BlockSpec((1, step), lambda k: (0, k)),
-            pl.BlockSpec((step, cols), lambda k: (k, 0)),
-        ],
-        out_specs=(
-            pl.BlockSpec((rows, step), lambda k: (0, k)),
-            pl.BlockSpec((rows, 1), lambda k: (0, 0)),
-            pl.BlockSpec((rows, cols), lambda k: (0, 0)),
-        ),
-        scratch_shapes=[pltpu.VMEM((rows, cols), F32), pltpu.VMEM((rows, 128), F32)],
-        compiler_params=pltpu.CompilerParams(vmem_limit_bytes=24 << 20),
+        in_specs=[whole] * 3,
+        out_specs=(whole,) * 3,
+        compiler_params=pltpu.CompilerParams(vmem_limit_bytes=32 << 20),
         cost_estimate=pl.CostEstimate(
             flops=2 * rows * depth * cols,
             bytes_accessed=2 * (2 * rows * depth + depth * cols + rows * cols),
@@ -237,25 +220,35 @@
     arrived = arrived.reshape(places * slots, 2 * quarter)
 
     taken = from_places(given, lambda c, x: (c, mate_of(c, x)))
-    down_by = [down_cut[0]] + [shift(down_cut[k], "x", k) for k in range(1, nx)]
-    arrived, taken, down_by = lax.optimization_barrier((arrived, taken, down_by))
+    half = down_cut[2].shape[0] // 2
+    hop_up, hop_down = shift(down_cut[2][:half], "x", 1), shift(down_cut[2][half:], "x", -1)
+    down_by = [down_cut[0], shift(down_cut[1], "x", 1), None, shift(down_cut[3], "x", 3)]
+    arrived, taken, down_by[1], down_by[3], hop_up, hop_down = lax.optimization_barrier(
+        (arrived, taken, down_by[1], down_by[3], hop_up, hop_down)
+    )
+    hop_up, hop_down = shift(hop_up, "x", 1), shift(hop_down, "x", -1)
 
     gain = jnp.concatenate(
         [lax.dynamic_slice(norm_gain, (q * quarter,), (quarter,)) for q in (x, twin)]
     )
     to_mate = lambda value: from_places(value, lambda c, x: (c, mate_of(c, x)))
     gained, square, theirs = first_product(arrived, gain, taken)
+    theirs, hop_up, hop_down = lax.optimization_barrier((theirs, hop_up, hop_down))
     came_back = to_mate(theirs)
     inverse = lax.rsqrt((square + to_mate(square)) / width + 1e-06)
-    total = jnp.dot(gained, kept, preferred_element_type=F32) + came_back.astype(F32)
+    total = jnp.dot(gained, kept, preferred_element_type=F32)
+    total, came_back = lax.optimization_barrier((total, came_back))
+    total = total + came_back.astype(F32)
     total = total * inverse
     hid = total.shape[1] // 2
     activated = (jax.nn.silu(total[:, :hid]) * total[:, hid:]).astype(BF16)
-    result = None
-    for k in (0, 1, 3, 2):
-        block = activated if k == 0 else shift(activated, "x", k)
-        piece = jnp.dot(block, down_by[k], preferred_element_type=F32)
-        result = piece if result is None else result + piece
+    result = jnp.dot(activated, down_by[0], preferred_element_type=F32)
+    for k in (1, 3):
+        block = shift(activated, "x", k)
+        result += jnp.dot(block, down_by[k], preferred_element_type=F32)
+    block = shift(activated, "x", 2)
+    result += jnp.dot(block[:, :half], hop_up, preferred_element_type=F32)
+    result += jnp.dot(block[:, half:], hop_down, preferred_element_type=F32)
 
     returned = exchange(result.astype(BF16).reshape(places, slots, quarter), ("y", "z"))
     returned = returned.reshape(places * slots, quarter)

time: 268 us -> 259 us (0.966)
  waiting for transfers between devices: 145 us -> 129 us
  starting transfers between devices: 27.8 us -> 33.8 us
  local copies, waits for them, and re-layouts: 5.27 us -> 11.1 us
  Pallas kernels: 24.9 us -> 20.1 us
    ppermute x11 -> x14, waiting for transfers between devices: 90.6 us -> 80.8 us  [shift(): lax.ppermute(value, axis, [(i, (i + amount) % size) for i in range(size)])]
    ppermute x6, waiting for transfers between devices: 20.6 us -> 14.4 us  [from_places(): return lax.ppermute(value, ('c', 'x'), pairs)]
    ppermute x11 -> x14, starting transfers between devices: 12.4 us -> 18.3 us  [shift(): lax.ppermute(value, axis, [(i, (i + amount) % size) for i in range(size)])]
    unnamed x4 -> x22, local copies, waits for them, and re-layouts: 0.01 us -> 5.88 us
    pallas_call x1, Pallas kernels: 7.74 us -> 5.05 us  [first_product(): pl.pallas_call(first_body, out_shape=(jax.ShapeDtypeStruct((rows, depth),...]
    dot_general x5 -> x6, matrix products: 6.86 us -> 6.77 us  [the longest x1 2.52 us: local(): total = jnp.dot(gained, kept, preferred_element_type=F32)]
  transfers between devices with their start and end apart: 19 -> 22, of which waited for: 9 -> 9; matrix products, arithmetic and copies ran while one was open for 3% -> 4% of each run, Pallas kernels for 6% -> 8%
where the time goes in v3:
time: 259 us; the launch traced here: 258 us
  waiting for transfers between devices  129 us (50%)
  blocking collectives  46.1 us (18%)
  starting transfers between devices  33.8 us (13%)
  Pallas kernels  20.1 us (8%)
  local copies, waits for them, and re-layouts  11.1 us (4%)
  matrix products  10.8 us (4%)
  other arithmetic  6.54 us (3%)
    ppermute x14, waiting for transfers between devices, shift(): lax.ppermute(value, axis, [(i, (i + amount) % size) for i in range(size)])  80.8 us
    all_to_all x2, blocking collectives, exchange(): return lax.all_to_all(value, axes, split_axis=0, concat_axis=0, tiled=True)  46.1 us
    all_to_all x2, waiting for transfers between devices, exchange(): return lax.all_to_all(value, axes, split_axis=0, concat_axis=0, tiled=True)  34.1 us
    ppermute x14, starting transfers between devices, shift(): lax.ppermute(value, axis, [(i, (i + amount) % size) for i in range(size)])  18.3 us
    ppermute x6, waiting for transfers between devices, from_places(): return lax.ppermute(value, ('c', 'x'), pairs)  14.4 us
    all_to_all x2, starting transfers between devices, exchange(): return lax.all_to_all(value, axes, split_axis=0, concat_axis=0, tiled=True)  12.6 us
    pallas_call x2, Pallas kernels, pack(): pl.pallas_call(pack_body, out_shape=jax.ShapeDtypeStruct((steps * cut, 2...  8.23 us
    pallas_call x1, Pallas kernels, project(): pl.pallas_call(project_body, out_shape=jax.ShapeDtypeStruct((blocks, rows...  6.85 us
  transfers between devices with their start and end apart: 22, of which 9 were waited for; matrix products, arithmetic and copies ran while one was open for 4% of the time, Pallas kernels for 8%

profile of v3, /device:TPU:0, one launch (start us, length us, event | category | flops | bytes accessed | tf_op | source)
XLA Modules:
  0.0 258.1 jit_solution(17530274658718160407)
XLA Ops:
  1.4 2.8 %collective-permute-start.2 = (bf16[16,128]{0,1:T(8,128)(2,1)S(1)}, bf16[16,128]{0,1:T(8,128)(2,1)S(1)}, u32[]{:S(2)}, u32[]{:S(2)}) collective-permute-start(bf16[16,128]{0,1:T(8,128)(2,1)S(1)} %fusion.21), channel_id=1, source_target_pairs={{0,3},{1,0},{2,1},{3,2},{4,7},{5,4},{6,5},{7,6},{8,11},{9,8},{10,9... | collective-permute-start | bytes 12296 | tf_op jit(solution)/shard_map/ppermute | solution.py:16
  5.9 6.8 %shard_map.91 = bf16[4,256,1792]{2,1,0:T(8,128)(2,1)} custom-call(s32[1]{0:T(128)} %bitcast.mine_ref, bf16[256,512]{1,0:T(8,128)(2,1)} %a_ref.1, bf16[512,7168]{1,0:T(8,128)(2,1)} %b_ref.1, bf16[16,7168]{1,0:T(8,128)(2,1)} %r_ref.1), custom_call_target="tpu_custom_call" | custom-call | flops 1879048192 | bytes 11272192 | tf_op jit(solution)/shard_map/pallas_call | solution.py:54
  12.8 7.3 %all-to-all-start = ((bf16[16,64,1792]{2,1,0:T(8,128)(2,1)}), bf16[16,64,1792]{2,1,0:T(8,128)(2,1)}, u32[]{:S(2)}, u32[]{:S(2)}) async-start(bf16[16,64,1792]{2,1,0:T(8,128)(2,1)} %bitcast.54), calls=%async_computation | async-start | bytes 7340032 | tf_op jit(solution)/shard_map/all_to_all | solution.py:20
  20.8 3.5 %dynamic-slice_bitcast_fusion = (bf16[256,1792]{1,0:T(8,128)(2,1)}, bf16[256,1792]{1,0:T(8,128)(2,1)}, bf16[256,1792]{1,0:T(8,128)(2,1)S(1)}, bf16[256,1792]{1,0:T(8,128)(2,1)S(1)}) fusion(bf16[1,256,7168]{2,1,0:T(8,128)(2,1)} %param.17, s32[]{:T(128)S(6)} %select_n.61, s32[]{:T(128)S(6)} %select_n.59, s32[]{:T(128)S(6)} %select_n.58, s32[]{:T(128)S(6)} %select_n.60), kind=kLoop, calls=%fused_computation.10 | loop fusion | bytes 7340048 | tf_op jit(solution)/shard_map/dynamic_slice | solution.py:198
  24.8 4.2 %shard_map.92 = bf16[3584,512]{1,0:T(8,128)(2,1)} custom-call(s32[2]{0:T(128)} %get-tuple-element.71.at_ref, bf16[1,7168,256]{2,1,0:T(8,128)(2,1)} %g_ref.3, bf16[1,7168,256]{2,1,0:T(8,128)(2,1)} %u_ref.3), custom_call_target="tpu_custom_call" | custom-call | bytes 7340032 | tf_op jit(solution)/shard_map/pallas_call | solution.py:127
  29.0 4.1 %shard_map.93 = bf16[3584,512]{1,0:T(8,128)(2,1)} custom-call(s32[2]{0:T(128)} %get-tuple-element.72.at_ref, bf16[1,7168,256]{2,1,0:T(8,128)(2,1)} %g_ref.3, bf16[1,7168,256]{2,1,0:T(8,128)(2,1)} %u_ref.3), custom_call_target="tpu_custom_call" | custom-call | bytes 7340032 | tf_op jit(solution)/shard_map/pallas_call | solution.py:127
  34.7 34.1 %all-to-all-done = bf16[16,64,1792]{2,1,0:T(8,128)(2,1)} async-done(((bf16[16,64,1792]{2,1,0:T(8,128)(2,1)}), bf16[16,64,1792]{2,1,0:T(8,128)(2,1)}, u32[]{:S(2)}, u32[]{:S(2)}) %all-to-all-start) | async-done | bytes 3670048 | tf_op jit(solution)/shard_map/all_to_all | solution.py:20
  68.8 2.6 reduce_sum.22
  72.0 7.9 %collective-permute-done.6 = bf16[64,1792]{1,0:T(8,128)(2,1)S(1)} collective-permute-done((bf16[64,1792]{1,0:T(8,128)(2,1)S(1)}, bf16[64,1792]{1,0:T(8,128)(2,1)S(1)}, u32[]{:S(2)}, u32[]{:S(2)}) %collective-permute-start.6) | collective-permute-done | bytes 229408 | tf_op jit(solution)/shard_map/ppermute | solution.py:37
  80.5 3.5 %convolution_convert_fusion = bf16[640,3584]{1,0:T(8,128)(2,1)} fusion(bf16[640,128]{1,0:T(8,128)(2,1)S(1)} %fusion.11, bf16[64,1792]{1,0:T(8,128)(2,1)S(1)} %collective-permute-done.6, bf16[64,1792]{1,0:T(8,128)(2,1)S(1)} %collective-permute-done.5, bf16[64,1792]{1,0:T(8,128)(2,1)S(1)} %collective-permute-done.4, bf16[64,1792]{1,0:T(8,128)(2,1)S(1)} %reduce_sum.22), kind=kOutput, calls=%fused_computation | convolution fusion | flops 593166336 | bytes 5668864 | tf_op jit(solution)/shard_map/dot_general | solution.py:218
  84.0 5.3 %all-to-all-start.1 = ((bf16[16,40,3584]{2,1,0:T(8,128)(2,1)}), bf16[16,40,3584]{2,1,0:T(8,128)(2,1)}, u32[]{:S(2)}, u32[]{:S(2)}) async-start(bf16[16,40,3584]{2,1,0:T(8,128)(2,1)} %bitcast.53), calls=%async_computation.1 | async-start | bytes 9175040 | tf_op jit(solution)/shard_map/all_to_all | solution.py:20
  89.4 2.0 collective-permute-start.8
  91.5 1.3 collective-permute-start.9
  93.1 1.8 collective-permute-start.10
  94.9 65.5 %collective-permute-done.11 = bf16[128,1792]{1,0:T(8,128)(2,1)S(1)} collective-permute-done((bf16[128,1792]{1,0:T(8,128)(2,1)S(1)}, bf16[128,1792]{1,0:T(8,128)(2,1)S(1)}, u32[]{:S(2)}, u32[]{:S(2)}) %collective-permute-start.11) | collective-permute-done | bytes 458784 | tf_op jit(solution)/shard_map/ppermute | solution.py:16
  160.4 1.0 copy-done.3
  161.4 1.8 copy-done
  163.5 2.9 %collective-permute-start.13 = (bf16[128,1792]{1,0:T(8,128)(2,1)}, bf16[128,1792]{1,0:T(8,128)(2,1)S(1)}, u32[]{:S(2)}, u32[]{:S(2)}) collective-permute-start(bf16[128,1792]{1,0:T(8,128)(2,1)} %copy-done.10), channel_id=1, source_target_pairs={{0,3},{1,0},{2,1},{3,2},{4,7},{5,4},{6,5},{7,6},{8,11},{9,8},{10,9... | collective-permute-start | bytes 1376264 | tf_op jit(solution)/shard_map/ppermute | solution.py:16
  166.5 2.0 copy-done.1
  168.6 5.1 %shard_map.94 = (bf16[640,3584]{1,0:T(8,128)(2,1)S(1)}, f32[640,1]{1,0:T(8,128)S(1)}, bf16[640,512]{1,0:T(8,128)(2,1)S(1)}) custom-call(bf16[640,3584]{1,0:T(8,128)(2,1)} %bitcast.15.a_ref, f32[1,3584]{1,0:T(1,128)S(1)} %broadcast_in_dim.50.gain_ref, bf16[3584,512]{1,0:T(8,128)(2,1)S(1)} %copy-done.1), custom_call_target="tpu_custom_call" | custom-call | flops 2348810240 | bytes 13500416 | tf_op jit(solution)/shard_map/pallas_call | solution.py:99
  173.7 1.8 collective-permute-done.12
  175.5 1.0 collective-permute-done.13
  177.3 2.2 collective-permute-start.14
  179.4 2.5 fusion.31
  182.1 5.8 %collective-permute-done.14 = bf16[640,512]{1,0:T(8,128)(2,1)S(1)} collective-permute-done((bf16[640,512]{1,0:T(8,128)(2,1)S(1)}, bf16[640,512]{1,0:T(8,128)(2,1)S(1)}, u32[]{:S(2)}, u32[]{:S(2)}) %collective-permute-start.14) | collective-permute-done | bytes 655392 | tf_op jit(solution)/shard_map/ppermute | solution.py:37
  188.4 3.0 %collective-permute-start.18 = (bf16[640,256]{1,0:T(8,128)(2,1)S(1)}, bf16[640,256]{1,0:T(8,128)(2,1)S(1)}, u32[]{:S(2)}, u32[]{:S(2)}) collective-permute-start(bf16[640,256]{1,0:T(8,128)(2,1)S(1)} %fusion.7), channel_id=1, source_target_pairs={{0,2},{1,3},{2,0},{3,1},{4,6},{5,7},{6,4},{7,5},{8,10},{9,11},{10,... | collective-permute-start | bytes 983048 | tf_op jit(solution)/shard_map/ppermute | solution.py:16
  191.4 1.8 collective-permute-start.17
  194.2 10.7 %collective-permute-done.16 = bf16[640,256]{1,0:T(8,128)(2,1)S(1)} collective-permute-done((bf16[640,256]{1,0:T(8,128)(2,1)S(1)}, bf16[640,256]{1,0:T(8,128)(2,1)S(1)}, u32[]{:S(2)}, u32[]{:S(2)}) %collective-permute-start.16) | collective-permute-done | bytes 327712 | tf_op jit(solution)/shard_map/ppermute | solution.py:16
  207.5 1.2 add_convert_fusion
  208.7 35.8 %all_to_all.20 = bf16[16,40,1792]{2,1,0:T(8,128)(2,1)S(1)} all-to-all(bf16[16,40,1792]{2,1,0:T(8,128)(2,1)S(1)} %bitcast.56), channel_id=1, replica_groups=mesh['y'=4,'c'=2,'z'=4,'x'=4] {'y','z'}, dimensions={0} | all-to-all | bytes 4587520 | tf_op jit(solution)/shard_map/all_to_all | solution.py:20
  245.2 1.8 collective-permute-done.19
  247.1 10.3 %all_to_all.21 = bf16[4,16,1792]{2,1,0:T(8,128)(2,1)S(1)} all-to-all(bf16[4,16,1792]{2,1,0:T(8,128)(2,1)S(1)} %bitcast.58), channel_id=1, replica_groups=mesh['y'=4,'c'=2,'z'=4,'x'=4] {'x'}, dimensions={0} | all-to-all | bytes 458752 | tf_op jit(solution)/shard_map/all_to_all | solution.py:20
  (83 shorter events, 14.5 us)
Async XLA Ops:
  1.4 11.4 %collective-permute-start.2 = (bf16[16,128]{0,1:T(8,128)(2,1)S(1)}, bf16[16,128]{0,1:T(8,128)(2,1)S(1)}, u32[]{:S(2)}, u32[]{:S(2)}) collective-permute-start(bf16[16,128]{0,1:T(8,128)(2,1)S(1)} %fusion.21), channel_id=1, source_target_pairs={{0,3},{1,0},{2,1},{3,2},{4,7},{5,4},{6,5},{7,6},{8,11},{9,8},{10,9... | collective-permute-start | bytes 12296 | tf_op jit(solution)/shard_map/ppermute | solution.py:16
  4.2 8.5 %collective-permute-start.1 = (bf16[16,128]{0,1:T(8,128)(2,1)S(1)}, bf16[16,128]{0,1:T(8,128)(2,1)S(1)}, u32[]{:S(2)}, u32[]{:S(2)}) collective-permute-start(bf16[16,128]{0,1:T(8,128)(2,1)S(1)} %fusion.21), channel_id=1, source_target_pairs={{0,2},{1,3},{2,0},{3,1},{4,6},{5,7},{6,4},{7,5},{8,10},{9,11},{10,... | collective-permute-start | bytes 12296 | tf_op jit(solution)/shard_map/ppermute | solution.py:16
  5.0 7.7 %collective-permute-start = (bf16[16,128]{0,1:T(8,128)(2,1)S(1)}, bf16[16,128]{0,1:T(8,128)(2,1)S(1)}, u32[]{:S(2)}, u32[]{:S(2)}) collective-permute-start(bf16[16,128]{0,1:T(8,128)(2,1)S(1)} %fusion.21), channel_id=1, source_target_pairs={{0,1},{1,2},{2,3},{3,0},{4,5},{5,6},{6,7},{7,4},{8,9},{9,10},{10,1... | collective-permute-start | bytes 12296 | tf_op jit(solution)/shard_map/ppermute | solution.py:16
  12.8 56.0 %all-to-all-start = ((bf16[16,64,1792]{2,1,0:T(8,128)(2,1)}), bf16[16,64,1792]{2,1,0:T(8,128)(2,1)}, u32[]{:S(2)}, u32[]{:S(2)}) async-start(bf16[16,64,1792]{2,1,0:T(8,128)(2,1)} %bitcast.54), calls=%async_computation | async-start | bytes 7340032 | tf_op jit(solution)/shard_map/all_to_all | solution.py:20
  24.5 8.5 %collective-permute-start.3 = (bf16[64,128]{0,1:T(8,128)(2,1)S(1)}, bf16[64,128]{0,1:T(8,128)(2,1)S(1)}, u32[]{:S(2)}, u32[]{:S(2)}) collective-permute-start(bf16[64,128]{0,1:T(8,128)(2,1)S(1)} %constant_dynamic-slice_fusion), channel_id=1, source_target_pairs={{0,16},{16,0},{1,17},{17,1},{2,18},{18,2},{3,19},{19,3},{4,20},{20... | collective-permute-start | bytes 49160 | tf_op jit(solution)/shard_map/ppermute | solution.py:16
  71.3 8.6 %collective-permute-start.6 = (bf16[64,1792]{1,0:T(8,128)(2,1)S(1)}, bf16[64,1792]{1,0:T(8,128)(2,1)S(1)}, u32[]{:S(2)}, u32[]{:S(2)}) collective-permute-start(bf16[64,1792]{1,0:T(8,128)(2,1)S(1)} %reduce_sum.22), channel_id=1, source_target_pairs={{19,0},{18,1},{17,2},{16,3},{1,16},{0,17},{3,18},{2,19},{23,4},{22... | collective-permute-start | bytes 688136 | tf_op jit(solution)/shard_map/ppermute | solution.py:37
  71.4 9.1 %collective-permute-start.5 = (bf16[64,1792]{1,0:T(8,128)(2,1)S(1)}, bf16[64,1792]{1,0:T(8,128)(2,1)S(1)}, u32[]{:S(2)}, u32[]{:S(2)}) collective-permute-start(bf16[64,1792]{1,0:T(8,128)(2,1)S(1)} %reduce_sum.22), channel_id=1, source_target_pairs={{3,0},{2,1},{1,2},{0,3},{17,16},{16,17},{19,18},{18,19},{7,4},{6,5... | collective-permute-start | bytes 688136 | tf_op jit(solution)/shard_map/ppermute | solution.py:37
  71.5 9.0 %collective-permute-start.4 = (bf16[64,1792]{1,0:T(8,128)(2,1)S(1)}, bf16[64,1792]{1,0:T(8,128)(2,1)S(1)}, u32[]{:S(2)}, u32[]{:S(2)}) collective-permute-start(bf16[64,1792]{1,0:T(8,128)(2,1)S(1)} %reduce_sum.22), channel_id=1, source_target_pairs={{16,0},{17,1},{18,2},{19,3},{0,16},{1,17},{2,18},{3,19},{20,4},{21... | collective-permute-start | bytes 688136 | tf_op jit(solution)/shard_map/ppermute | solution.py:37
  84.0 82.4 %copy-start.9 = (f32[7168]{0:T(1024)S(1)}, f32[7168]{0:T(1024)}, u32[]{:S(2)}) copy-start(f32[7168]{0:T(1024)} %param.12) | copy-start | bytes 86020
  84.0 79.2 %all-to-all-start.1 = ((bf16[16,40,3584]{2,1,0:T(8,128)(2,1)}), bf16[16,40,3584]{2,1,0:T(8,128)(2,1)}, u32[]{:S(2)}, u32[]{:S(2)}) async-start(bf16[16,40,3584]{2,1,0:T(8,128)(2,1)} %bitcast.53), calls=%async_computation.1 | async-start | bytes 9175040 | tf_op jit(solution)/shard_map/all_to_all | solution.py:20
  89.3 72.1 %collective-permute-start.7 = (bf16[3584,512]{1,0:T(8,128)(2,1)}, bf16[3584,512]{1,0:T(8,128)(2,1)S(1)}, u32[]{:S(2)}, u32[]{:S(2)}) collective-permute-start(bf16[3584,512]{1,0:T(8,128)(2,1)} %shard_map.93), channel_id=1, source_target_pairs={{1,0},{0,1},{3,2},{2,3},{19,16},{18,17},{17,18},{16,19},{5,4},{4,5... | collective-permute-start | bytes 11010056 | tf_op jit(solution)/shard_map/ppermute | solution.py:37
  89.4 71.0 %collective-permute-start.8 = (bf16[256,1792]{1,0:T(8,128)(2,1)}, bf16[256,1792]{1,0:T(8,128)(2,1)S(1)}, u32[]{:S(2)}, u32[]{:S(2)}) collective-permute-start(bf16[256,1792]{1,0:T(8,128)(2,1)} %get-tuple-element.42), channel_id=1, source_target_pairs={{0,1},{1,2},{2,3},{3,0},{4,5},{5,6},{6,7},{7,4},{8,9},{9,10},{10,1... | collective-permute-start | bytes 2752520 | tf_op jit(solution)/shard_map/ppermute | solution.py:16
  91.5 69.0 %collective-permute-start.9 = (bf16[256,1792]{1,0:T(8,128)(2,1)}, bf16[256,1792]{1,0:T(8,128)(2,1)S(1)}, u32[]{:S(2)}, u32[]{:S(2)}) collective-permute-start(bf16[256,1792]{1,0:T(8,128)(2,1)} %get-tuple-element.43), channel_id=1, source_target_pairs={{0,3},{1,0},{2,1},{3,2},{4,7},{5,4},{6,5},{7,6},{8,11},{9,8},{10,9... | collective-permute-start | bytes 2752520 | tf_op jit(solution)/shard_map/ppermute | solution.py:16
  92.8 67.6 %collective-permute-start.11 = (bf16[128,1792]{1,0:T(8,128)(2,1)S(1)}, bf16[128,1792]{1,0:T(8,128)(2,1)S(1)}, u32[]{:S(2)}, u32[]{:S(2)}) collective-permute-start(bf16[128,1792]{1,0:T(8,128)(2,1)S(1)} %get-tuple-element.65), channel_id=1, source_target_pairs={{0,3},{1,0},{2,1},{3,2},{4,7},{5,4},{6,5},{7,6},{8,11},{9,8},{10,9... | collective-permute-start | bytes 1376264 | tf_op jit(solution)/shard_map/ppermute | solution.py:16
  93.1 67.3 %collective-permute-start.10 = (bf16[128,1792]{1,0:T(8,128)(2,1)S(1)}, bf16[128,1792]{1,0:T(8,128)(2,1)}, u32[]{:S(2)}, u32[]{:S(2)}) collective-permute-start(bf16[128,1792]{1,0:T(8,128)(2,1)S(1)} %get-tuple-element.66), channel_id=1, source_target_pairs={{0,1},{1,2},{2,3},{3,0},{4,5},{5,6},{6,7},{7,4},{8,9},{9,10},{10,1... | collective-permute-start | bytes 1376264 | tf_op jit(solution)/shard_map/ppermute | solution.py:16
  160.4 2.8 %copy-start.10 = (bf16[128,1792]{1,0:T(8,128)(2,1)}, bf16[128,1792]{1,0:T(8,128)(2,1)S(1)}, u32[]{:S(2)}) copy-start(bf16[128,1792]{1,0:T(8,128)(2,1)S(1)} %collective-permute-done.11) | copy-start | bytes 1376260
  160.4 1.0 copy-start.3
  161.4 1.8 copy-start
  163.2 12.3 %collective-permute-start.12 = (bf16[128,1792]{1,0:T(8,128)(2,1)}, bf16[128,1792]{1,0:T(8,128)(2,1)S(1)}, u32[]{:S(2)}, u32[]{:S(2)}) collective-permute-start(bf16[128,1792]{1,0:T(8,128)(2,1)} %collective-permute-done.10), channel_id=1, source_target_pairs={{0,1},{1,2},{2,3},{3,0},{4,5},{5,6},{6,7},{7,4},{8,9},{9,10},{10,1... | collective-permute-start | bytes 1376264 | tf_op jit(solution)/shard_map/ppermute | solution.py:16
  163.5 12.9 %collective-permute-start.13 = (bf16[128,1792]{1,0:T(8,128)(2,1)}, bf16[128,1792]{1,0:T(8,128)(2,1)S(1)}, u32[]{:S(2)}, u32[]{:S(2)}) collective-permute-start(bf16[128,1792]{1,0:T(8,128)(2,1)} %copy-done.10), channel_id=1, source_target_pairs={{0,3},{1,0},{2,1},{3,2},{4,7},{5,4},{6,5},{7,6},{8,11},{9,8},{10,9... | collective-permute-start | bytes 1376264 | tf_op jit(solution)/shard_map/ppermute | solution.py:16
  166.5 2.0 copy-start.1
  168.6 10.8 %copy-start.2 = (bf16[3584,512]{1,0:T(8,128)(2,1)S(1)}, bf16[3584,512]{1,0:T(8,128)(2,1)}, u32[]{:S(2)}) copy-start(bf16[3584,512]{1,0:T(8,128)(2,1)} %shard_map.92) | copy-start | bytes 11010052
  173.6 8.3 %collective-permute-start.15 = (f32[640,1]{1,0:T(8,128)S(1)}, f32[640,1]{1,0:T(8,128)S(1)}, u32[]{:S(2)}, u32[]{:S(2)}) collective-permute-start(f32[640,1]{1,0:T(8,128)S(1)} %get-tuple-element.55), channel_id=1, source_target_pairs={{1,0},{0,1},{3,2},{2,3},{19,16},{18,17},{17,18},{16,19},{5,4},{4,5... | collective-permute-start | bytes 7688 | tf_op jit(solution)/shard_map/ppermute | solution.py:37
  175.5 1.0 copy-start.5
  177.3 10.7 %collective-permute-start.14 = (bf16[640,512]{1,0:T(8,128)(2,1)S(1)}, bf16[640,512]{1,0:T(8,128)(2,1)S(1)}, u32[]{:S(2)}, u32[]{:S(2)}) collective-permute-start(bf16[640,512]{1,0:T(8,128)(2,1)S(1)} %get-tuple-element.52), channel_id=1, source_target_pairs={{1,0},{0,1},{3,2},{2,3},{19,16},{18,17},{17,18},{16,19},{5,4},{4,5... | collective-permute-start | bytes 1966088 | tf_op jit(solution)/shard_map/ppermute | solution.py:37
  188.4 16.5 %copy-start.4 = (bf16[256,1792]{1,0:T(8,128)(2,1)S(1)}, bf16[256,1792]{1,0:T(8,128)(2,1)}, u32[]{:S(2)}) copy-start(bf16[256,1792]{1,0:T(8,128)(2,1)} %copy-done.3) | copy-start | bytes 2752516
  188.4 18.0 %collective-permute-start.18 = (bf16[640,256]{1,0:T(8,128)(2,1)S(1)}, bf16[640,256]{1,0:T(8,128)(2,1)S(1)}, u32[]{:S(2)}, u32[]{:S(2)}) collective-permute-start(bf16[640,256]{1,0:T(8,128)(2,1)S(1)} %fusion.7), channel_id=1, source_target_pairs={{0,2},{1,3},{2,0},{3,1},{4,6},{5,7},{6,4},{7,5},{8,10},{9,11},{10,... | collective-permute-start | bytes 983048 | tf_op jit(solution)/shard_map/ppermute | solution.py:16
  191.4 14.3 %collective-permute-start.17 = (bf16[640,256]{1,0:T(8,128)(2,1)S(1)}, bf16[640,256]{1,0:T(8,128)(2,1)S(1)}, u32[]{:S(2)}, u32[]{:S(2)}) collective-permute-start(bf16[640,256]{1,0:T(8,128)(2,1)S(1)} %fusion.7), channel_id=1, source_target_pairs={{0,3},{1,0},{2,1},{3,2},{4,7},{5,4},{6,5},{7,6},{8,11},{9,8},{10,9... | collective-permute-start | bytes 983048 | tf_op jit(solution)/shard_map/ppermute | solution.py:16
  193.2 11.7 %collective-permute-start.16 = (bf16[640,256]{1,0:T(8,128)(2,1)S(1)}, bf16[640,256]{1,0:T(8,128)(2,1)S(1)}, u32[]{:S(2)}, u32[]{:S(2)}) collective-permute-start(bf16[640,256]{1,0:T(8,128)(2,1)S(1)} %fusion.7), channel_id=1, source_target_pairs={{0,1},{1,2},{2,3},{3,0},{4,5},{5,6},{6,7},{7,4},{8,9},{9,10},{10,1... | collective-permute-start | bytes 983048 | tf_op jit(solution)/shard_map/ppermute | solution.py:16
  205.7 1.0 copy-start.6
  206.5 1.1 copy-start.8
  245.1 1.9 collective-permute-start.19
  (1 other events, 0.8 us)

commit v4 on v3

--- a/solution.py
+++ b/solution.py
@@ -1,3 +1,5 @@
+import functools
+
 import jax
 import jax.numpy as jnp
 from jax import lax
@@ -76,26 +78,28 @@
 
 def first_body(a_ref, gain_ref, w_ref, g_ref, s_ref, o_ref):
     depth = a_ref.shape[1]
-    step = depth // 7
-    total = None
+    h = w_ref.shape[1]
     squares = None
-    for at in range(0, depth, step):
-        wide = a_ref[:, at : at + step].astype(F32)
-        for i in range(0, step, 128):
+    for at in range(0, depth, 256):
+        wide = a_ref[:, at : at + 256].astype(F32)
+        for i in range(0, 256, 128):
             part = wide[:, i : i + 128]
             squares = part * part if squares is None else squares + part * part
-        gained = (wide * gain_ref[:, at : at + step]).astype(BF16)
-        g_ref[:, at : at + step] = gained
-        piece = jnp.dot(gained, w_ref[at : at + step, :], preferred_element_type=F32)
-        total = piece if total is None else total + piece
-    o_ref[...] = total.astype(BF16)
+        g_ref[:, at : at + 256] = (wide * gain_ref[:, at : at + 256]).astype(BF16)
+    gained = g_ref[...]
+    for i in range(2):
+        o_ref[:, i * h : (i + 1) * h] = jnp.dot(
+            gained, w_ref[i * depth : (i + 1) * depth, :], preferred_element_type=F32
+        ).astype(BF16)
     s_ref[...] = jnp.sum(squares, axis=1, keepdims=True)
+
+
+WHOLE = pl.BlockSpec(memory_space=pltpu.VMEM)
 
 
 def first_product(arrived, gain, weight):
     rows, depth = arrived.shape
-    cols = weight.shape[1]
-    whole = pl.BlockSpec(memory_space=pltpu.VMEM)
+    cols = 2 * weight.shape[1]
     return pl.pallas_call(
         first_body,
         out_shape=(
@@ -103,15 +107,91 @@
             jax.ShapeDtypeStruct((rows, 1), F32),
             jax.ShapeDtypeStruct((rows, cols), BF16),
         ),
-        in_specs=[whole] * 3,
-        out_specs=(whole,) * 3,
+        in_specs=[WHOLE] * 3,
+        out_specs=(WHOLE,) * 3,
         compiler_params=pltpu.CompilerParams(vmem_limit_bytes=32 << 20),
         cost_estimate=pl.CostEstimate(
             flops=2 * rows * depth * cols,
             bytes_accessed=2 * (2 * rows * depth + depth * cols + rows * cols),
             transcendentals=0,
         ),
-    )(arrived, gain[None, :], weight)
+    )(arrived, gain, weight)
+
+
+def down_body(start, *refs):
+    own, from_mate, from_twin, from_far, w_own, w_mate, w_twin, w_far, o_ref = refs
+    h = own.shape[1]
+    for j in range(o_ref.shape[1] // h):
+        cols = slice(j * h, (j + 1) * h)
+        at = slice(start + j * h, start + (j + 1) * h)
+        total = jnp.dot(own[...], w_own[:, cols], preferred_element_type=F32)
+        total += jnp.dot(from_mate[...], w_mate[at, :], preferred_element_type=F32)
+        total += jnp.dot(from_twin[...], w_twin[:, cols], preferred_element_type=F32)
+        total += jnp.dot(from_far[...], w_far[cols, :], preferred_element_type=F32)
+        o_ref[:, cols] = total.astype(BF16)
+
+
+def down_product(blocks, weights, start):
+    rows, h = blocks[0].shape
+    cols = weights[0].shape[1]
+    return pl.pallas_call(
+        functools.partial(down_body, start),
+        out_shape=jax.ShapeDtypeStruct((rows, cols), BF16),
+        in_specs=[WHOLE] * 8,
+        out_specs=WHOLE,
+        compiler_params=pltpu.CompilerParams(vmem_limit_bytes=32 << 20),
+        cost_estimate=pl.CostEstimate(
+            flops=8 * rows * h * cols,
+            bytes_accessed=2 * (4 * rows * h + 4 * h * cols + rows * cols),
+            transcendentals=0,
+        ),
+    )(*blocks, *weights)
+
+
+def bundle_body(at_ref, g_ref, u_ref, d_ref, o_ref):
+    step = pl.program_id(0)
+    h = o_ref.shape[1]
+
+    @pl.when(step < 2)
+    def _():
+        o_ref[...] = g_ref[0]
+
+    @pl.when((step >= 2) & (step < 4))
+    def _():
+        o_ref[...] = u_ref[0]
+
+    @pl.when(step >= 4)
+    def _():
+        for j in range(d_ref.shape[2] // h):
+            o_ref[j * h : (j + 1) * h, :] = d_ref[0, :, j * h : (j + 1) * h]
+
+
+def bundle(at, gate, up, down):
+    deep, h = gate.shape[1:]
+    cut = deep // 4
+
+    def pick(last_first):
+        return lambda i, at: at[jnp.where(i <= last_first, 0, 1)]
+
+    gate_at, up_at, down_at = pick(0), pick(2), pick(4)
+    return pl.pallas_call(
+        bundle_body,
+        out_shape=jax.ShapeDtypeStruct((6 * cut, h), BF16),
+        grid_spec=pltpu.PrefetchScalarGridSpec(
+            num_scalar_prefetch=1,
+            grid=(6,),
+            in_specs=[
+                pl.BlockSpec((1, cut, h), lambda i, at: (0, gate_at(i, at), 0)),
+                pl.BlockSpec((1, cut, h), lambda i, at: (0, up_at(i, at), 0)),
+                pl.BlockSpec((1, h, cut), lambda i, at: (0, 0, down_at(i, at))),
+            ],
+            out_specs=pl.BlockSpec((cut, h), lambda i, at: (i, 0)),
+        ),
+        compiler_params=pltpu.CompilerParams(vmem_limit_bytes=56 << 20),
+        cost_estimate=pl.CostEstimate(
+            flops=0, bytes_accessed=24 * cut * h, transcendentals=0
+        ),
+    )(at, gate, up, down)
 
 
 def pack_body(at_ref, g_ref, u_ref, o_ref):
@@ -156,13 +236,24 @@
     tokens_core = nx * rows_here
     tokens = nc * tokens_core
 
+    to_mate = lambda value: from_places(value, lambda c, x: (c, mate_of(c, x)))
+    to_twin = lambda value: from_places(value, lambda c, x: (c, twin_of(c, x)))
+
+    def cut_down(at):
+        return lax.dynamic_slice(
+            down_proj[0], (0, at * quarter), (down_proj.shape[1], quarter)
+        )
+
+    twin_cut, context = lax.optimization_barrier((cut_down(twin), context))
+    twin_down = to_twin(twin_cut)
+
     mine = lax.axis_index("z") * nx + x
     part = project(mine[None].astype(jnp.int32), context, out_proj, residual, nx)
 
     meta = jnp.concatenate([expert_ids.astype(BF16), gates], axis=1)
     meta = jnp.pad(meta, ((0, 0), (0, 128 - meta.shape[1])))
     came = [meta] + [shift(meta, "x", k) for k in range(1, nx)]
-    part, came = lax.optimization_barrier((part, came))
+    part, came, twin_down, down_proj = lax.optimization_barrier((part, came, twin_down, down_proj))
     part = exchange(part.reshape(nx * nz, tokens_core, quarter), ("x", "z"))
     ring = [came[(nx - m) % nx] for m in range(nx)]
     ring = jnp.concatenate(ring + ring[:-1], axis=0)
@@ -191,15 +282,13 @@
     scaled = jnp.where(chosen, weighted.T[:, None, :], F32(0)).astype(BF16)
     scaled = scaled.reshape(places * slots, tokens)
     kept = pack(jnp.stack([x, twin]).astype(jnp.int32), gate_proj, up_proj)
-    given = pack(jnp.stack([mate, x ^ 2]).astype(jnp.int32), gate_proj, up_proj)
-
-    def cut_down(k):
-        at = lax.rem(x + k, nx) * quarter
-        return lax.dynamic_slice(down_proj[0], (0, at), (down_proj.shape[1], quarter))
-
-    down_cut = [cut_down(k) for k in range(nx)]
-    selector, scaled, part, kept, given, down_cut = lax.optimization_barrier(
-        (selector, scaled, part, kept, given, down_cut)
+    given = bundle(jnp.stack([mate, x ^ 2]).astype(jnp.int32), gate_proj, up_proj, down_proj)
+    own_down = cut_down(x)
+    gain = jnp.concatenate(
+        [lax.dynamic_slice(norm_gain, (q * quarter,), (quarter,)) for q in (x, twin)]
+    )[None, :]
+    selector, scaled, part, kept, given, own_down, gain = lax.optimization_barrier(
+        (selector, scaled, part, kept, given, own_down, gain)
     )
 
     hidden = jnp.sum(part.astype(F32), axis=0).astype(BF16)
@@ -208,6 +297,9 @@
     twin_own = from_places(hidden, lambda c, x: (c, twin_of(c, x)))
     near_other = from_places(hidden, lambda c, x: (1 - c, x))
     twin_other = from_places(hidden, lambda c, x: (1 - c, twin_of(c, x)))
+    twin_own, near_other, twin_other, given = lax.optimization_barrier(
+        (twin_own, near_other, twin_other, given)
+    )
     rows = jnp.concatenate(
         [
             jnp.concatenate([hidden, near_other], axis=0),
@@ -219,21 +311,12 @@
     arrived = exchange(outgoing.reshape(places, slots, 2 * quarter), ("y", "z"))
     arrived = arrived.reshape(places * slots, 2 * quarter)
 
-    taken = from_places(given, lambda c, x: (c, mate_of(c, x)))
-    half = down_cut[2].shape[0] // 2
-    hop_up, hop_down = shift(down_cut[2][:half], "x", 1), shift(down_cut[2][half:], "x", -1)
-    down_by = [down_cut[0], shift(down_cut[1], "x", 1), None, shift(down_cut[3], "x", 3)]
-    arrived, taken, down_by[1], down_by[3], hop_up, hop_down = lax.optimization_barrier(
-        (arrived, taken, down_by[1], down_by[3], hop_up, hop_down)
-    )
-    hop_up, hop_down = shift(hop_up, "x", 1), shift(hop_down, "x", -1)
-
-    gain = jnp.concatenate(
-        [lax.dynamic_slice(norm_gain, (q * quarter,), (quarter,)) for q in (x, twin)]
-    )
-    to_mate = lambda value: from_places(value, lambda c, x: (c, mate_of(c, x)))
+    taken = to_mate(given)
+    arrived, taken = lax.optimization_barrier((arrived, taken))
     gained, square, theirs = first_product(arrived, gain, taken)
-    theirs, hop_up, hop_down = lax.optimization_barrier((theirs, hop_up, hop_down))
+    theirs, taken = lax.optimization_barrier((theirs, taken))
+    deep = taken.shape[0] // 6
+    far_down = to_twin(taken[5 * deep :])
     came_back = to_mate(theirs)
     inverse = lax.rsqrt((square + to_mate(square)) / width + 1e-06)
     total = jnp.dot(gained, kept, preferred_element_type=F32)
@@ -242,15 +325,11 @@
     total = total * inverse
     hid = total.shape[1] // 2
     activated = (jax.nn.silu(total[:, :hid]) * total[:, hid:]).astype(BF16)
-    result = jnp.dot(activated, down_by[0], preferred_element_type=F32)
-    for k in (1, 3):
-        block = shift(activated, "x", k)
-        result += jnp.dot(block, down_by[k], preferred_element_type=F32)
-    block = shift(activated, "x", 2)
-    result += jnp.dot(block[:, :half], hop_up, preferred_element_type=F32)
-    result += jnp.dot(block[:, half:], hop_down, preferred_element_type=F32)
-
-    returned = exchange(result.astype(BF16).reshape(places, slots, quarter), ("y", "z"))
+    activated, far_down = lax.optimization_barrier((activated, far_down))
+    blocks = (activated, to_mate(activated), to_twin(activated), shift(activated, "x", 2))
+    result = down_product(blocks, (own_down, taken, twin_down, far_down), 4 * deep)
+
+    returned = exchange(result.reshape(places, slots, quarter), ("y", "z"))
     returned = returned.reshape(places * slots, quarter)
     mixture = lax.dot_general(
         scaled, returned, (((0,), (0,)), ((), ())), preferred_element_type=F32

time: 259 us -> 242 us (0.934)
  blocking collectives: 46.1 us -> 106 us
  waiting for transfers between devices: 129 us -> 72.3 us
  starting transfers between devices: 33.8 us -> 23.9 us
  local copies, waits for them, and re-layouts: 11.1 us -> 4.2 us
  matrix products: 10.8 us -> 4.42 us
  Pallas kernels: 20.1 us -> 24.4 us
    ppermute x14 -> x6, waiting for transfers between devices: 80.8 us -> 13.1 us  [shift(): lax.ppermute(value, axis, [(i, (i + amount) % size) for i in range(size)])]
    all_to_all x2 -> x3, blocking collectives: 46.1 us -> 106 us  [exchange(): return lax.all_to_all(value, axes, split_axis=0, concat_axis=0, tiled=True)]
    ppermute x14 -> x6, starting transfers between devices: 18.3 us -> 3.48 us  [shift(): lax.ppermute(value, axis, [(i, (i + amount) % size) for i in range(size)])]
    ppermute x6 -> x10, waiting for transfers between devices: 14.4 us -> 28.8 us  [from_places(): return lax.ppermute(value, ('c', 'x'), pairs)]
    pallas_call x0 -> x2, Pallas kernels: none -> 10.4 us  [the longest x1 7.88 us: bundle(): pl.pallas_call(bundle_body, out_shape=jax.ShapeDtypeStruct((6 * cut, h),...]
    ppermute x6 -> x10, starting transfers between devices: 2.97 us -> 12.6 us  [from_places(): return lax.ppermute(value, ('c', 'x'), pairs)]
    unnamed x22 -> x4, local copies, waits for them, and re-layouts: 5.88 us -> 0.01 us
    all_to_all x2 -> x1, starting transfers between devices: 12.6 us -> 7.77 us  [exchange(): return lax.all_to_all(value, axes, split_axis=0, concat_axis=0, tiled=True)]
  transfers between devices with their start and end apart: 22 -> 17, of which waited for: 9 -> 11; matrix products, arithmetic and copies ran while one was open for 4% -> 4% of each run, Pallas kernels for 8% -> 8%
where the time goes in v4:
time: 242 us
  blocking collectives  106 us (44%)
  waiting for transfers between devices  72.3 us (30%)
  Pallas kernels  24.4 us (10%)
  starting transfers between devices  23.9 us (10%)
  other arithmetic  6.5 us (3%)
  matrix products  4.42 us (2%)
  local copies, waits for them, and re-layouts  4.2 us (2%)
    all_to_all x3, blocking collectives, exchange(): return lax.all_to_all(value, axes, split_axis=0, concat_axis=0, tiled=True)  106 us
    all_to_all x1, waiting for transfers between devices, exchange(): return lax.all_to_all(value, axes, split_axis=0, concat_axis=0, tiled=True)  30.4 us
    ppermute x10, waiting for transfers between devices, from_places(): return lax.ppermute(value, ('c', 'x'), pairs)  28.8 us
    ppermute x6, waiting for transfers between devices, shift(): lax.ppermute(value, axis, [(i, (i + amount) % size) for i in range(size)])  13.1 us
    ppermute x10, starting transfers between devices, from_places(): return lax.ppermute(value, ('c', 'x'), pairs)  12.6 us
    pallas_call x1, Pallas kernels, bundle(): pl.pallas_call(bundle_body, out_shape=jax.ShapeDtypeStruct((6 * cut, h),...  7.88 us
    all_to_all x1, starting transfers between devices, exchange(): return lax.all_to_all(value, axes, split_axis=0, concat_axis=0, tiled=True)  7.77 us
    pallas_call x1, Pallas kernels, project(): pl.pallas_call(project_body, out_shape=jax.ShapeDtypeStruct((blocks, rows...  6.91 us
  transfers between devices with their start and end apart: 17, of which 11 were waited for; matrix products, arithmetic and copies ran while one was open for 4% of the time, Pallas kernels for 8%

profile of v4, /device:TPU:0, one launch (start us, length us, event | category | flops | bytes accessed | tf_op | source)
XLA Modules:
  0.0 241.7 jit_solution(5660704521822275996)
XLA Ops:
  0.0 1.2 dynamic-slice_bitcast_fusion.1
  1.2 2.9 %collective-permute-start.3 = (bf16[256,1792]{1,0:T(8,128)(2,1)S(1)}, bf16[256,1792]{1,0:T(8,128)(2,1)S(1)}, u32[]{:S(2)}, u32[]{:S(2)}) collective-permute-start(bf16[256,1792]{1,0:T(8,128)(2,1)S(1)} %dynamic-slice_bitcast_fusion.1), channel_id=1, source_target_pairs={{3,0},{2,1},{1,2},{0,3},{17,16},{16,17},{19,18},{18,19},{7,4},{6,5... | collective-permute-start | bytes 2752520 | tf_op jit(solution)/shard_map/ppermute | solution.py:39
  5.9 1.9 collective-permute-start.1
  7.8 6.9 %shard_map.91 = bf16[4,256,1792]{2,1,0:T(8,128)(2,1)} custom-call(s32[1]{0:T(128)} %bitcast.mine_ref, bf16[256,512]{1,0:T(8,128)(2,1)} %a_ref, bf16[512,7168]{1,0:T(8,128)(2,1)} %b_ref.1, bf16[16,7168]{1,0:T(8,128)(2,1)} %r_ref.1), custom_call_target="tpu_custom_call" | custom-call | flops 1879048192 | bytes 11272192 | tf_op jit(solution)/shard_map/pallas_call | solution.py:56
  14.7 1.7 collective-permute-done.2
  16.5 0.8 collective-permute-done
  17.3 7.8 %all-to-all-start = ((bf16[16,64,1792]{2,1,0:T(8,128)(2,1)}), bf16[16,64,1792]{2,1,0:T(8,128)(2,1)}, u32[]{:S(2)}, u32[]{:S(2)}) async-start(bf16[16,64,1792]{2,1,0:T(8,128)(2,1)} %bitcast.44), calls=%async_computation | async-start | bytes 7340032 | tf_op jit(solution)/shard_map/all_to_all | solution.py:22
  26.2 4.1 %shard_map.92 = bf16[3584,512]{1,0:T(8,128)(2,1)} custom-call(s32[2]{0:T(128)} %get-tuple-element.71.at_ref, bf16[1,7168,256]{2,1,0:T(8,128)(2,1)} %g_ref.3, bf16[1,7168,256]{2,1,0:T(8,128)(2,1)} %u_ref.3), custom_call_target="tpu_custom_call" | custom-call | bytes 7340032 | tf_op jit(solution)/shard_map/pallas_call | solution.py:207
  30.6 1.2 dynamic-slice_bitcast_fusion.refs_4_
  31.8 7.9 %shard_map.93 = bf16[10752,256]{1,0:T(8,128)(2,1)} custom-call(s32[2]{0:T(128)} %get-tuple-element.72.at_ref, bf16[1,7168,256]{2,1,0:T(8,128)(2,1)} %g_ref.3, bf16[1,7168,256]{2,1,0:T(8,128)(2,1)} %u_ref.3, bf16[1,256,7168]{2,1,0:T(8,128)(2,1)} %d_ref), custom_call_target="tpu_custom_call" | custom-call | bytes 11010048 | tf_op jit(solution)/shard_map/pallas_call | solution.py:177
  41.3 30.4 %all-to-all-done = bf16[16,64,1792]{2,1,0:T(8,128)(2,1)} async-done(((bf16[16,64,1792]{2,1,0:T(8,128)(2,1)}), bf16[16,64,1792]{2,1,0:T(8,128)(2,1)}, u32[]{:S(2)}, u32[]{:S(2)}) %all-to-all-start) | async-done | bytes 3670048 | tf_op jit(solution)/shard_map/all_to_all | solution.py:22
  71.7 2.6 %reduce_sum.22 = bf16[64,1792]{1,0:T(8,128)(2,1)S(1)} reduce(bf16[16,64,1792]{2,1,0:T(8,128)(2,1)} %all-to-all-done, bf16[]{:T(256)} %constant.62.clone.1), dimensions={0}, to_apply=%region_3.4 | reduce | flops 1720320 | bytes 3899394 | tf_op jit(solution)/shard_map/reduce_sum | solution.py:294
  74.8 2.8 %collective-permute-start.5 = (bf16[64,1792]{1,0:T(8,128)(2,1)S(1)}, bf16[64,1792]{1,0:T(8,128)(2,1)S(1)}, u32[]{:S(2)}, u32[]{:S(2)}) collective-permute-start(bf16[64,1792]{1,0:T(8,128)(2,1)S(1)} %reduce_sum.22), channel_id=1, source_target_pairs={{3,0},{2,1},{1,2},{0,3},{17,16},{16,17},{19,18},{18,19},{7,4},{6,5... | collective-permute-start | bytes 688136 | tf_op jit(solution)/shard_map/ppermute | solution.py:39
  77.7 4.7 %collective-permute-done.7 = bf16[64,1792]{1,0:T(8,128)(2,1)S(1)} collective-permute-done((bf16[64,1792]{1,0:T(8,128)(2,1)S(1)}, bf16[64,1792]{1,0:T(8,128)(2,1)S(1)}, u32[]{:S(2)}, u32[]{:S(2)}) %collective-permute-start.7) | collective-permute-done | bytes 229408 | tf_op jit(solution)/shard_map/ppermute | solution.py:39
  82.3 1.1 collective-permute-done.5
  83.5 1.3 convolution_convert_fusion
  84.8 60.5 %all_to_all.20 = bf16[16,40,3584]{2,1,0:T(8,128)(2,1)S(1)} all-to-all(bf16[16,40,3584]{2,1,0:T(8,128)(2,1)S(1)} %bitcast.43), channel_id=1, replica_groups=mesh['y'=4,'c'=2,'z'=4,'x'=4] {'y','z'}, dimensions={0} | all-to-all | bytes 9175040 | tf_op jit(solution)/shard_map/all_to_all | solution.py:22
  145.3 1.0 collective-permute-done.8.w_ref.refs_5_
  146.2 3.0 %shard_map.94 = (bf16[640,3584]{1,0:T(8,128)(2,1)S(1)}, f32[640,1]{1,0:T(8,128)S(1)}, bf16[640,512]{1,0:T(8,128)(2,1)S(1)}) custom-call(bf16[640,3584]{1,0:T(8,128)(2,1)S(1)} %bitcast.41, f32[1,3584]{1,0:T(1,128)S(1)} %broadcast_in_dim.50.gain_ref, bf16[10752,256]{1,0:T(8,128)(2,1)S(1)} %collective-permute-done.8.w_ref.refs_5_), custom_call_target="tpu_custom_call" | custom-call | flops 2348810240 | bytes 13500416 | tf_op jit(solution)/shard_map/pallas_call | solution.py:103
  149.2 2.0 collective-permute-start.9
  151.3 1.7 collective-permute-start.11
  153.0 2.5 %fusion.24 = f32[640,512]{1,0:T(8,128)S(1)} fusion(bf16[640,3584]{1,0:T(8,128)(2,1)S(1)} %get-tuple-element.55, bf16[3584,512]{1,0:T(8,128)(2,1)S(1)} %copy-done), kind=kOutput, calls=%fused_computation.48 | convolution fusion | flops 2348810240 | bytes 9568256 | tf_op jit(solution)/shard_map/dot_general | solution.py:322
  155.5 4.2 %collective-permute-done.10 = f32[640,1]{1,0:T(8,128)S(1)} collective-permute-done((f32[640,1]{1,0:T(8,128)S(1)}, f32[640,1]{1,0:T(8,128)S(1)}, u32[]{:S(2)}, u32[]{:S(2)}) %collective-permute-start.10) | collective-permute-done | bytes 2592 | tf_op jit(solution)/shard_map/ppermute | solution.py:39
  160.0 13.1 %collective-permute-done.9 = bf16[640,512]{1,0:T(8,128)(2,1)S(1)} collective-permute-done((bf16[640,512]{1,0:T(8,128)(2,1)S(1)}, bf16[640,512]{1,0:T(8,128)(2,1)S(1)}, u32[]{:S(2)}, u32[]{:S(2)}) %collective-permute-start.9) | collective-permute-done | bytes 655392 | tf_op jit(solution)/shard_map/ppermute | solution.py:39
  173.5 1.1 collective-permute-start.14
  174.5 1.8 collective-permute-start.13
  177.0 8.7 %collective-permute-done.14.refs_3_ = bf16[640,256]{1,0:T(8,128)(2,1)S(1)} collective-permute-done((bf16[640,256]{1,0:T(8,128)(2,1)S(1)}, bf16[640,256]{1,0:T(8,128)(2,1)S(1)}, u32[]{:S(2)}, u32[]{:S(2)}) %collective-permute-start.14) | collective-permute-done | bytes 327712 | tf_op jit(solution)/shard_map/ppermute | solution.py:18
  185.7 4.8 %collective-permute-done.13.refs_2_ = bf16[640,256]{1,0:T(8,128)(2,1)S(1)} collective-permute-done((bf16[640,256]{1,0:T(8,128)(2,1)S(1)}, bf16[640,256]{1,0:T(8,128)(2,1)S(1)}, u32[]{:S(2)}, u32[]{:S(2)}) %collective-permute-start.13) | collective-permute-done | bytes 327712 | tf_op jit(solution)/shard_map/ppermute | solution.py:39
  190.5 2.5 %shard_map.95 = bf16[640,1792]{1,0:T(8,128)(2,1)S(1)} custom-call(bf16[640,256]{1,0:T(8,128)(2,1)S(1)} %fusion.7.refs_0_, bf16[640,256]{1,0:T(8,128)(2,1)S(1)} %collective-permute-done.12.refs_1_, bf16[640,256]{1,0:T(8,128)(2,1)S(1)} %collective-permute-done.13.refs_2_, bf16[640,256]{1,0:T(8,128)(2,1)S(1)} %collective-permute-done.14.refs_3_, ...), custom_call_target="tpu_custom_call" | custom-call | flops 2348810240 | bytes 7274496 | tf_op jit(solution)/shard_map/pallas_call | solution.py:137
  193.1 35.8 %all_to_all.21 = bf16[16,40,1792]{2,1,0:T(8,128)(2,1)S(1)} all-to-all(bf16[16,40,1792]{2,1,0:T(8,128)(2,1)S(1)} %bitcast.42), channel_id=1, replica_groups=mesh['y'=4,'c'=2,'z'=4,'x'=4] {'y','z'}, dimensions={0} | all-to-all | bytes 4587520 | tf_op jit(solution)/shard_map/all_to_all | solution.py:22
  229.5 1.8 collective-permute-done.15
  231.4 9.6 %all_to_all.22 = bf16[4,16,1792]{2,1,0:T(8,128)(2,1)S(1)} all-to-all(bf16[4,16,1792]{2,1,0:T(8,128)(2,1)S(1)} %bitcast.47), channel_id=1, replica_groups=mesh['y'=4,'c'=2,'z'=4,'x'=4] {'x'}, dimensions={0} | all-to-all | bytes 458752 | tf_op jit(solution)/shard_map/all_to_all | solution.py:22
  (53 shorter events, 8.1 us)
Async XLA Ops:
  1.2 16.1 %collective-permute-start.3 = (bf16[256,1792]{1,0:T(8,128)(2,1)S(1)}, bf16[256,1792]{1,0:T(8,128)(2,1)S(1)}, u32[]{:S(2)}, u32[]{:S(2)}) collective-permute-start(bf16[256,1792]{1,0:T(8,128)(2,1)S(1)} %dynamic-slice_bitcast_fusion.1), channel_id=1, source_target_pairs={{3,0},{2,1},{1,2},{0,3},{17,16},{16,17},{19,18},{18,19},{7,4},{6,5... | collective-permute-start | bytes 2752520 | tf_op jit(solution)/shard_map/ppermute | solution.py:39
  5.5 10.9 %collective-permute-start.2 = (bf16[16,128]{0,1:T(8,128)(2,1)S(1)}, bf16[16,128]{0,1:T(8,128)(2,1)S(1)}, u32[]{:S(2)}, u32[]{:S(2)}) collective-permute-start(bf16[16,128]{0,1:T(8,128)(2,1)S(1)} %fusion.15), channel_id=1, source_target_pairs={{0,3},{1,0},{2,1},{3,2},{4,7},{5,4},{6,5},{7,6},{8,11},{9,8},{10,9... | collective-permute-start | bytes 12296 | tf_op jit(solution)/shard_map/ppermute | solution.py:18
  5.9 10.5 %collective-permute-start.1 = (bf16[16,128]{0,1:T(8,128)(2,1)S(1)}, bf16[16,128]{0,1:T(8,128)(2,1)S(1)}, u32[]{:S(2)}, u32[]{:S(2)}) collective-permute-start(bf16[16,128]{0,1:T(8,128)(2,1)S(1)} %fusion.15), channel_id=1, source_target_pairs={{0,2},{1,3},{2,0},{3,1},{4,6},{5,7},{6,4},{7,5},{8,10},{9,11},{10,... | collective-permute-start | bytes 12296 | tf_op jit(solution)/shard_map/ppermute | solution.py:18
  7.8 9.5 %collective-permute-start = (bf16[16,128]{0,1:T(8,128)(2,1)S(1)}, bf16[16,128]{0,1:T(8,128)(2,1)S(1)}, u32[]{:S(2)}, u32[]{:S(2)}) collective-permute-start(bf16[16,128]{0,1:T(8,128)(2,1)S(1)} %fusion.15), channel_id=1, source_target_pairs={{0,1},{1,2},{2,3},{3,0},{4,5},{5,6},{6,7},{7,4},{8,9},{9,10},{10,1... | collective-permute-start | bytes 12296 | tf_op jit(solution)/shard_map/ppermute | solution.py:18
  17.3 8.1 %copy-start.1 = (f32[7168]{0:T(1024)S(1)}, f32[7168]{0:T(1024)}, u32[]{:S(2)}) copy-start(f32[7168]{0:T(1024)} %param.12) | copy-start | bytes 86020
  17.3 54.4 %all-to-all-start = ((bf16[16,64,1792]{2,1,0:T(8,128)(2,1)}), bf16[16,64,1792]{2,1,0:T(8,128)(2,1)}, u32[]{:S(2)}, u32[]{:S(2)}) async-start(bf16[16,64,1792]{2,1,0:T(8,128)(2,1)} %bitcast.44), calls=%async_computation | async-start | bytes 7340032 | tf_op jit(solution)/shard_map/all_to_all | solution.py:22
  30.5 9.2 %collective-permute-start.4 = (bf16[64,128]{0,1:T(8,128)(2,1)S(1)}, bf16[64,128]{0,1:T(8,128)(2,1)S(1)}, u32[]{:S(2)}, u32[]{:S(2)}) collective-permute-start(bf16[64,128]{0,1:T(8,128)(2,1)S(1)} %constant_dynamic-slice_fusion), channel_id=1, source_target_pairs={{0,16},{16,0},{1,17},{17,1},{2,18},{18,2},{3,19},{19,3},{4,20},{20... | collective-permute-start | bytes 49160 | tf_op jit(solution)/shard_map/ppermute | solution.py:18
  74.3 8.1 %collective-permute-start.7 = (bf16[64,1792]{1,0:T(8,128)(2,1)S(1)}, bf16[64,1792]{1,0:T(8,128)(2,1)S(1)}, u32[]{:S(2)}, u32[]{:S(2)}) collective-permute-start(bf16[64,1792]{1,0:T(8,128)(2,1)S(1)} %reduce_sum.22), channel_id=1, source_target_pairs={{19,0},{18,1},{17,2},{16,3},{1,16},{0,17},{3,18},{2,19},{23,4},{22... | collective-permute-start | bytes 688136 | tf_op jit(solution)/shard_map/ppermute | solution.py:39
  74.3 8.0 %collective-permute-start.6 = (bf16[64,1792]{1,0:T(8,128)(2,1)S(1)}, bf16[64,1792]{1,0:T(8,128)(2,1)S(1)}, u32[]{:S(2)}, u32[]{:S(2)}) collective-permute-start(bf16[64,1792]{1,0:T(8,128)(2,1)S(1)} %reduce_sum.22), channel_id=1, source_target_pairs={{16,0},{17,1},{18,2},{19,3},{0,16},{1,17},{2,18},{3,19},{20,4},{21... | collective-permute-start | bytes 688136 | tf_op jit(solution)/shard_map/ppermute | solution.py:39
  74.8 8.6 %collective-permute-start.5 = (bf16[64,1792]{1,0:T(8,128)(2,1)S(1)}, bf16[64,1792]{1,0:T(8,128)(2,1)S(1)}, u32[]{:S(2)}, u32[]{:S(2)}) collective-permute-start(bf16[64,1792]{1,0:T(8,128)(2,1)S(1)} %reduce_sum.22), channel_id=1, source_target_pairs={{3,0},{2,1},{1,2},{0,3},{17,16},{16,17},{19,18},{18,19},{7,4},{6,5... | collective-permute-start | bytes 688136 | tf_op jit(solution)/shard_map/ppermute | solution.py:39
  83.4 62.8 %collective-permute-start.8 = (bf16[10752,256]{1,0:T(8,128)(2,1)}, bf16[10752,256]{1,0:T(8,128)(2,1)S(1)}, u32[]{:S(2)}, u32[]{:S(2)}) collective-permute-start(bf16[10752,256]{1,0:T(8,128)(2,1)} %shard_map.93), channel_id=1, source_target_pairs={{1,0},{0,1},{3,2},{2,3},{19,16},{18,17},{17,18},{16,19},{5,4},{4,5... | collective-permute-start | bytes 16515080 | tf_op jit(solution)/shard_map/ppermute | solution.py:39
  146.2 6.8 %copy-start = (bf16[3584,512]{1,0:T(8,128)(2,1)S(1)}, bf16[3584,512]{1,0:T(8,128)(2,1)}, u32[]{:S(2)}) copy-start(bf16[3584,512]{1,0:T(8,128)(2,1)} %shard_map.92) | copy-start | bytes 11010052
  149.2 10.6 %collective-permute-start.10 = (f32[640,1]{1,0:T(8,128)S(1)}, f32[640,1]{1,0:T(8,128)S(1)}, u32[]{:S(2)}, u32[]{:S(2)}) collective-permute-start(f32[640,1]{1,0:T(8,128)S(1)} %get-tuple-element.61), channel_id=1, source_target_pairs={{1,0},{0,1},{3,2},{2,3},{19,16},{18,17},{17,18},{16,19},{5,4},{4,5... | collective-permute-start | bytes 7688 | tf_op jit(solution)/shard_map/ppermute | solution.py:39
  149.2 23.8 %collective-permute-start.9 = (bf16[640,512]{1,0:T(8,128)(2,1)S(1)}, bf16[640,512]{1,0:T(8,128)(2,1)S(1)}, u32[]{:S(2)}, u32[]{:S(2)}) collective-permute-start(bf16[640,512]{1,0:T(8,128)(2,1)S(1)} %get-tuple-element.58), channel_id=1, source_target_pairs={{1,0},{0,1},{3,2},{2,3},{19,16},{18,17},{17,18},{16,19},{5,4},{4,5... | collective-permute-start | bytes 1966088 | tf_op jit(solution)/shard_map/ppermute | solution.py:39
  151.3 22.2 %collective-permute-start.11 = (bf16[1792,256]{1,0:T(8,128)(2,1)S(1)}, bf16[1792,256]{1,0:T(8,128)(2,1)S(1)}, u32[]{:S(2)}, u32[]{:S(2)}) collective-permute-start(bf16[1792,256]{1,0:T(8,128)(2,1)S(1)} %slice.25), channel_id=1, source_target_pairs={{3,0},{2,1},{1,2},{0,3},{17,16},{16,17},{19,18},{18,19},{7,4},{6,5... | collective-permute-start | bytes 2752520 | tf_op jit(solution)/shard_map/ppermute | solution.py:39
  173.5 12.3 %collective-permute-start.14 = (bf16[640,256]{1,0:T(8,128)(2,1)S(1)}, bf16[640,256]{1,0:T(8,128)(2,1)S(1)}, u32[]{:S(2)}, u32[]{:S(2)}) collective-permute-start(bf16[640,256]{1,0:T(8,128)(2,1)S(1)} %fusion.7.refs_0_), channel_id=1, source_target_pairs={{0,2},{1,3},{2,0},{3,1},{4,6},{5,7},{6,4},{7,5},{8,10},{9,11},{10,... | collective-permute-start | bytes 983048 | tf_op jit(solution)/shard_map/ppermute | solution.py:18
  174.5 16.0 %collective-permute-start.13 = (bf16[640,256]{1,0:T(8,128)(2,1)S(1)}, bf16[640,256]{1,0:T(8,128)(2,1)S(1)}, u32[]{:S(2)}, u32[]{:S(2)}) collective-permute-start(bf16[640,256]{1,0:T(8,128)(2,1)S(1)} %fusion.7.refs_0_), channel_id=1, source_target_pairs={{3,0},{2,1},{1,2},{0,3},{17,16},{16,17},{19,18},{18,19},{7,4},{6,5... | collective-permute-start | bytes 983048 | tf_op jit(solution)/shard_map/ppermute | solution.py:39
  176.3 14.2 %collective-permute-start.12 = (bf16[640,256]{1,0:T(8,128)(2,1)S(1)}, bf16[640,256]{1,0:T(8,128)(2,1)S(1)}, u32[]{:S(2)}, u32[]{:S(2)}) collective-permute-start(bf16[640,256]{1,0:T(8,128)(2,1)S(1)} %fusion.7.refs_0_), channel_id=1, source_target_pairs={{1,0},{0,1},{3,2},{2,3},{19,16},{18,17},{17,18},{16,19},{5,4},{4,5... | collective-permute-start | bytes 983048 | tf_op jit(solution)/shard_map/ppermute | solution.py:39
  229.4 1.9 collective-permute-start.15

commit v5 on v4

--- a/solution.py
+++ b/solution.py
@@ -9,6 +9,7 @@
 from jax.sharding import PartitionSpec as P
 
 TOPK = 8
+EARLY = 3
 F32 = jnp.float32
 BF16 = jnp.bfloat16
 
@@ -119,7 +120,7 @@
 
 
 def down_body(start, *refs):
-    own, from_mate, from_twin, from_far, w_own, w_mate, w_twin, w_far, o_ref = refs
+    own, from_mate, from_twin, from_far, w_own, w_mate, w_twin, w_far, w_rest, o_ref = refs
     h = own.shape[1]
     for j in range(o_ref.shape[1] // h):
         cols = slice(j * h, (j + 1) * h)
@@ -127,7 +128,9 @@
         total = jnp.dot(own[...], w_own[:, cols], preferred_element_type=F32)
         total += jnp.dot(from_mate[...], w_mate[at, :], preferred_element_type=F32)
         total += jnp.dot(from_twin[...], w_twin[:, cols], preferred_element_type=F32)
-        total += jnp.dot(from_far[...], w_far[cols, :], preferred_element_type=F32)
+        there = j * h - w_far.shape[0]
+        far = w_far[cols, :] if there < 0 else w_rest[there : there + h, :]
+        total += jnp.dot(from_far[...], far, preferred_element_type=F32)
         o_ref[:, cols] = total.astype(BF16)
 
 
@@ -137,7 +140,7 @@
     return pl.pallas_call(
         functools.partial(down_body, start),
         out_shape=jax.ShapeDtypeStruct((rows, cols), BF16),
-        in_specs=[WHOLE] * 8,
+        in_specs=[WHOLE] * 9,
         out_specs=WHOLE,
         compiler_params=pltpu.CompilerParams(vmem_limit_bytes=32 << 20),
         cost_estimate=pl.CostEstimate(
@@ -313,21 +316,26 @@
 
     taken = to_mate(given)
     arrived, taken = lax.optimization_barrier((arrived, taken))
+    deep = taken.shape[0] // 6
+    early = 5 * deep + EARLY * gate_proj.shape[2]
+    arrived, far_down, far_rest = lax.optimization_barrier(
+        (arrived, taken[5 * deep : early], taken[early:])
+    )
+    far_down = to_twin(far_down)
     gained, square, theirs = first_product(arrived, gain, taken)
-    theirs, taken = lax.optimization_barrier((theirs, taken))
-    deep = taken.shape[0] // 6
-    far_down = to_twin(taken[5 * deep :])
     came_back = to_mate(theirs)
     inverse = lax.rsqrt((square + to_mate(square)) / width + 1e-06)
     total = jnp.dot(gained, kept, preferred_element_type=F32)
-    total, came_back = lax.optimization_barrier((total, came_back))
+    total, came_back, far_down, far_rest = lax.optimization_barrier(
+        (total, came_back, far_down, far_rest)
+    )
+    far_rest = to_twin(far_rest)
     total = total + came_back.astype(F32)
     total = total * inverse
     hid = total.shape[1] // 2
     activated = (jax.nn.silu(total[:, :hid]) * total[:, hid:]).astype(BF16)
-    activated, far_down = lax.optimization_barrier((activated, far_down))
     blocks = (activated, to_mate(activated), to_twin(activated), shift(activated, "x", 2))
-    result = down_product(blocks, (own_down, taken, twin_down, far_down), 4 * deep)
+    result = down_product(blocks, (own_down, taken, twin_down, far_down, far_rest), 4 * deep)
 
     returned = exchange(result.reshape(places, slots, quarter), ("y", "z"))
     returned = returned.reshape(places * slots, quarter)

time: 242 us -> 239 us (0.988)
  waiting for transfers between devices: 72.3 us -> 69.5 us
    ppermute x10 -> x11, waiting for transfers between devices: 28.8 us -> 26 us  [from_places(): return lax.ppermute(value, ('c', 'x'), pairs)]
    ppermute x10 -> x11, starting transfers between devices: 12.6 us -> 14.9 us  [from_places(): return lax.ppermute(value, ('c', 'x'), pairs)]
  transfers between devices with their start and end apart: 17 -> 18, of which waited for: 11 -> 12; matrix products, arithmetic and copies ran while one was open for 4% -> 4% of each run, Pallas kernels for 8% -> 9%
where the time goes in v5:
time: 239 us; the launch traced here: 238 us
  blocking collectives  104 us (44%)
  waiting for transfers between devices  69.5 us (29%)
  starting transfers between devices  25.4 us (11%)
  Pallas kernels  24.4 us (10%)
  other arithmetic  6.49 us (3%)
  matrix products  4.42 us (2%)
  local copies, waits for them, and re-layouts  4.2 us (2%)
    all_to_all x3, blocking collectives, exchange(): return lax.all_to_all(value, axes, split_axis=0, concat_axis=0, tiled=True)  104 us
    all_to_all x1, waiting for transfers between devices, exchange(): return lax.all_to_all(value, axes, split_axis=0, concat_axis=0, tiled=True)  30.4 us
    ppermute x11, waiting for transfers between devices, from_places(): return lax.ppermute(value, ('c', 'x'), pairs)  26 us
    ppermute x11, starting transfers between devices, from_places(): return lax.ppermute(value, ('c', 'x'), pairs)  14.9 us
    ppermute x6, waiting for transfers between devices, shift(): lax.ppermute(value, axis, [(i, (i + amount) % size) for i in range(size)])  13.2 us
    pallas_call x1, Pallas kernels, bundle(): pl.pallas_call(bundle_body, out_shape=jax.ShapeDtypeStruct((6 * cut, h),...  7.87 us
    all_to_all x1, starting transfers between devices, exchange(): return lax.all_to_all(value, axes, split_axis=0, concat_axis=0, tiled=True)  7.77 us
    pallas_call x1, Pallas kernels, project(): pl.pallas_call(project_body, out_shape=jax.ShapeDtypeStruct((blocks, rows...  6.9 us
  transfers between devices with their start and end apart: 18, of which 12 were waited for; matrix products, arithmetic and copies ran while one was open for 4% of the time, Pallas kernels for 9%

profile of v5, /device:TPU:0, one launch (start us, length us, event | category | flops | bytes accessed | tf_op | source)
XLA Modules:
  0.0 238.5 jit_solution(11182313752884466368)
XLA Ops:
  0.0 1.2 dynamic-slice_bitcast_fusion.1
  1.2 2.9 %collective-permute-start.3 = (bf16[256,1792]{1,0:T(8,128)(2,1)S(1)}, bf16[256,1792]{1,0:T(8,128)(2,1)S(1)}, u32[]{:S(2)}, u32[]{:S(2)}) collective-permute-start(bf16[256,1792]{1,0:T(8,128)(2,1)S(1)} %dynamic-slice_bitcast_fusion.1), channel_id=1, source_target_pairs={{3,0},{2,1},{1,2},{0,3},{17,16},{16,17},{19,18},{18,19},{7,4},{6,5... | collective-permute-start | bytes 2752520 | tf_op jit(solution)/shard_map/ppermute | solution.py:40
  5.9 1.9 collective-permute-start.1
  7.8 6.9 %shard_map.91 = bf16[4,256,1792]{2,1,0:T(8,128)(2,1)} custom-call(s32[1]{0:T(128)} %bitcast.mine_ref, bf16[256,512]{1,0:T(8,128)(2,1)} %a_ref, bf16[512,7168]{1,0:T(8,128)(2,1)} %b_ref.1, bf16[16,7168]{1,0:T(8,128)(2,1)} %r_ref.1), custom_call_target="tpu_custom_call" | custom-call | flops 1879048192 | bytes 11272192 | tf_op jit(solution)/shard_map/pallas_call | solution.py:57
  14.7 1.7 collective-permute-done.2
  17.3 7.8 %all-to-all-start = ((bf16[16,64,1792]{2,1,0:T(8,128)(2,1)}), bf16[16,64,1792]{2,1,0:T(8,128)(2,1)}, u32[]{:S(2)}, u32[]{:S(2)}) async-start(bf16[16,64,1792]{2,1,0:T(8,128)(2,1)} %bitcast.44), calls=%async_computation | async-start | bytes 7340032 | tf_op jit(solution)/shard_map/all_to_all | solution.py:23
  26.2 4.1 %shard_map.92 = bf16[3584,512]{1,0:T(8,128)(2,1)} custom-call(s32[2]{0:T(128)} %get-tuple-element.73.at_ref, bf16[1,7168,256]{2,1,0:T(8,128)(2,1)} %g_ref.3, bf16[1,7168,256]{2,1,0:T(8,128)(2,1)} %u_ref.3), custom_call_target="tpu_custom_call" | custom-call | bytes 7340032 | tf_op jit(solution)/shard_map/pallas_call | solution.py:210
  30.6 1.2 dynamic-slice_bitcast_fusion.refs_4_
  31.8 7.9 %shard_map.93 = bf16[10752,256]{1,0:T(8,128)(2,1)} custom-call(s32[2]{0:T(128)} %get-tuple-element.74.at_ref, bf16[1,7168,256]{2,1,0:T(8,128)(2,1)} %g_ref.3, bf16[1,7168,256]{2,1,0:T(8,128)(2,1)} %u_ref.3, bf16[1,256,7168]{2,1,0:T(8,128)(2,1)} %d_ref), custom_call_target="tpu_custom_call" | custom-call | bytes 11010048 | tf_op jit(solution)/shard_map/pallas_call | solution.py:180
  41.3 30.4 %all-to-all-done = bf16[16,64,1792]{2,1,0:T(8,128)(2,1)} async-done(((bf16[16,64,1792]{2,1,0:T(8,128)(2,1)}), bf16[16,64,1792]{2,1,0:T(8,128)(2,1)}, u32[]{:S(2)}, u32[]{:S(2)}) %all-to-all-start) | async-done | bytes 3670048 | tf_op jit(solution)/shard_map/all_to_all | solution.py:23
  71.7 2.6 %reduce_sum.22 = bf16[64,1792]{1,0:T(8,128)(2,1)S(1)} reduce(bf16[16,64,1792]{2,1,0:T(8,128)(2,1)} %all-to-all-done, bf16[]{:T(256)} %constant.62.clone.1), dimensions={0}, to_apply=%region_3.4 | reduce | flops 1720320 | bytes 3899394 | tf_op jit(solution)/shard_map/reduce_sum | solution.py:297
  74.8 2.8 %collective-permute-start.5 = (bf16[64,1792]{1,0:T(8,128)(2,1)S(1)}, bf16[64,1792]{1,0:T(8,128)(2,1)S(1)}, u32[]{:S(2)}, u32[]{:S(2)}) collective-permute-start(bf16[64,1792]{1,0:T(8,128)(2,1)S(1)} %reduce_sum.22), channel_id=1, source_target_pairs={{3,0},{2,1},{1,2},{0,3},{17,16},{16,17},{19,18},{18,19},{7,4},{6,5... | collective-permute-start | bytes 688136 | tf_op jit(solution)/shard_map/ppermute | solution.py:40
  77.7 4.7 %collective-permute-done.7 = bf16[64,1792]{1,0:T(8,128)(2,1)S(1)} collective-permute-done((bf16[64,1792]{1,0:T(8,128)(2,1)S(1)}, bf16[64,1792]{1,0:T(8,128)(2,1)S(1)}, u32[]{:S(2)}, u32[]{:S(2)}) %collective-permute-start.7) | collective-permute-done | bytes 229408 | tf_op jit(solution)/shard_map/ppermute | solution.py:40
  82.3 1.1 collective-permute-done.5
  83.5 1.3 convolution_convert_fusion
  84.8 60.5 %all_to_all.20 = bf16[16,40,3584]{2,1,0:T(8,128)(2,1)S(1)} all-to-all(bf16[16,40,3584]{2,1,0:T(8,128)(2,1)S(1)} %bitcast.43), channel_id=1, replica_groups=mesh['y'=4,'c'=2,'z'=4,'x'=4] {'y','z'}, dimensions={0} | all-to-all | bytes 9175040 | tf_op jit(solution)/shard_map/all_to_all | solution.py:23
  146.3 1.5 collective-permute-start.10
  147.8 3.0 %shard_map.94 = (bf16[640,3584]{1,0:T(8,128)(2,1)S(1)}, f32[640,1]{1,0:T(8,128)S(1)}, bf16[640,512]{1,0:T(8,128)(2,1)S(1)}) custom-call(bf16[640,3584]{1,0:T(8,128)(2,1)S(1)} %bitcast.41, f32[1,3584]{1,0:T(1,128)S(1)} %broadcast_in_dim.50.gain_ref, bf16[10752,256]{1,0:T(8,128)(2,1)S(1)} %collective-permute-done.8.w_ref.refs_5_), custom_call_target="tpu_custom_call" | custom-call | flops 2348810240 | bytes 13500416 | tf_op jit(solution)/shard_map/pallas_call | solution.py:104
  150.8 2.0 collective-permute-start.9
  152.9 2.5 %fusion.24 = f32[640,512]{1,0:T(8,128)S(1)} fusion(bf16[640,3584]{1,0:T(8,128)(2,1)S(1)} %get-tuple-element.57, bf16[3584,512]{1,0:T(8,128)(2,1)S(1)} %copy-done), kind=kOutput, calls=%fused_computation.48 | convolution fusion | flops 2348810240 | bytes 9568256 | tf_op jit(solution)/shard_map/dot_general | solution.py:328
  155.4 2.5 %collective-permute-done.11 = f32[640,1]{1,0:T(8,128)S(1)} collective-permute-done((f32[640,1]{1,0:T(8,128)S(1)}, f32[640,1]{1,0:T(8,128)S(1)}, u32[]{:S(2)}, u32[]{:S(2)}) %collective-permute-start.11) | collective-permute-done | bytes 2592 | tf_op jit(solution)/shard_map/ppermute | solution.py:40
  158.1 1.4 collective-permute-done.10.refs_7_
  159.5 5.4 %collective-permute-done.9 = bf16[640,512]{1,0:T(8,128)(2,1)S(1)} collective-permute-done((bf16[640,512]{1,0:T(8,128)(2,1)S(1)}, bf16[640,512]{1,0:T(8,128)(2,1)S(1)}, u32[]{:S(2)}, u32[]{:S(2)}) %collective-permute-start.9) | collective-permute-done | bytes 655392 | tf_op jit(solution)/shard_map/ppermute | solution.py:40
  164.9 1.8 collective-permute-start.15
  167.5 1.8 collective-permute-start.13
  169.3 1.4 collective-permute-start.12
  170.7 8.8 %collective-permute-done.14.refs_3_ = bf16[640,256]{1,0:T(8,128)(2,1)S(1)} collective-permute-done((bf16[640,256]{1,0:T(8,128)(2,1)S(1)}, bf16[640,256]{1,0:T(8,128)(2,1)S(1)}, u32[]{:S(2)}, u32[]{:S(2)}) %collective-permute-start.14) | collective-permute-done | bytes 327712 | tf_op jit(solution)/shard_map/ppermute | solution.py:19
  179.4 9.9 %collective-permute-done.13.refs_2_ = bf16[640,256]{1,0:T(8,128)(2,1)S(1)} collective-permute-done((bf16[640,256]{1,0:T(8,128)(2,1)S(1)}, bf16[640,256]{1,0:T(8,128)(2,1)S(1)}, u32[]{:S(2)}, u32[]{:S(2)}) %collective-permute-start.13) | collective-permute-done | bytes 327712 | tf_op jit(solution)/shard_map/ppermute | solution.py:40
  189.4 2.5 %shard_map.95 = bf16[640,1792]{1,0:T(8,128)(2,1)S(1)} custom-call(bf16[640,256]{1,0:T(8,128)(2,1)S(1)} %fusion.7.refs_0_, bf16[640,256]{1,0:T(8,128)(2,1)S(1)} %collective-permute-done.12.refs_1_, bf16[640,256]{1,0:T(8,128)(2,1)S(1)} %collective-permute-done.13.refs_2_, bf16[640,256]{1,0:T(8,128)(2,1)S(1)} %collective-permute-done.14.refs_3_, ...), custom_call_target="tpu_custom_call" | custom-call | flops 2348810240 | bytes 7274496 | tf_op jit(solution)/shard_map/pallas_call | solution.py:140
  191.9 34.0 %all_to_all.21 = bf16[16,40,1792]{2,1,0:T(8,128)(2,1)S(1)} all-to-all(bf16[16,40,1792]{2,1,0:T(8,128)(2,1)S(1)} %bitcast.42), channel_id=1, replica_groups=mesh['y'=4,'c'=2,'z'=4,'x'=4] {'y','z'}, dimensions={0} | all-to-all | bytes 4587520 | tf_op jit(solution)/shard_map/all_to_all | solution.py:23
  226.6 1.8 collective-permute-done.16
  228.5 9.3 %all_to_all.22 = bf16[4,16,1792]{2,1,0:T(8,128)(2,1)S(1)} all-to-all(bf16[4,16,1792]{2,1,0:T(8,128)(2,1)S(1)} %bitcast.47), channel_id=1, replica_groups=mesh['y'=4,'c'=2,'z'=4,'x'=4] {'x'}, dimensions={0} | all-to-all | bytes 458752 | tf_op jit(solution)/shard_map/all_to_all | solution.py:23
  (56 shorter events, 9.5 us)
Async XLA Ops:
  1.2 16.1 %collective-permute-start.3 = (bf16[256,1792]{1,0:T(8,128)(2,1)S(1)}, bf16[256,1792]{1,0:T(8,128)(2,1)S(1)}, u32[]{:S(2)}, u32[]{:S(2)}) collective-permute-start(bf16[256,1792]{1,0:T(8,128)(2,1)S(1)} %dynamic-slice_bitcast_fusion.1), channel_id=1, source_target_pairs={{3,0},{2,1},{1,2},{0,3},{17,16},{16,17},{19,18},{18,19},{7,4},{6,5... | collective-permute-start | bytes 2752520 | tf_op jit(solution)/shard_map/ppermute | solution.py:40
  5.5 10.9 %collective-permute-start.2 = (bf16[16,128]{0,1:T(8,128)(2,1)S(1)}, bf16[16,128]{0,1:T(8,128)(2,1)S(1)}, u32[]{:S(2)}, u32[]{:S(2)}) collective-permute-start(bf16[16,128]{0,1:T(8,128)(2,1)S(1)} %fusion.15), channel_id=1, source_target_pairs={{0,3},{1,0},{2,1},{3,2},{4,7},{5,4},{6,5},{7,6},{8,11},{9,8},{10,9... | collective-permute-start | bytes 12296 | tf_op jit(solution)/shard_map/ppermute | solution.py:19
  5.9 10.5 %collective-permute-start.1 = (bf16[16,128]{0,1:T(8,128)(2,1)S(1)}, bf16[16,128]{0,1:T(8,128)(2,1)S(1)}, u32[]{:S(2)}, u32[]{:S(2)}) collective-permute-start(bf16[16,128]{0,1:T(8,128)(2,1)S(1)} %fusion.15), channel_id=1, source_target_pairs={{0,2},{1,3},{2,0},{3,1},{4,6},{5,7},{6,4},{7,5},{8,10},{9,11},{10,... | collective-permute-start | bytes 12296 | tf_op jit(solution)/shard_map/ppermute | solution.py:19
  7.8 9.5 %collective-permute-start = (bf16[16,128]{0,1:T(8,128)(2,1)S(1)}, bf16[16,128]{0,1:T(8,128)(2,1)S(1)}, u32[]{:S(2)}, u32[]{:S(2)}) collective-permute-start(bf16[16,128]{0,1:T(8,128)(2,1)S(1)} %fusion.15), channel_id=1, source_target_pairs={{0,1},{1,2},{2,3},{3,0},{4,5},{5,6},{6,7},{7,4},{8,9},{9,10},{10,1... | collective-permute-start | bytes 12296 | tf_op jit(solution)/shard_map/ppermute | solution.py:19
  17.3 8.1 %copy-start.1 = (f32[7168]{0:T(1024)S(1)}, f32[7168]{0:T(1024)}, u32[]{:S(2)}) copy-start(f32[7168]{0:T(1024)} %param.12) | copy-start | bytes 86020
  17.3 54.4 %all-to-all-start = ((bf16[16,64,1792]{2,1,0:T(8,128)(2,1)}), bf16[16,64,1792]{2,1,0:T(8,128)(2,1)}, u32[]{:S(2)}, u32[]{:S(2)}) async-start(bf16[16,64,1792]{2,1,0:T(8,128)(2,1)} %bitcast.44), calls=%async_computation | async-start | bytes 7340032 | tf_op jit(solution)/shard_map/all_to_all | solution.py:23
  30.5 9.2 %collective-permute-start.4 = (bf16[64,128]{0,1:T(8,128)(2,1)S(1)}, bf16[64,128]{0,1:T(8,128)(2,1)S(1)}, u32[]{:S(2)}, u32[]{:S(2)}) collective-permute-start(bf16[64,128]{0,1:T(8,128)(2,1)S(1)} %constant_dynamic-slice_fusion), channel_id=1, source_target_pairs={{0,16},{16,0},{1,17},{17,1},{2,18},{18,2},{3,19},{19,3},{4,20},{20... | collective-permute-start | bytes 49160 | tf_op jit(solution)/shard_map/ppermute | solution.py:19
  74.3 8.1 %collective-permute-start.7 = (bf16[64,1792]{1,0:T(8,128)(2,1)S(1)}, bf16[64,1792]{1,0:T(8,128)(2,1)S(1)}, u32[]{:S(2)}, u32[]{:S(2)}) collective-permute-start(bf16[64,1792]{1,0:T(8,128)(2,1)S(1)} %reduce_sum.22), channel_id=1, source_target_pairs={{19,0},{18,1},{17,2},{16,3},{1,16},{0,17},{3,18},{2,19},{23,4},{22... | collective-permute-start | bytes 688136 | tf_op jit(solution)/shard_map/ppermute | solution.py:40
  74.3 8.0 %collective-permute-start.6 = (bf16[64,1792]{1,0:T(8,128)(2,1)S(1)}, bf16[64,1792]{1,0:T(8,128)(2,1)S(1)}, u32[]{:S(2)}, u32[]{:S(2)}) collective-permute-start(bf16[64,1792]{1,0:T(8,128)(2,1)S(1)} %reduce_sum.22), channel_id=1, source_target_pairs={{16,0},{17,1},{18,2},{19,3},{0,16},{1,17},{2,18},{3,19},{20,4},{21... | collective-permute-start | bytes 688136 | tf_op jit(solution)/shard_map/ppermute | solution.py:40
  74.8 8.6 %collective-permute-start.5 = (bf16[64,1792]{1,0:T(8,128)(2,1)S(1)}, bf16[64,1792]{1,0:T(8,128)(2,1)S(1)}, u32[]{:S(2)}, u32[]{:S(2)}) collective-permute-start(bf16[64,1792]{1,0:T(8,128)(2,1)S(1)} %reduce_sum.22), channel_id=1, source_target_pairs={{3,0},{2,1},{1,2},{0,3},{17,16},{16,17},{19,18},{18,19},{7,4},{6,5... | collective-permute-start | bytes 688136 | tf_op jit(solution)/shard_map/ppermute | solution.py:40
  83.4 62.8 %collective-permute-start.8 = (bf16[10752,256]{1,0:T(8,128)(2,1)}, bf16[10752,256]{1,0:T(8,128)(2,1)S(1)}, u32[]{:S(2)}, u32[]{:S(2)}) collective-permute-start(bf16[10752,256]{1,0:T(8,128)(2,1)} %shard_map.93), channel_id=1, source_target_pairs={{1,0},{0,1},{3,2},{2,3},{19,16},{18,17},{17,18},{16,19},{5,4},{4,5... | collective-permute-start | bytes 16515080 | tf_op jit(solution)/shard_map/ppermute | solution.py:40
  146.3 6.6 %copy-start = (bf16[3584,512]{1,0:T(8,128)(2,1)S(1)}, bf16[3584,512]{1,0:T(8,128)(2,1)}, u32[]{:S(2)}) copy-start(bf16[3584,512]{1,0:T(8,128)(2,1)} %shard_map.92) | copy-start | bytes 11010052
  146.3 13.2 %collective-permute-start.10 = (bf16[768,256]{1,0:T(8,128)(2,1)S(1)}, bf16[768,256]{1,0:T(8,128)(2,1)S(1)}, u32[]{:S(2)}, u32[]{:S(2)}) collective-permute-start(bf16[768,256]{1,0:T(8,128)(2,1)S(1)} %slice.26), channel_id=1, source_target_pairs={{3,0},{2,1},{1,2},{0,3},{17,16},{16,17},{19,18},{18,19},{7,4},{6,5... | collective-permute-start | bytes 1179656 | tf_op jit(solution)/shard_map/ppermute | solution.py:40
  150.8 7.1 %collective-permute-start.11 = (f32[640,1]{1,0:T(8,128)S(1)}, f32[640,1]{1,0:T(8,128)S(1)}, u32[]{:S(2)}, u32[]{:S(2)}) collective-permute-start(f32[640,1]{1,0:T(8,128)S(1)} %get-tuple-element.64), channel_id=1, source_target_pairs={{1,0},{0,1},{3,2},{2,3},{19,16},{18,17},{17,18},{16,19},{5,4},{4,5... | collective-permute-start | bytes 7688 | tf_op jit(solution)/shard_map/ppermute | solution.py:40
  150.8 14.1 %collective-permute-start.9 = (bf16[640,512]{1,0:T(8,128)(2,1)S(1)}, bf16[640,512]{1,0:T(8,128)(2,1)S(1)}, u32[]{:S(2)}, u32[]{:S(2)}) collective-permute-start(bf16[640,512]{1,0:T(8,128)(2,1)S(1)} %get-tuple-element.59), channel_id=1, source_target_pairs={{1,0},{0,1},{3,2},{2,3},{19,16},{18,17},{17,18},{16,19},{5,4},{4,5... | collective-permute-start | bytes 1966088 | tf_op jit(solution)/shard_map/ppermute | solution.py:40
  164.9 24.4 %collective-permute-start.15 = (bf16[1024,256]{1,0:T(8,128)(2,1)S(1)}, bf16[1024,256]{1,0:T(8,128)(2,1)S(1)}, u32[]{:S(2)}, u32[]{:S(2)}) collective-permute-start(bf16[1024,256]{1,0:T(8,128)(2,1)S(1)} %slice.27), channel_id=1, source_target_pairs={{3,0},{2,1},{1,2},{0,3},{17,16},{16,17},{19,18},{18,19},{7,4},{6,5... | collective-permute-start | bytes 1572872 | tf_op jit(solution)/shard_map/ppermute | solution.py:40
  167.1 12.3 %collective-permute-start.14 = (bf16[640,256]{1,0:T(8,128)(2,1)S(1)}, bf16[640,256]{1,0:T(8,128)(2,1)S(1)}, u32[]{:S(2)}, u32[]{:S(2)}) collective-permute-start(bf16[640,256]{1,0:T(8,128)(2,1)S(1)} %fusion.7.refs_0_), channel_id=1, source_target_pairs={{0,2},{1,3},{2,0},{3,1},{4,6},{5,7},{6,4},{7,5},{8,10},{9,11},{10,... | collective-permute-start | bytes 983048 | tf_op jit(solution)/shard_map/ppermute | solution.py:19
  167.5 21.9 %collective-permute-start.13 = (bf16[640,256]{1,0:T(8,128)(2,1)S(1)}, bf16[640,256]{1,0:T(8,128)(2,1)S(1)}, u32[]{:S(2)}, u32[]{:S(2)}) collective-permute-start(bf16[640,256]{1,0:T(8,128)(2,1)S(1)} %fusion.7.refs_0_), channel_id=1, source_target_pairs={{3,0},{2,1},{1,2},{0,3},{17,16},{16,17},{19,18},{18,19},{7,4},{6,5... | collective-permute-start | bytes 983048 | tf_op jit(solution)/shard_map/ppermute | solution.py:40
  169.3 20.1 %collective-permute-start.12 = (bf16[640,256]{1,0:T(8,128)(2,1)S(1)}, bf16[640,256]{1,0:T(8,128)(2,1)S(1)}, u32[]{:S(2)}, u32[]{:S(2)}) collective-permute-start(bf16[640,256]{1,0:T(8,128)(2,1)S(1)} %fusion.7.refs_0_), channel_id=1, source_target_pairs={{1,0},{0,1},{3,2},{2,3},{19,16},{18,17},{17,18},{16,19},{5,4},{4,5... | collective-permute-start | bytes 983048 | tf_op jit(solution)/shard_map/ppermute | solution.py:40
  226.5 1.9 collective-permute-start.16

commit v6 on v4

--- a/solution.py
+++ b/solution.py
@@ -44,27 +44,25 @@
     acc_ref[...] = jnp.dot(a_ref[...], b_ref[...], preferred_element_type=F32)
     here = pl.ds(pl.multiple_of(mine_ref[0] * own, own), own)
     acc_ref[here, :] += r_ref[...].astype(F32)
-    o_ref[0] = acc_ref[...].astype(BF16)
+    o_ref[...] = acc_ref[...].astype(BF16)
 
 
 def project(mine, context, weight, residual, blocks):
     rows, depth = context.shape
     own, width = residual.shape
-    cut = width // blocks
-    halves = 1
-    step = cut // halves
+    step = width // blocks
     return pl.pallas_call(
         project_body,
-        out_shape=jax.ShapeDtypeStruct((blocks, rows, cut), BF16),
+        out_shape=jax.ShapeDtypeStruct((rows, width), BF16),
         grid_spec=pltpu.PrefetchScalarGridSpec(
             num_scalar_prefetch=1,
-            grid=(blocks, halves),
+            grid=(blocks,),
             in_specs=[
-                pl.BlockSpec((rows, depth), lambda q, j, m: (0, 0)),
-                pl.BlockSpec((depth, step), lambda q, j, m: (0, q * halves + j)),
-                pl.BlockSpec((own, step), lambda q, j, m: (0, q * halves + j)),
+                pl.BlockSpec((rows, depth), lambda q, m: (0, 0)),
+                pl.BlockSpec((depth, step), lambda q, m: (0, q)),
+                pl.BlockSpec((own, step), lambda q, m: (0, q)),
             ],
-            out_specs=pl.BlockSpec((1, rows, step), lambda q, j, m: (q, 0, j)),
+            out_specs=pl.BlockSpec((rows, step), lambda q, m: (0, q)),
             scratch_shapes=[pltpu.VMEM((rows, step), F32)],
         ),
         compiler_params=pltpu.CompilerParams(vmem_limit_bytes=56 << 20),
@@ -74,6 +72,31 @@
             transcendentals=0,
         ),
     )(mine, context, weight, residual)
+
+
+def gather_sum_body(a_ref, o_ref):
+    total = a_ref[0].astype(F32)
+    for i in range(1, a_ref.shape[0]):
+        total += a_ref[i].astype(F32)
+    o_ref[0] = total.astype(BF16)
+
+
+def gather_sum(terms, blocks):
+    count, rows, width = terms.shape
+    step = width // blocks
+    return pl.pallas_call(
+        gather_sum_body,
+        out_shape=jax.ShapeDtypeStruct((blocks, rows, step), BF16),
+        grid=(blocks,),
+        in_specs=[pl.BlockSpec((count, rows, step), lambda q: (0, 0, q))],
+        out_specs=pl.BlockSpec((1, rows, step), lambda q: (q, 0, 0)),
+        compiler_params=pltpu.CompilerParams(vmem_limit_bytes=24 << 20),
+        cost_estimate=pl.CostEstimate(
+            flops=count * rows * width,
+            bytes_accessed=2 * (count + 1) * rows * width,
+            transcendentals=0,
+        ),
+    )(terms)
 
 
 def first_body(a_ref, gain_ref, w_ref, g_ref, s_ref, o_ref):
@@ -127,7 +150,7 @@
         total = jnp.dot(own[...], w_own[:, cols], preferred_element_type=F32)
         total += jnp.dot(from_mate[...], w_mate[at, :], preferred_element_type=F32)
         total += jnp.dot(from_twin[...], w_twin[:, cols], preferred_element_type=F32)
-        total += jnp.dot(from_far[...], w_far[cols, :], preferred_element_type=F32)
+        total += jnp.dot(from_far[...], w_far[:, cols], preferred_element_type=F32)
         o_ref[:, cols] = total.astype(BF16)
 
 
@@ -170,26 +193,24 @@
     deep, h = gate.shape[1:]
     cut = deep // 4
 
-    def pick(last_first):
-        return lambda i, at: at[jnp.where(i <= last_first, 0, 1)]
-
-    gate_at, up_at, down_at = pick(0), pick(2), pick(4)
+    gate_at = lambda i, at: at[jnp.where(i <= 0, 0, 1)]
+    up_at = lambda i, at: at[jnp.where(i <= 2, 0, 1)]
     return pl.pallas_call(
         bundle_body,
-        out_shape=jax.ShapeDtypeStruct((6 * cut, h), BF16),
+        out_shape=jax.ShapeDtypeStruct((5 * cut, h), BF16),
         grid_spec=pltpu.PrefetchScalarGridSpec(
             num_scalar_prefetch=1,
-            grid=(6,),
+            grid=(5,),
             in_specs=[
                 pl.BlockSpec((1, cut, h), lambda i, at: (0, gate_at(i, at), 0)),
                 pl.BlockSpec((1, cut, h), lambda i, at: (0, up_at(i, at), 0)),
-                pl.BlockSpec((1, h, cut), lambda i, at: (0, 0, down_at(i, at))),
+                pl.BlockSpec((1, h, cut), lambda i, at: (0, 0, at[0])),
             ],
             out_specs=pl.BlockSpec((cut, h), lambda i, at: (i, 0)),
         ),
         compiler_params=pltpu.CompilerParams(vmem_limit_bytes=56 << 20),
         cost_estimate=pl.CostEstimate(
-            flops=0, bytes_accessed=24 * cut * h, transcendentals=0
+            flops=0, bytes_accessed=20 * cut * h, transcendentals=0
         ),
     )(at, gate, up, down)
 
@@ -244,17 +265,13 @@
             down_proj[0], (0, at * quarter), (down_proj.shape[1], quarter)
         )
 
-    twin_cut, context = lax.optimization_barrier((cut_down(twin), context))
-    twin_down = to_twin(twin_cut)
-
     mine = lax.axis_index("z") * nx + x
     part = project(mine[None].astype(jnp.int32), context, out_proj, residual, nx)
 
     meta = jnp.concatenate([expert_ids.astype(BF16), gates], axis=1)
     meta = jnp.pad(meta, ((0, 0), (0, 128 - meta.shape[1])))
     came = [meta] + [shift(meta, "x", k) for k in range(1, nx)]
-    part, came, twin_down, down_proj = lax.optimization_barrier((part, came, twin_down, down_proj))
-    part = exchange(part.reshape(nx * nz, tokens_core, quarter), ("x", "z"))
+    part = exchange(part.reshape(nz, tokens_core, width), "z")
     ring = [came[(nx - m) % nx] for m in range(nx)]
     ring = jnp.concatenate(ring + ring[:-1], axis=0)
     meta_own = lax.dynamic_slice(
@@ -283,13 +300,18 @@
     scaled = scaled.reshape(places * slots, tokens)
     kept = pack(jnp.stack([x, twin]).astype(jnp.int32), gate_proj, up_proj)
     given = bundle(jnp.stack([mate, x ^ 2]).astype(jnp.int32), gate_proj, up_proj, down_proj)
-    own_down = cut_down(x)
+    own_down, twin_cut, far_cut = cut_down(x), cut_down(twin), cut_down(x ^ 2)
+    twin_down = to_twin(twin_cut)
+    far_down = to_twin(to_mate(far_cut))
     gain = jnp.concatenate(
         [lax.dynamic_slice(norm_gain, (q * quarter,), (quarter,)) for q in (x, twin)]
     )[None, :]
-    selector, scaled, part, kept, given, own_down, gain = lax.optimization_barrier(
-        (selector, scaled, part, kept, given, own_down, gain)
-    )
+    selector, scaled, part, kept, given, own_down, gain, twin_down, far_down = (
+        lax.optimization_barrier(
+            (selector, scaled, part, kept, given, own_down, gain, twin_down, far_down)
+        )
+    )
+    part = exchange(gather_sum(part, nx), "x")
 
     hidden = jnp.sum(part.astype(F32), axis=0).astype(BF16)
     hidden_wide = hidden.astype(F32)
@@ -314,9 +336,6 @@
     taken = to_mate(given)
     arrived, taken = lax.optimization_barrier((arrived, taken))
     gained, square, theirs = first_product(arrived, gain, taken)
-    theirs, taken = lax.optimization_barrier((theirs, taken))
-    deep = taken.shape[0] // 6
-    far_down = to_twin(taken[5 * deep :])
     came_back = to_mate(theirs)
     inverse = lax.rsqrt((square + to_mate(square)) / width + 1e-06)
     total = jnp.dot(gained, kept, preferred_element_type=F32)
@@ -325,9 +344,8 @@
     total = total * inverse
     hid = total.shape[1] // 2
     activated = (jax.nn.silu(total[:, :hid]) * total[:, hid:]).astype(BF16)
-    activated, far_down = lax.optimization_barrier((activated, far_down))
     blocks = (activated, to_mate(activated), to_twin(activated), shift(activated, "x", 2))
-    result = down_product(blocks, (own_down, taken, twin_down, far_down), 4 * deep)
+    result = down_product(blocks, (own_down, taken, twin_down, far_down), 4 * quarter)
 
     returned = exchange(result.reshape(places, slots, quarter), ("y", "z"))
     returned = returned.reshape(places * slots, quarter)

time: 242 us -> 233 us (0.963)
  waiting for transfers between devices: 72.3 us -> 49.4 us
  blocking collectives: 106 us -> 122 us
  other arithmetic: 6.5 us -> 3.88 us
    all_to_all x1, waiting for transfers between devices: 30.4 us -> 1.05 us  [exchange(): return lax.all_to_all(value, axes, split_axis=0, concat_axis=0, tiled=True)]
    all_to_all x3 -> x4, blocking collectives: 106 us -> 122 us  [exchange(): return lax.all_to_all(value, axes, split_axis=0, concat_axis=0, tiled=True)]
    ppermute x6, waiting for transfers between devices: 13.1 us -> 27.1 us  [shift(): lax.ppermute(value, axis, [(i, (i + amount) % size) for i in range(size)])]
    ppermute x10 -> x11, waiting for transfers between devices: 28.8 us -> 21.2 us  [from_places(): return lax.ppermute(value, ('c', 'x'), pairs)]
    ppermute x6, starting transfers between devices: 3.48 us -> 7.76 us  [shift(): lax.ppermute(value, axis, [(i, (i + amount) % size) for i in range(size)])]
    ppermute x10 -> x11, starting transfers between devices: 12.6 us -> 8.43 us  [from_places(): return lax.ppermute(value, ('c', 'x'), pairs)]
    pallas_call x2 -> x3, Pallas kernels: 14.8 us -> 16.1 us  [the longest x1 6.9 us: project(): pl.pallas_call(project_body, out_shape=jax.ShapeDtypeStruct((rows, width)...]
  transfers between devices with their start and end apart: 17 -> 18, of which waited for: 11 -> 12; matrix products, arithmetic and copies ran while one was open for 4% -> 4% of each run, Pallas kernels for 8% -> 4%
where the time goes in v6:
time: 233 us; the launch traced here: 232 us
  blocking collectives  122 us (52%)
  waiting for transfers between devices  49.4 us (21%)
  Pallas kernels  25.7 us (11%)
  starting transfers between devices  21.6 us (9%)
  local copies, waits for them, and re-layouts  4.54 us (2%)
  matrix products  4.42 us (2%)
  other arithmetic  3.88 us (2%)
    all_to_all x4, blocking collectives, exchange(): return lax.all_to_all(value, axes, split_axis=0, concat_axis=0, tiled=True)  122 us
    ppermute x6, waiting for transfers between devices, shift(): lax.ppermute(value, axis, [(i, (i + amount) % size) for i in range(size)])  27.1 us
    ppermute x11, waiting for transfers between devices, from_places(): return lax.ppermute(value, ('c', 'x'), pairs)  21.2 us
    ppermute x11, starting transfers between devices, from_places(): return lax.ppermute(value, ('c', 'x'), pairs)  8.43 us
    ppermute x6, starting transfers between devices, shift(): lax.ppermute(value, axis, [(i, (i + amount) % size) for i in range(size)])  7.76 us
    pallas_call x1, Pallas kernels, project(): pl.pallas_call(project_body, out_shape=jax.ShapeDtypeStruct((rows, width)...  6.9 us
    pallas_call x1, Pallas kernels, bundle(): pl.pallas_call(bundle_body, out_shape=jax.ShapeDtypeStruct((5 * cut, h),...  6.24 us
    all_to_all x1, starting transfers between devices, exchange(): return lax.all_to_all(value, axes, split_axis=0, concat_axis=0, tiled=True)  5.39 us
  transfers between devices with their start and end apart: 18, of which 12 were waited for; matrix products, arithmetic and copies ran while one was open for 4% of the time, Pallas kernels for 4%

profile of v6, /device:TPU:0, one launch (start us, length us, event | category | flops | bytes accessed | tf_op | source)
XLA Modules:
  0.0 232.0 jit_solution(2452852544582653572)
XLA Ops:
  0.0 6.9 %shard_map.91 = bf16[256,7168]{1,0:T(8,128)(2,1)} custom-call(s32[1]{0:T(128)} %bitcast.4.mine_ref, bf16[256,512]{1,0:T(8,128)(2,1)} %a_ref.1, bf16[512,7168]{1,0:T(8,128)(2,1)} %b_ref.1, bf16[16,7168]{1,0:T(8,128)(2,1)} %r_ref.1), custom_call_target="tpu_custom_call" | custom-call | flops 1879048192 | bytes 11272192 | tf_op jit(solution)/shard_map/pallas_call | solution.py:54
  6.9 5.4 %all-to-all-start = ((bf16[4,64,7168]{2,1,0:T(8,128)(2,1)}), bf16[4,64,7168]{2,1,0:T(8,128)(2,1)}, u32[]{:S(2)}, u32[]{:S(2)}) async-start(bf16[4,64,7168]{2,1,0:T(8,128)(2,1)} %bitcast.46), calls=%async_computation | async-start | bytes 7340032 | tf_op jit(solution)/shard_map/all_to_all | solution.py:22
  12.3 2.9 %dynamic-slice_bitcast_fusion = (bf16[256,1792]{1,0:T(8,128)(2,1)S(1)}, bf16[256,1792]{1,0:T(8,128)(2,1)S(1)}, bf16[256,1792]{1,0:T(8,128)(2,1)}) fusion(bf16[1,256,7168]{2,1,0:T(8,128)(2,1)} %d_ref.1, s32[]{:T(128)S(6)} %select_n.53, s32[]{:T(128)S(6)} %select_n.51, s32[]{:T(128)S(6)} %select_n.52), kind=kLoop, calls=%fused_computation.9 | loop fusion | bytes 5505036 | tf_op jit(solution)/shard_map/dynamic_slice | solution.py:264
  15.2 1.5 collective-permute-start.5
  17.3 3.0 %collective-permute-start.1 = (bf16[16,128]{0,1:T(8,128)(2,1)S(1)}, bf16[16,128]{0,1:T(8,128)(2,1)S(1)}, u32[]{:S(2)}, u32[]{:S(2)}) collective-permute-start(bf16[16,128]{0,1:T(8,128)(2,1)S(1)} %fusion.15), channel_id=1, source_target_pairs={{0,2},{1,3},{2,0},{3,1},{4,6},{5,7},{6,4},{7,5},{8,10},{9,11},{10,... | collective-permute-start | bytes 12296 | tf_op jit(solution)/shard_map/ppermute | solution.py:18
  20.4 1.8 collective-permute-start
  23.0 13.0 %collective-permute-done.2 = bf16[16,128]{0,1:T(8,128)(2,1)S(1)} collective-permute-done((bf16[16,128]{0,1:T(8,128)(2,1)S(1)}, bf16[16,128]{0,1:T(8,128)(2,1)S(1)}, u32[]{:S(2)}, u32[]{:S(2)}) %collective-permute-start.2) | collective-permute-done | bytes 4128 | tf_op jit(solution)/shard_map/ppermute | solution.py:18
  36.0 3.9 %collective-permute-done.1 = bf16[16,128]{0,1:T(8,128)(2,1)S(1)} collective-permute-done((bf16[16,128]{0,1:T(8,128)(2,1)S(1)}, bf16[16,128]{0,1:T(8,128)(2,1)S(1)}, u32[]{:S(2)}, u32[]{:S(2)}) %collective-permute-start.1) | collective-permute-done | bytes 4128 | tf_op jit(solution)/shard_map/ppermute | solution.py:18
  40.6 4.1 %shard_map.92 = bf16[3584,512]{1,0:T(8,128)(2,1)} custom-call(s32[2]{0:T(128)} %get-tuple-element.52.at_ref, bf16[1,7168,256]{2,1,0:T(8,128)(2,1)} %g_ref.3, bf16[1,7168,256]{2,1,0:T(8,128)(2,1)} %u_ref.3), custom_call_target="tpu_custom_call" | custom-call | bytes 7340032 | tf_op jit(solution)/shard_map/pallas_call | solution.py:228
  44.7 6.2 %shard_map.93 = bf16[8960,256]{1,0:T(8,128)(2,1)} custom-call(s32[2]{0:T(128)} %get-tuple-element.53.at_ref, bf16[1,7168,256]{2,1,0:T(8,128)(2,1)} %g_ref.3, bf16[1,7168,256]{2,1,0:T(8,128)(2,1)} %u_ref.3, bf16[1,256,7168]{2,1,0:T(8,128)(2,1)} %d_ref.1), custom_call_target="tpu_custom_call" | custom-call | bytes 9175040 | tf_op jit(solution)/shard_map/pallas_call | solution.py:198
  52.6 2.4 %collective-permute-done.6.refs_7_ = bf16[256,1792]{1,0:T(8,128)(2,1)S(1)} collective-permute-done((bf16[256,1792]{1,0:T(8,128)(2,1)}, bf16[256,1792]{1,0:T(8,128)(2,1)S(1)}, u32[]{:S(2)}, u32[]{:S(2)}) %collective-permute-start.6) | collective-permute-done | bytes 917536 | tf_op jit(solution)/shard_map/ppermute | solution.py:39
  56.0 2.9 %shard_map.94 = bf16[4,64,1792]{2,1,0:T(8,128)(2,1)S(1)} custom-call(bf16[4,64,7168]{2,1,0:T(8,128)(2,1)} %all-to-all-done.a_ref), custom_call_target="tpu_custom_call" | custom-call | flops 1835008 | bytes 4587520 | tf_op jit(solution)/shard_map/pallas_call | solution.py:87
  59.0 17.0 %all_to_all.25 = bf16[4,64,1792]{2,1,0:T(8,128)(2,1)} all-to-all(bf16[4,64,1792]{2,1,0:T(8,128)(2,1)S(1)} %shard_map.94), channel_id=1, replica_groups=mesh['y'=4,'c'=2,'z'=4,'x'=4] {'x'}, dimensions={0} | all-to-all | bytes 1835008 | tf_op jit(solution)/shard_map/all_to_all | solution.py:22
  76.0 1.3 reduce_sum.22
  77.4 1.3 collective-permute-start.8
  78.6 2.1 collective-permute-start.7
  80.7 3.8 %collective-permute-done.9 = bf16[64,1792]{1,0:T(8,128)(2,1)S(1)} collective-permute-done((bf16[64,1792]{1,0:T(8,128)(2,1)S(1)}, bf16[64,1792]{1,0:T(8,128)(2,1)S(1)}, u32[]{:S(2)}, u32[]{:S(2)}) %collective-permute-start.9) | collective-permute-done | bytes 229408 | tf_op jit(solution)/shard_map/ppermute | solution.py:39
  84.5 1.9 collective-permute-done.7
  86.5 1.3 convolution_convert_fusion
  87.8 59.7 %all_to_all.26 = bf16[16,40,3584]{2,1,0:T(8,128)(2,1)S(1)} all-to-all(bf16[16,40,3584]{2,1,0:T(8,128)(2,1)S(1)} %bitcast.45), channel_id=1, replica_groups=mesh['y'=4,'c'=2,'z'=4,'x'=4] {'y','z'}, dimensions={0} | all-to-all | bytes 9175040 | tf_op jit(solution)/shard_map/all_to_all | solution.py:22
  147.5 3.0 %shard_map.95 = (bf16[640,3584]{1,0:T(8,128)(2,1)S(1)}, f32[640,1]{1,0:T(8,128)S(1)}, bf16[640,512]{1,0:T(8,128)(2,1)S(1)}) custom-call(bf16[640,3584]{1,0:T(8,128)(2,1)S(1)} %bitcast.43, f32[1,3584]{1,0:T(1,128)S(1)} %broadcast_in_dim.50.gain_ref, bf16[8960,256]{1,0:T(8,128)(2,1)S(1)} %collective-permute-done.10.w_ref.refs_5_), custom_call_target="tpu_custom_call" | custom-call | flops 2348810240 | bytes 13500416 | tf_op jit(solution)/shard_map/pallas_call | solution.py:126
  150.8 1.7 collective-permute-start.11
  152.5 2.5 %fusion.24 = f32[640,512]{1,0:T(8,128)S(1)} fusion(bf16[640,3584]{1,0:T(8,128)(2,1)S(1)} %get-tuple-element.36, bf16[3584,512]{1,0:T(8,128)(2,1)S(1)} %copy-done), kind=kOutput, calls=%fused_computation.49 | convolution fusion | flops 2348810240 | bytes 9568256 | tf_op jit(solution)/shard_map/dot_general | solution.py:341
  155.0 2.5 %collective-permute-done.12 = f32[640,1]{1,0:T(8,128)S(1)} collective-permute-done((f32[640,1]{1,0:T(8,128)S(1)}, f32[640,1]{1,0:T(8,128)S(1)}, u32[]{:S(2)}, u32[]{:S(2)}) %collective-permute-start.12) | collective-permute-done | bytes 2592 | tf_op jit(solution)/shard_map/ppermute | solution.py:39
  157.7 6.8 %collective-permute-done.11 = bf16[640,512]{1,0:T(8,128)(2,1)S(1)} collective-permute-done((bf16[640,512]{1,0:T(8,128)(2,1)S(1)}, bf16[640,512]{1,0:T(8,128)(2,1)S(1)}, u32[]{:S(2)}, u32[]{:S(2)}) %collective-permute-start.11) | collective-permute-done | bytes 655392 | tf_op jit(solution)/shard_map/ppermute | solution.py:39
  165.0 2.2 collective-permute-start.15
  168.5 8.4 %collective-permute-done.15.refs_3_ = bf16[640,256]{1,0:T(8,128)(2,1)S(1)} collective-permute-done((bf16[640,256]{1,0:T(8,128)(2,1)S(1)}, bf16[640,256]{1,0:T(8,128)(2,1)S(1)}, u32[]{:S(2)}, u32[]{:S(2)}) %collective-permute-start.15) | collective-permute-done | bytes 327712 | tf_op jit(solution)/shard_map/ppermute | solution.py:18
  176.9 3.5 %collective-permute-done.14.refs_2_ = bf16[640,256]{1,0:T(8,128)(2,1)S(1)} collective-permute-done((bf16[640,256]{1,0:T(8,128)(2,1)S(1)}, bf16[640,256]{1,0:T(8,128)(2,1)S(1)}, u32[]{:S(2)}, u32[]{:S(2)}) %collective-permute-start.14) | collective-permute-done | bytes 327712 | tf_op jit(solution)/shard_map/ppermute | solution.py:39
  180.6 2.5 %shard_map.96 = bf16[640,1792]{1,0:T(8,128)(2,1)S(1)} custom-call(bf16[640,256]{1,0:T(8,128)(2,1)S(1)} %fusion.7.refs_0_, bf16[640,256]{1,0:T(8,128)(2,1)S(1)} %collective-permute-done.13.refs_1_, bf16[640,256]{1,0:T(8,128)(2,1)S(1)} %collective-permute-done.14.refs_2_, bf16[640,256]{1,0:T(8,128)(2,1)S(1)} %collective-permute-done.15.refs_3_, ...), custom_call_target="tpu_custom_call" | custom-call | flops 2348810240 | bytes 7274496 | tf_op jit(solution)/shard_map/pallas_call | solution.py:160
  183.1 35.9 %all_to_all.27 = bf16[16,40,1792]{2,1,0:T(8,128)(2,1)S(1)} all-to-all(bf16[16,40,1792]{2,1,0:T(8,128)(2,1)S(1)} %bitcast.44), channel_id=1, replica_groups=mesh['y'=4,'c'=2,'z'=4,'x'=4] {'y','z'}, dimensions={0} | all-to-all | bytes 4587520 | tf_op jit(solution)/shard_map/all_to_all | solution.py:22
  219.7 1.8 collective-permute-done.16
  221.6 9.7 %all_to_all.28 = bf16[4,16,1792]{2,1,0:T(8,128)(2,1)S(1)} all-to-all(bf16[4,16,1792]{2,1,0:T(8,128)(2,1)S(1)} %bitcast.49), channel_id=1, replica_groups=mesh['y'=4,'c'=2,'z'=4,'x'=4] {'x'}, dimensions={0} | all-to-all | bytes 458752 | tf_op jit(solution)/shard_map/all_to_all | solution.py:22
  (59 shorter events, 8.7 us)
Async XLA Ops:
  6.9 49.1 %all-to-all-start = ((bf16[4,64,7168]{2,1,0:T(8,128)(2,1)}), bf16[4,64,7168]{2,1,0:T(8,128)(2,1)}, u32[]{:S(2)}, u32[]{:S(2)}) async-start(bf16[4,64,7168]{2,1,0:T(8,128)(2,1)} %bitcast.46), calls=%async_computation | async-start | bytes 7340032 | tf_op jit(solution)/shard_map/all_to_all | solution.py:22
  12.3 4.4 %copy-start.2 = (s32[16,8]{0,1:T(8,128)S(1)}, s32[16,8]{0,1:T(8,128)}, u32[]{:S(2)}) copy-start(s32[16,8]{0,1:T(8,128)} %param.13) | copy-start | bytes 1540
  12.3 4.4 %copy-start.3 = (bf16[16,8]{0,1:T(8,128)(2,1)S(1)}, bf16[16,8]{0,1:T(8,128)(2,1)}, u32[]{:S(2)}) copy-start(bf16[16,8]{0,1:T(8,128)(2,1)} %param.14) | copy-start | bytes 772
  12.3 10.6 %copy-start.1 = (f32[7168]{0:T(1024)S(1)}, f32[7168]{0:T(1024)}, u32[]{:S(2)}) copy-start(f32[7168]{0:T(1024)} %param.12) | copy-start | bytes 86020
  15.2 24.9 %collective-permute-start.5 = (bf16[256,1792]{1,0:T(8,128)(2,1)S(1)}, bf16[256,1792]{1,0:T(8,128)(2,1)}, u32[]{:S(2)}, u32[]{:S(2)}) collective-permute-start(bf16[256,1792]{1,0:T(8,128)(2,1)S(1)} %get-tuple-element.45), channel_id=1, source_target_pairs={{1,0},{0,1},{3,2},{2,3},{19,16},{18,17},{17,18},{16,19},{5,4},{4,5... | collective-permute-start | bytes 2752520 | tf_op jit(solution)/shard_map/ppermute | solution.py:39
  16.7 19.2 %collective-permute-start.2 = (bf16[16,128]{0,1:T(8,128)(2,1)S(1)}, bf16[16,128]{0,1:T(8,128)(2,1)S(1)}, u32[]{:S(2)}, u32[]{:S(2)}) collective-permute-start(bf16[16,128]{0,1:T(8,128)(2,1)S(1)} %fusion.15), channel_id=1, source_target_pairs={{0,1},{1,2},{2,3},{3,0},{4,5},{5,6},{6,7},{7,4},{8,9},{9,10},{10,1... | collective-permute-start | bytes 12296 | tf_op jit(solution)/shard_map/ppermute | solution.py:18
  17.3 22.6 %collective-permute-start.1 = (bf16[16,128]{0,1:T(8,128)(2,1)S(1)}, bf16[16,128]{0,1:T(8,128)(2,1)S(1)}, u32[]{:S(2)}, u32[]{:S(2)}) collective-permute-start(bf16[16,128]{0,1:T(8,128)(2,1)S(1)} %fusion.15), channel_id=1, source_target_pairs={{0,2},{1,3},{2,0},{3,1},{4,6},{5,7},{6,4},{7,5},{8,10},{9,11},{10,... | collective-permute-start | bytes 12296 | tf_op jit(solution)/shard_map/ppermute | solution.py:18
  20.4 19.6 %collective-permute-start = (bf16[16,128]{0,1:T(8,128)(2,1)S(1)}, bf16[16,128]{0,1:T(8,128)(2,1)S(1)}, u32[]{:S(2)}, u32[]{:S(2)}) collective-permute-start(bf16[16,128]{0,1:T(8,128)(2,1)S(1)} %fusion.15), channel_id=1, source_target_pairs={{0,3},{1,0},{2,1},{3,2},{4,7},{5,4},{6,5},{7,6},{8,11},{9,8},{10,9... | collective-permute-start | bytes 12296 | tf_op jit(solution)/shard_map/ppermute | solution.py:18
  22.2 30.4 %collective-permute-start.4 = (bf16[256,1792]{1,0:T(8,128)(2,1)}, bf16[256,1792]{1,0:T(8,128)(2,1)S(1)}, u32[]{:S(2)}, u32[]{:S(2)}) collective-permute-start(bf16[256,1792]{1,0:T(8,128)(2,1)} %get-tuple-element.47), channel_id=1, source_target_pairs={{3,0},{2,1},{1,2},{0,3},{17,16},{16,17},{19,18},{18,19},{7,4},{6,5... | collective-permute-start | bytes 2752520 | tf_op jit(solution)/shard_map/ppermute | solution.py:39
  40.1 14.9 %collective-permute-start.6 = (bf16[256,1792]{1,0:T(8,128)(2,1)}, bf16[256,1792]{1,0:T(8,128)(2,1)S(1)}, u32[]{:S(2)}, u32[]{:S(2)}) collective-permute-start(bf16[256,1792]{1,0:T(8,128)(2,1)} %collective-permute-done.5), channel_id=1, source_target_pairs={{3,0},{2,1},{1,2},{0,3},{17,16},{16,17},{19,18},{18,19},{7,4},{6,5... | collective-permute-start | bytes 2752520 | tf_op jit(solution)/shard_map/ppermute | solution.py:39
  40.3 10.7 %collective-permute-start.3 = (bf16[64,128]{0,1:T(8,128)(2,1)S(1)}, bf16[64,128]{0,1:T(8,128)(2,1)S(1)}, u32[]{:S(2)}, u32[]{:S(2)}) collective-permute-start(bf16[64,128]{0,1:T(8,128)(2,1)S(1)} %constant_dynamic-slice_fusion), channel_id=1, source_target_pairs={{0,16},{16,0},{1,17},{17,1},{2,18},{18,2},{3,19},{19,3},{4,20},{20... | collective-permute-start | bytes 49160 | tf_op jit(solution)/shard_map/ppermute | solution.py:18
  77.3 7.3 %collective-permute-start.9 = (bf16[64,1792]{1,0:T(8,128)(2,1)S(1)}, bf16[64,1792]{1,0:T(8,128)(2,1)S(1)}, u32[]{:S(2)}, u32[]{:S(2)}) collective-permute-start(bf16[64,1792]{1,0:T(8,128)(2,1)S(1)} %reduce_sum.22), channel_id=1, source_target_pairs={{19,0},{18,1},{17,2},{16,3},{1,16},{0,17},{3,18},{2,19},{23,4},{22... | collective-permute-start | bytes 688136 | tf_op jit(solution)/shard_map/ppermute | solution.py:39
  77.4 7.2 %collective-permute-start.8 = (bf16[64,1792]{1,0:T(8,128)(2,1)S(1)}, bf16[64,1792]{1,0:T(8,128)(2,1)S(1)}, u32[]{:S(2)}, u32[]{:S(2)}) collective-permute-start(bf16[64,1792]{1,0:T(8,128)(2,1)S(1)} %reduce_sum.22), channel_id=1, source_target_pairs={{16,0},{17,1},{18,2},{19,3},{0,16},{1,17},{2,18},{3,19},{20,4},{21... | collective-permute-start | bytes 688136 | tf_op jit(solution)/shard_map/ppermute | solution.py:39
  78.6 7.8 %collective-permute-start.7 = (bf16[64,1792]{1,0:T(8,128)(2,1)S(1)}, bf16[64,1792]{1,0:T(8,128)(2,1)S(1)}, u32[]{:S(2)}, u32[]{:S(2)}) collective-permute-start(bf16[64,1792]{1,0:T(8,128)(2,1)S(1)} %reduce_sum.22), channel_id=1, source_target_pairs={{3,0},{2,1},{1,2},{0,3},{17,16},{16,17},{19,18},{18,19},{7,4},{6,5... | collective-permute-start | bytes 688136 | tf_op jit(solution)/shard_map/ppermute | solution.py:39
  86.5 61.0 %collective-permute-start.10 = (bf16[8960,256]{1,0:T(8,128)(2,1)}, bf16[8960,256]{1,0:T(8,128)(2,1)S(1)}, u32[]{:S(2)}, u32[]{:S(2)}) collective-permute-start(bf16[8960,256]{1,0:T(8,128)(2,1)} %shard_map.93), channel_id=1, source_target_pairs={{1,0},{0,1},{3,2},{2,3},{19,16},{18,17},{17,18},{16,19},{5,4},{4,5... | collective-permute-start | bytes 13762568 | tf_op jit(solution)/shard_map/ppermute | solution.py:39
  147.5 5.0 %copy-start = (bf16[3584,512]{1,0:T(8,128)(2,1)S(1)}, bf16[3584,512]{1,0:T(8,128)(2,1)}, u32[]{:S(2)}) copy-start(bf16[3584,512]{1,0:T(8,128)(2,1)} %shard_map.92) | copy-start | bytes 11010052
  150.4 7.1 %collective-permute-start.12 = (f32[640,1]{1,0:T(8,128)S(1)}, f32[640,1]{1,0:T(8,128)S(1)}, u32[]{:S(2)}, u32[]{:S(2)}) collective-permute-start(f32[640,1]{1,0:T(8,128)S(1)} %get-tuple-element.41), channel_id=1, source_target_pairs={{1,0},{0,1},{3,2},{2,3},{19,16},{18,17},{17,18},{16,19},{5,4},{4,5... | collective-permute-start | bytes 7688 | tf_op jit(solution)/shard_map/ppermute | solution.py:39
  150.8 13.7 %collective-permute-start.11 = (bf16[640,512]{1,0:T(8,128)(2,1)S(1)}, bf16[640,512]{1,0:T(8,128)(2,1)S(1)}, u32[]{:S(2)}, u32[]{:S(2)}) collective-permute-start(bf16[640,512]{1,0:T(8,128)(2,1)S(1)} %get-tuple-element.38), channel_id=1, source_target_pairs={{1,0},{0,1},{3,2},{2,3},{19,16},{18,17},{17,18},{16,19},{5,4},{4,5... | collective-permute-start | bytes 1966088 | tf_op jit(solution)/shard_map/ppermute | solution.py:39
  165.0 11.9 %collective-permute-start.15 = (bf16[640,256]{1,0:T(8,128)(2,1)S(1)}, bf16[640,256]{1,0:T(8,128)(2,1)S(1)}, u32[]{:S(2)}, u32[]{:S(2)}) collective-permute-start(bf16[640,256]{1,0:T(8,128)(2,1)S(1)} %fusion.7.refs_0_), channel_id=1, source_target_pairs={{0,2},{1,3},{2,0},{3,1},{4,6},{5,7},{6,4},{7,5},{8,10},{9,11},{10,... | collective-permute-start | bytes 983048 | tf_op jit(solution)/shard_map/ppermute | solution.py:18
  167.2 13.2 %collective-permute-start.14 = (bf16[640,256]{1,0:T(8,128)(2,1)S(1)}, bf16[640,256]{1,0:T(8,128)(2,1)S(1)}, u32[]{:S(2)}, u32[]{:S(2)}) collective-permute-start(bf16[640,256]{1,0:T(8,128)(2,1)S(1)} %fusion.7.refs_0_), channel_id=1, source_target_pairs={{3,0},{2,1},{1,2},{0,3},{17,16},{16,17},{19,18},{18,19},{7,4},{6,5... | collective-permute-start | bytes 983048 | tf_op jit(solution)/shard_map/ppermute | solution.py:39
  168.1 12.5 %collective-permute-start.13 = (bf16[640,256]{1,0:T(8,128)(2,1)S(1)}, bf16[640,256]{1,0:T(8,128)(2,1)S(1)}, u32[]{:S(2)}, u32[]{:S(2)}) collective-permute-start(bf16[640,256]{1,0:T(8,128)(2,1)S(1)} %fusion.7.refs_0_), channel_id=1, source_target_pairs={{1,0},{0,1},{3,2},{2,3},{19,16},{18,17},{17,18},{16,19},{5,4},{4,5... | collective-permute-start | bytes 983048 | tf_op jit(solution)/shard_map/ppermute | solution.py:39
  219.6 1.9 collective-permute-start.16

commit v7 on v6

--- a/solution.py
+++ b/solution.py
@@ -39,64 +39,73 @@
     return lax.ppermute(value, ("c", "x"), pairs)
 
 
-def project_body(mine_ref, a_ref, b_ref, r_ref, o_ref, acc_ref):
-    own = r_ref.shape[0]
-    acc_ref[...] = jnp.dot(a_ref[...], b_ref[...], preferred_element_type=F32)
-    here = pl.ds(pl.multiple_of(mine_ref[0] * own, own), own)
-    acc_ref[here, :] += r_ref[...].astype(F32)
-    o_ref[...] = acc_ref[...].astype(BF16)
-
-
-def project(mine, context, weight, residual, blocks):
+def project_body(a_ref, b_ref, o_ref):
+    o_ref[...] = jnp.dot(a_ref[...], b_ref[...], preferred_element_type=F32).astype(BF16)
+
+
+def project(context, weight, blocks):
     rows, depth = context.shape
-    own, width = residual.shape
+    width = weight.shape[1]
     step = width // blocks
     return pl.pallas_call(
         project_body,
         out_shape=jax.ShapeDtypeStruct((rows, width), BF16),
+        grid=(blocks,),
+        in_specs=[
+            pl.BlockSpec((rows, depth), lambda q: (0, 0)),
+            pl.BlockSpec((depth, step), lambda q: (0, q)),
+        ],
+        out_specs=pl.BlockSpec((rows, step), lambda q: (0, q)),
+        compiler_params=pltpu.CompilerParams(vmem_limit_bytes=56 << 20),
+        cost_estimate=pl.CostEstimate(
+            flops=2 * rows * depth * width,
+            bytes_accessed=2 * (rows * depth + depth * width + rows * width),
+            transcendentals=0,
+        ),
+    )(context, weight)
+
+
+def owner_sum_body(at_ref, a_ref, r_ref, *refs):
+    outs, acc_ref = refs[:-1], refs[-1]
+    step = pl.program_id(0)
+    own = r_ref.shape[0]
+    total = a_ref[0].astype(F32)
+    for i in range(1, a_ref.shape[0]):
+        total += a_ref[i].astype(F32)
+    acc_ref[...] = total
+    here = pl.ds(pl.multiple_of(at_ref[0] * own, own), own)
+    acc_ref[here, :] += r_ref[...].astype(F32)
+    for k, o_ref in enumerate(outs):
+
+        @pl.when(step == k)
+        def _():
+            o_ref[...] = acc_ref[...].astype(BF16)
+
+
+def owner_sum(at, terms, residual, blocks):
+    count, rows, width = terms.shape
+    step = width // blocks
+    turn = lambda q, at: lax.rem(at[0] + q, blocks)
+    return pl.pallas_call(
+        owner_sum_body,
+        out_shape=[jax.ShapeDtypeStruct((rows, step), BF16)] * blocks,
         grid_spec=pltpu.PrefetchScalarGridSpec(
             num_scalar_prefetch=1,
             grid=(blocks,),
             in_specs=[
-                pl.BlockSpec((rows, depth), lambda q, m: (0, 0)),
-                pl.BlockSpec((depth, step), lambda q, m: (0, q)),
-                pl.BlockSpec((own, step), lambda q, m: (0, q)),
+                pl.BlockSpec((count, rows, step), lambda q, at: (0, 0, turn(q, at))),
+                pl.BlockSpec((residual.shape[0], step), lambda q, at: (0, turn(q, at))),
             ],
-            out_specs=pl.BlockSpec((rows, step), lambda q, m: (0, q)),
+            out_specs=[pl.BlockSpec((rows, step), lambda q, at: (0, 0))] * blocks,
             scratch_shapes=[pltpu.VMEM((rows, step), F32)],
         ),
-        compiler_params=pltpu.CompilerParams(vmem_limit_bytes=56 << 20),
-        cost_estimate=pl.CostEstimate(
-            flops=2 * rows * depth * width,
-            bytes_accessed=2 * (rows * depth + depth * width + rows * width),
-            transcendentals=0,
-        ),
-    )(mine, context, weight, residual)
-
-
-def gather_sum_body(a_ref, o_ref):
-    total = a_ref[0].astype(F32)
-    for i in range(1, a_ref.shape[0]):
-        total += a_ref[i].astype(F32)
-    o_ref[0] = total.astype(BF16)
-
-
-def gather_sum(terms, blocks):
-    count, rows, width = terms.shape
-    step = width // blocks
-    return pl.pallas_call(
-        gather_sum_body,
-        out_shape=jax.ShapeDtypeStruct((blocks, rows, step), BF16),
-        grid=(blocks,),
-        in_specs=[pl.BlockSpec((count, rows, step), lambda q: (0, 0, q))],
-        out_specs=pl.BlockSpec((1, rows, step), lambda q: (q, 0, 0)),
         compiler_params=pltpu.CompilerParams(vmem_limit_bytes=24 << 20),
         cost_estimate=pl.CostEstimate(
             flops=count * rows * width,
             bytes_accessed=2 * (count + 1) * rows * width,
             transcendentals=0,
         ),
-    )(terms)
+    )(at, terms, residual)
 
 
 def first_body(a_ref, gain_ref, w_ref, g_ref, s_ref, o_ref):
@@ -265,8 +274,7 @@
             down_proj[0], (0, at * quarter), (down_proj.shape[1], quarter)
         )
 
-    mine = lax.axis_index("z") * nx + x
-    part = project(mine[None].astype(jnp.int32), context, out_proj, residual, nx)
+    part = project(context, out_proj, nx)
 
     meta = jnp.concatenate([expert_ids.astype(BF16), gates], axis=1)
     meta = jnp.pad(meta, ((0, 0), (0, 128 - meta.shape[1])))
@@ -311,9 +319,10 @@
             (selector, scaled, part, kept, given, own_down, gain, twin_down, far_down)
         )
     )
-    part = exchange(gather_sum(part, nx), "x")
-
-    hidden = jnp.sum(part.astype(F32), axis=0).astype(BF16)
+    parts = owner_sum(x[None].astype(jnp.int32), part, residual, nx)
+    came = [parts[0]] + [shift(parts[k], "x", k) for k in (2, 1, 3)]
+
+    hidden = sum(term.astype(F32) for term in came).astype(BF16)
     hidden_wide = hidden.astype(F32)
 
     twin_own = from_places(hidden, lambda c, x: (c, twin_of(c, x)))

time: 233 us -> 231 us (level)
  blocking collectives: 122 us -> 106 us
  waiting for transfers between devices: 49.4 us -> 58.3 us
  starting transfers between devices: 21.6 us -> 27.9 us
    all_to_all x4 -> x3, blocking collectives: 122 us -> 106 us  [exchange(): return lax.all_to_all(value, axes, split_axis=0, concat_axis=0, tiled=True)]
    ppermute x6 -> x9, waiting for transfers between devices: 27.1 us -> 34.1 us  [shift(): lax.ppermute(value, axis, [(i, (i + amount) % size) for i in range(size)])]
    ppermute x6 -> x9, starting transfers between devices: 7.76 us -> 12.1 us  [shift(): lax.ppermute(value, axis, [(i, (i + amount) % size) for i in range(size)])]
  transfers between devices with their start and end apart: 18 -> 21, of which waited for: 12 -> 14; matrix products, arithmetic and copies ran while one was open for 4% -> 4% of each run, Pallas kernels for 4% -> 5%
where the time goes in v7:
time: 231 us; the launch traced here: 230 us
  blocking collectives  106 us (46%)
  waiting for transfers between devices  58.3 us (25%)
  starting transfers between devices  27.9 us (12%)
  Pallas kernels  26.1 us (11%)
  local copies, waits for them, and re-layouts  4.53 us (2%)
  matrix products  4.42 us (2%)
  other arithmetic  2.64 us (1%)
    all_to_all x3, blocking collectives, exchange(): return lax.all_to_all(value, axes, split_axis=0, concat_axis=0, tiled=True)  106 us
    ppermute x9, waiting for transfers between devices, shift(): lax.ppermute(value, axis, [(i, (i + amount) % size) for i in range(size)])  34.1 us
    ppermute x11, waiting for transfers between devices, from_places(): return lax.ppermute(value, ('c', 'x'), pairs)  23.1 us
    ppermute x9, starting transfers between devices, shift(): lax.ppermute(value, axis, [(i, (i + amount) % size) for i in range(size)])  12.1 us
    ppermute x11, starting transfers between devices, from_places(): return lax.ppermute(value, ('c', 'x'), pairs)  10.4 us
    pallas_call x1, Pallas kernels, project(): pl.pallas_call(project_body, out_shape=jax.ShapeDtypeStruct((rows, width)...  6.57 us
    pallas_call x1, Pallas kernels, bundle(): pl.pallas_call(bundle_body, out_shape=jax.ShapeDtypeStruct((5 * cut, h),...  6.38 us
    all_to_all x1, starting transfers between devices, exchange(): return lax.all_to_all(value, axes, split_axis=0, concat_axis=0, tiled=True)  5.39 us
  transfers between devices with their start and end apart: 21, of which 14 were waited for; matrix products, arithmetic and copies ran while one was open for 4% of the time, Pallas kernels for 5%

profile of v7, /device:TPU:0, one launch (start us, length us, event | category | flops | bytes accessed | tf_op | source)
XLA Modules:
  0.0 229.8 jit_solution(14113310237853277337)
XLA Ops:
  0.0 6.6 %shard_map.91 = bf16[256,7168]{1,0:T(8,128)(2,1)} custom-call(bf16[256,512]{1,0:T(8,128)(2,1)} %a_ref.1, bf16[512,7168]{1,0:T(8,128)(2,1)} %b_ref.1), custom_call_target="tpu_custom_call" | custom-call | flops 1879048192 | bytes 11272192 | tf_op jit(solution)/shard_map/pallas_call | solution.py:50
  6.6 5.4 %all-to-all-start = ((bf16[4,64,7168]{2,1,0:T(8,128)(2,1)}), bf16[4,64,7168]{2,1,0:T(8,128)(2,1)}, u32[]{:S(2)}, u32[]{:S(2)}) async-start(bf16[4,64,7168]{2,1,0:T(8,128)(2,1)} %bitcast.45), calls=%async_computation | async-start | bytes 7340032 | tf_op jit(solution)/shard_map/all_to_all | solution.py:22
  12.0 2.9 %dynamic-slice_bitcast_fusion = (bf16[256,1792]{1,0:T(8,128)(2,1)S(1)}, bf16[256,1792]{1,0:T(8,128)(2,1)S(1)}, bf16[256,1792]{1,0:T(8,128)(2,1)}) fusion(bf16[1,256,7168]{2,1,0:T(8,128)(2,1)} %d_ref.1, s32[]{:T(128)S(6)} %select_n.53, s32[]{:T(128)S(6)} %select_n.51, s32[]{:T(128)S(6)} %select_n.52), kind=kLoop, calls=%fused_computation.9 | loop fusion | bytes 5505036 | tf_op jit(solution)/shard_map/dynamic_slice | solution.py:273
  14.9 1.5 collective-permute-start.5
  17.0 3.0 %collective-permute-start.1 = (bf16[16,128]{0,1:T(8,128)(2,1)S(1)}, bf16[16,128]{0,1:T(8,128)(2,1)S(1)}, u32[]{:S(2)}, u32[]{:S(2)}) collective-permute-start(bf16[16,128]{0,1:T(8,128)(2,1)S(1)} %fusion.15), channel_id=1, source_target_pairs={{0,2},{1,3},{2,0},{3,1},{4,6},{5,7},{6,4},{7,5},{8,10},{9,11},{10,... | collective-permute-start | bytes 12296 | tf_op jit(solution)/shard_map/ppermute | solution.py:18
  20.0 1.8 collective-permute-start
  22.6 13.0 %collective-permute-done.2 = bf16[16,128]{0,1:T(8,128)(2,1)S(1)} collective-permute-done((bf16[16,128]{0,1:T(8,128)(2,1)S(1)}, bf16[16,128]{0,1:T(8,128)(2,1)S(1)}, u32[]{:S(2)}, u32[]{:S(2)}) %collective-permute-start.2) | collective-permute-done | bytes 4128 | tf_op jit(solution)/shard_map/ppermute | solution.py:18
  35.6 3.9 %collective-permute-done.1 = bf16[16,128]{0,1:T(8,128)(2,1)S(1)} collective-permute-done((bf16[16,128]{0,1:T(8,128)(2,1)S(1)}, bf16[16,128]{0,1:T(8,128)(2,1)S(1)}, u32[]{:S(2)}, u32[]{:S(2)}) %collective-permute-start.1) | collective-permute-done | bytes 4128 | tf_op jit(solution)/shard_map/ppermute | solution.py:18
  40.2 4.1 %shard_map.92 = bf16[3584,512]{1,0:T(8,128)(2,1)} custom-call(s32[2]{0:T(128)} %get-tuple-element.60.at_ref, bf16[1,7168,256]{2,1,0:T(8,128)(2,1)} %g_ref.3, bf16[1,7168,256]{2,1,0:T(8,128)(2,1)} %u_ref.3), custom_call_target="tpu_custom_call" | custom-call | bytes 7340032 | tf_op jit(solution)/shard_map/pallas_call | solution.py:237
  44.3 6.4 %shard_map.93 = bf16[8960,256]{1,0:T(8,128)(2,1)} custom-call(s32[2]{0:T(128)} %get-tuple-element.61.at_ref, bf16[1,7168,256]{2,1,0:T(8,128)(2,1)} %g_ref.3, bf16[1,7168,256]{2,1,0:T(8,128)(2,1)} %u_ref.3, bf16[1,256,7168]{2,1,0:T(8,128)(2,1)} %d_ref.1), custom_call_target="tpu_custom_call" | custom-call | bytes 9175040 | tf_op jit(solution)/shard_map/pallas_call | solution.py:207
  52.4 2.2 collective-permute-done.6.refs_7_
  55.8 3.5 %shard_map.94 = (bf16[64,1792]{1,0:T(8,128)(2,1)S(1)}, bf16[64,1792]{1,0:T(8,128)(2,1)S(1)}, bf16[64,1792]{1,0:T(8,128)(2,1)S(1)}, bf16[64,1792]{1,0:T(8,128)(2,1)S(1)}) custom-call(s32[1]{0:T(128)} %bitcast.at_ref, bf16[4,64,7168]{2,1,0:T(8,128)(2,1)} %all-to-all-done.a_ref, bf16[16,7168]{1,0:T(8,128)(2,1)S(1)} %copy-done), custom_call_target="tpu_custom_call" | custom-call | flops 1835008 | bytes 4587520 | tf_op jit(solution)/shard_map/pallas_call | solution.py:89
  59.3 3.1 %collective-permute-start.7 = (bf16[64,1792]{1,0:T(8,128)(2,1)S(1)}, bf16[64,1792]{1,0:T(8,128)(2,1)S(1)}, u32[]{:S(2)}, u32[]{:S(2)}) collective-permute-start(bf16[64,1792]{1,0:T(8,128)(2,1)S(1)} %get-tuple-element.31), channel_id=1, source_target_pairs={{0,2},{1,3},{2,0},{3,1},{4,6},{5,7},{6,4},{7,5},{8,10},{9,11},{10,... | collective-permute-start | bytes 688136 | tf_op jit(solution)/shard_map/ppermute | solution.py:18
  63.0 2.6 %collective-permute-start.9 = (bf16[64,1792]{1,0:T(8,128)(2,1)S(1)}, bf16[64,1792]{1,0:T(8,128)(2,1)S(1)}, u32[]{:S(2)}, u32[]{:S(2)}) collective-permute-start(bf16[64,1792]{1,0:T(8,128)(2,1)S(1)} %get-tuple-element.33), channel_id=1, source_target_pairs={{0,3},{1,0},{2,1},{3,2},{4,7},{5,4},{6,5},{7,6},{8,11},{9,8},{10,9... | collective-permute-start | bytes 688136 | tf_op jit(solution)/shard_map/ppermute | solution.py:18
  65.6 3.8 %collective-permute-done.7 = bf16[64,1792]{1,0:T(8,128)(2,1)S(1)} collective-permute-done((bf16[64,1792]{1,0:T(8,128)(2,1)S(1)}, bf16[64,1792]{1,0:T(8,128)(2,1)S(1)}, u32[]{:S(2)}, u32[]{:S(2)}) %collective-permute-start.7) | collective-permute-done | bytes 229408 | tf_op jit(solution)/shard_map/ppermute | solution.py:18
  69.4 2.7 %collective-permute-done.8 = bf16[64,1792]{1,0:T(8,128)(2,1)S(1)} collective-permute-done((bf16[64,1792]{1,0:T(8,128)(2,1)S(1)}, bf16[64,1792]{1,0:T(8,128)(2,1)S(1)}, u32[]{:S(2)}, u32[]{:S(2)}) %collective-permute-start.8) | collective-permute-done | bytes 229408 | tf_op jit(solution)/shard_map/ppermute | solution.py:18
  73.5 1.8 collective-permute-start.11
  75.8 3.3 %collective-permute-done.12 = bf16[64,1792]{1,0:T(8,128)(2,1)S(1)} collective-permute-done((bf16[64,1792]{1,0:T(8,128)(2,1)S(1)}, bf16[64,1792]{1,0:T(8,128)(2,1)S(1)}, u32[]{:S(2)}, u32[]{:S(2)}) %collective-permute-start.12) | collective-permute-done | bytes 229408 | tf_op jit(solution)/shard_map/ppermute | solution.py:39
  79.1 3.4 %collective-permute-done.10 = bf16[64,1792]{1,0:T(8,128)(2,1)S(1)} collective-permute-done((bf16[64,1792]{1,0:T(8,128)(2,1)S(1)}, bf16[64,1792]{1,0:T(8,128)(2,1)S(1)}, u32[]{:S(2)}, u32[]{:S(2)}) %collective-permute-start.10) | collective-permute-done | bytes 229408 | tf_op jit(solution)/shard_map/ppermute | solution.py:39
  83.8 61.5 %all_to_all.20 = bf16[16,40,3584]{2,1,0:T(8,128)(2,1)S(1)} all-to-all(bf16[16,40,3584]{2,1,0:T(8,128)(2,1)S(1)} %bitcast.44), channel_id=1, replica_groups=mesh['y'=4,'c'=2,'z'=4,'x'=4] {'y','z'}, dimensions={0} | all-to-all | bytes 9175040 | tf_op jit(solution)/shard_map/all_to_all | solution.py:22
  145.3 3.0 %shard_map.95 = (bf16[640,3584]{1,0:T(8,128)(2,1)S(1)}, f32[640,1]{1,0:T(8,128)S(1)}, bf16[640,512]{1,0:T(8,128)(2,1)S(1)}) custom-call(bf16[640,3584]{1,0:T(8,128)(2,1)S(1)} %bitcast.42, f32[1,3584]{1,0:T(1,128)S(1)} %broadcast_in_dim.50.gain_ref, bf16[8960,256]{1,0:T(8,128)(2,1)S(1)} %collective-permute-done.13.w_ref.refs_5_), custom_call_target="tpu_custom_call" | custom-call | flops 2348810240 | bytes 13500416 | tf_op jit(solution)/shard_map/pallas_call | solution.py:135
  148.3 2.0 collective-permute-start.14
  150.3 2.5 %fusion.24 = f32[640,512]{1,0:T(8,128)S(1)} fusion(bf16[640,3584]{1,0:T(8,128)(2,1)S(1)} %get-tuple-element.44, bf16[3584,512]{1,0:T(8,128)(2,1)S(1)} %copy-done.2), kind=kOutput, calls=%fused_computation.50 | convolution fusion | flops 2348810240 | bytes 9568256 | tf_op jit(solution)/shard_map/dot_general | solution.py:350
  152.9 2.5 %collective-permute-done.15 = f32[640,1]{1,0:T(8,128)S(1)} collective-permute-done((f32[640,1]{1,0:T(8,128)S(1)}, f32[640,1]{1,0:T(8,128)S(1)}, u32[]{:S(2)}, u32[]{:S(2)}) %collective-permute-start.15) | collective-permute-done | bytes 2592 | tf_op jit(solution)/shard_map/ppermute | solution.py:39
  155.6 6.8 %collective-permute-done.14 = bf16[640,512]{1,0:T(8,128)(2,1)S(1)} collective-permute-done((bf16[640,512]{1,0:T(8,128)(2,1)S(1)}, bf16[640,512]{1,0:T(8,128)(2,1)S(1)}, u32[]{:S(2)}, u32[]{:S(2)}) %collective-permute-start.14) | collective-permute-done | bytes 655392 | tf_op jit(solution)/shard_map/ppermute | solution.py:39
  163.0 2.5 %collective-permute-start.17 = (bf16[640,256]{1,0:T(8,128)(2,1)S(1)}, bf16[640,256]{1,0:T(8,128)(2,1)S(1)}, u32[]{:S(2)}, u32[]{:S(2)}) collective-permute-start(bf16[640,256]{1,0:T(8,128)(2,1)S(1)} %fusion.7.refs_0_), channel_id=1, source_target_pairs={{3,0},{2,1},{1,2},{0,3},{17,16},{16,17},{19,18},{18,19},{7,4},{6,5... | collective-permute-start | bytes 983048 | tf_op jit(solution)/shard_map/ppermute | solution.py:39
  166.4 8.7 %collective-permute-done.18.refs_3_ = bf16[640,256]{1,0:T(8,128)(2,1)S(1)} collective-permute-done((bf16[640,256]{1,0:T(8,128)(2,1)S(1)}, bf16[640,256]{1,0:T(8,128)(2,1)S(1)}, u32[]{:S(2)}, u32[]{:S(2)}) %collective-permute-start.18) | collective-permute-done | bytes 327712 | tf_op jit(solution)/shard_map/ppermute | solution.py:18
  175.1 4.8 %collective-permute-done.17.refs_2_ = bf16[640,256]{1,0:T(8,128)(2,1)S(1)} collective-permute-done((bf16[640,256]{1,0:T(8,128)(2,1)S(1)}, bf16[640,256]{1,0:T(8,128)(2,1)S(1)}, u32[]{:S(2)}, u32[]{:S(2)}) %collective-permute-start.17) | collective-permute-done | bytes 327712 | tf_op jit(solution)/shard_map/ppermute | solution.py:39
  179.9 2.5 %shard_map.96 = bf16[640,1792]{1,0:T(8,128)(2,1)S(1)} custom-call(bf16[640,256]{1,0:T(8,128)(2,1)S(1)} %fusion.7.refs_0_, bf16[640,256]{1,0:T(8,128)(2,1)S(1)} %collective-permute-done.16.refs_1_, bf16[640,256]{1,0:T(8,128)(2,1)S(1)} %collective-permute-done.17.refs_2_, bf16[640,256]{1,0:T(8,128)(2,1)S(1)} %collective-permute-done.18.refs_3_, ...), custom_call_target="tpu_custom_call" | custom-call | flops 2348810240 | bytes 7274496 | tf_op jit(solution)/shard_map/pallas_call | solution.py:169
  182.4 34.9 %all_to_all.21 = bf16[16,40,1792]{2,1,0:T(8,128)(2,1)S(1)} all-to-all(bf16[16,40,1792]{2,1,0:T(8,128)(2,1)S(1)} %bitcast.43), channel_id=1, replica_groups=mesh['y'=4,'c'=2,'z'=4,'x'=4] {'y','z'}, dimensions={0} | all-to-all | bytes 4587520 | tf_op jit(solution)/shard_map/all_to_all | solution.py:22
  218.0 1.8 collective-permute-done.19
  219.9 9.3 %all_to_all.22 = bf16[4,16,1792]{2,1,0:T(8,128)(2,1)S(1)} all-to-all(bf16[4,16,1792]{2,1,0:T(8,128)(2,1)S(1)} %bitcast.48), channel_id=1, replica_groups=mesh['y'=4,'c'=2,'z'=4,'x'=4] {'x'}, dimensions={0} | all-to-all | bytes 458752 | tf_op jit(solution)/shard_map/all_to_all | solution.py:22
  (68 shorter events, 11.6 us)
Async XLA Ops:
  6.6 49.2 %all-to-all-start = ((bf16[4,64,7168]{2,1,0:T(8,128)(2,1)}), bf16[4,64,7168]{2,1,0:T(8,128)(2,1)}, u32[]{:S(2)}, u32[]{:S(2)}) async-start(bf16[4,64,7168]{2,1,0:T(8,128)(2,1)} %bitcast.45), calls=%async_computation | async-start | bytes 7340032 | tf_op jit(solution)/shard_map/all_to_all | solution.py:22
  12.0 4.4 %copy-start.4 = (s32[16,8]{0,1:T(8,128)S(1)}, s32[16,8]{0,1:T(8,128)}, u32[]{:S(2)}) copy-start(s32[16,8]{0,1:T(8,128)} %param.13) | copy-start | bytes 1540
  12.0 4.4 %copy-start.5 = (bf16[16,8]{0,1:T(8,128)(2,1)S(1)}, bf16[16,8]{0,1:T(8,128)(2,1)}, u32[]{:S(2)}) copy-start(bf16[16,8]{0,1:T(8,128)(2,1)} %param.14) | copy-start | bytes 772
  12.0 10.5 %copy-start.3 = (f32[7168]{0:T(1024)S(1)}, f32[7168]{0:T(1024)}, u32[]{:S(2)}) copy-start(f32[7168]{0:T(1024)} %param.12) | copy-start | bytes 86020
  14.9 24.9 %collective-permute-start.5 = (bf16[256,1792]{1,0:T(8,128)(2,1)S(1)}, bf16[256,1792]{1,0:T(8,128)(2,1)}, u32[]{:S(2)}, u32[]{:S(2)}) collective-permute-start(bf16[256,1792]{1,0:T(8,128)(2,1)S(1)} %get-tuple-element.53), channel_id=1, source_target_pairs={{1,0},{0,1},{3,2},{2,3},{19,16},{18,17},{17,18},{16,19},{5,4},{4,5... | collective-permute-start | bytes 2752520 | tf_op jit(solution)/shard_map/ppermute | solution.py:39
  16.4 19.2 %collective-permute-start.2 = (bf16[16,128]{0,1:T(8,128)(2,1)S(1)}, bf16[16,128]{0,1:T(8,128)(2,1)S(1)}, u32[]{:S(2)}, u32[]{:S(2)}) collective-permute-start(bf16[16,128]{0,1:T(8,128)(2,1)S(1)} %fusion.15), channel_id=1, source_target_pairs={{0,1},{1,2},{2,3},{3,0},{4,5},{5,6},{6,7},{7,4},{8,9},{9,10},{10,1... | collective-permute-start | bytes 12296 | tf_op jit(solution)/shard_map/ppermute | solution.py:18
  17.0 22.6 %collective-permute-start.1 = (bf16[16,128]{0,1:T(8,128)(2,1)S(1)}, bf16[16,128]{0,1:T(8,128)(2,1)S(1)}, u32[]{:S(2)}, u32[]{:S(2)}) collective-permute-start(bf16[16,128]{0,1:T(8,128)(2,1)S(1)} %fusion.15), channel_id=1, source_target_pairs={{0,2},{1,3},{2,0},{3,1},{4,6},{5,7},{6,4},{7,5},{8,10},{9,11},{10,... | collective-permute-start | bytes 12296 | tf_op jit(solution)/shard_map/ppermute | solution.py:18
  20.0 19.6 %collective-permute-start = (bf16[16,128]{0,1:T(8,128)(2,1)S(1)}, bf16[16,128]{0,1:T(8,128)(2,1)S(1)}, u32[]{:S(2)}, u32[]{:S(2)}) collective-permute-start(bf16[16,128]{0,1:T(8,128)(2,1)S(1)} %fusion.15), channel_id=1, source_target_pairs={{0,3},{1,0},{2,1},{3,2},{4,7},{5,4},{6,5},{7,6},{8,11},{9,8},{10,9... | collective-permute-start | bytes 12296 | tf_op jit(solution)/shard_map/ppermute | solution.py:18
  21.8 30.6 %collective-permute-start.4 = (bf16[256,1792]{1,0:T(8,128)(2,1)}, bf16[256,1792]{1,0:T(8,128)(2,1)S(1)}, u32[]{:S(2)}, u32[]{:S(2)}) collective-permute-start(bf16[256,1792]{1,0:T(8,128)(2,1)} %get-tuple-element.55), channel_id=1, source_target_pairs={{3,0},{2,1},{1,2},{0,3},{17,16},{16,17},{19,18},{18,19},{7,4},{6,5... | collective-permute-start | bytes 2752520 | tf_op jit(solution)/shard_map/ppermute | solution.py:39
  39.7 14.9 %collective-permute-start.6 = (bf16[256,1792]{1,0:T(8,128)(2,1)}, bf16[256,1792]{1,0:T(8,128)(2,1)S(1)}, u32[]{:S(2)}, u32[]{:S(2)}) collective-permute-start(bf16[256,1792]{1,0:T(8,128)(2,1)} %collective-permute-done.5), channel_id=1, source_target_pairs={{3,0},{2,1},{1,2},{0,3},{17,16},{16,17},{19,18},{18,19},{7,4},{6,5... | collective-permute-start | bytes 2752520 | tf_op jit(solution)/shard_map/ppermute | solution.py:39
  39.9 10.8 %collective-permute-start.3 = (bf16[64,128]{0,1:T(8,128)(2,1)S(1)}, bf16[64,128]{0,1:T(8,128)(2,1)S(1)}, u32[]{:S(2)}, u32[]{:S(2)}) collective-permute-start(bf16[64,128]{0,1:T(8,128)(2,1)S(1)} %constant_dynamic-slice_fusion), channel_id=1, source_target_pairs={{0,16},{16,0},{1,17},{17,1},{2,18},{18,2},{3,19},{19,3},{4,20},{20... | collective-permute-start | bytes 49160 | tf_op jit(solution)/shard_map/ppermute | solution.py:18
  44.3 11.4 %copy-start = (bf16[16,7168]{1,0:T(8,128)(2,1)S(1)}, bf16[16,7168]{1,0:T(8,128)(2,1)}, u32[]{:S(2)}) copy-start(bf16[16,7168]{1,0:T(8,128)(2,1)} %r_ref.1) | copy-start | bytes 688132
  55.8 26.7 %copy-start.1 = (bf16[8960,256]{1,0:T(8,128)(2,1)S(1)}, bf16[8960,256]{1,0:T(8,128)(2,1)}, u32[]{:S(2)}) copy-start(bf16[8960,256]{1,0:T(8,128)(2,1)} %shard_map.93) | copy-start | bytes 13762564
  59.3 10.1 %collective-permute-start.7 = (bf16[64,1792]{1,0:T(8,128)(2,1)S(1)}, bf16[64,1792]{1,0:T(8,128)(2,1)S(1)}, u32[]{:S(2)}, u32[]{:S(2)}) collective-permute-start(bf16[64,1792]{1,0:T(8,128)(2,1)S(1)} %get-tuple-element.31), channel_id=1, source_target_pairs={{0,2},{1,3},{2,0},{3,1},{4,6},{5,7},{6,4},{7,5},{8,10},{9,11},{10,... | collective-permute-start | bytes 688136 | tf_op jit(solution)/shard_map/ppermute | solution.py:18
  62.4 9.8 %collective-permute-start.8 = (bf16[64,1792]{1,0:T(8,128)(2,1)S(1)}, bf16[64,1792]{1,0:T(8,128)(2,1)S(1)}, u32[]{:S(2)}, u32[]{:S(2)}) collective-permute-start(bf16[64,1792]{1,0:T(8,128)(2,1)S(1)} %get-tuple-element.32), channel_id=1, source_target_pairs={{0,1},{1,2},{2,3},{3,0},{4,5},{5,6},{6,7},{7,4},{8,9},{9,10},{10,1... | collective-permute-start | bytes 688136 | tf_op jit(solution)/shard_map/ppermute | solution.py:18
  63.0 9.2 %collective-permute-start.9 = (bf16[64,1792]{1,0:T(8,128)(2,1)S(1)}, bf16[64,1792]{1,0:T(8,128)(2,1)S(1)}, u32[]{:S(2)}, u32[]{:S(2)}) collective-permute-start(bf16[64,1792]{1,0:T(8,128)(2,1)S(1)} %get-tuple-element.33), channel_id=1, source_target_pairs={{0,3},{1,0},{2,1},{3,2},{4,7},{5,4},{6,5},{7,6},{8,11},{9,8},{10,9... | collective-permute-start | bytes 688136 | tf_op jit(solution)/shard_map/ppermute | solution.py:18
  72.4 6.7 %collective-permute-start.12 = (bf16[64,1792]{1,0:T(8,128)(2,1)S(1)}, bf16[64,1792]{1,0:T(8,128)(2,1)S(1)}, u32[]{:S(2)}, u32[]{:S(2)}) collective-permute-start(bf16[64,1792]{1,0:T(8,128)(2,1)S(1)} %add_convert_fusion), channel_id=1, source_target_pairs={{19,0},{18,1},{17,2},{16,3},{1,16},{0,17},{3,18},{2,19},{23,4},{22... | collective-permute-start | bytes 688136 | tf_op jit(solution)/shard_map/ppermute | solution.py:39
  73.5 5.6 %collective-permute-start.11 = (bf16[64,1792]{1,0:T(8,128)(2,1)S(1)}, bf16[64,1792]{1,0:T(8,128)(2,1)S(1)}, u32[]{:S(2)}, u32[]{:S(2)}) collective-permute-start(bf16[64,1792]{1,0:T(8,128)(2,1)S(1)} %add_convert_fusion), channel_id=1, source_target_pairs={{16,0},{17,1},{18,2},{19,3},{0,16},{1,17},{2,18},{3,19},{20,4},{21... | collective-permute-start | bytes 688136 | tf_op jit(solution)/shard_map/ppermute | solution.py:39
  75.2 7.2 %collective-permute-start.10 = (bf16[64,1792]{1,0:T(8,128)(2,1)S(1)}, bf16[64,1792]{1,0:T(8,128)(2,1)S(1)}, u32[]{:S(2)}, u32[]{:S(2)}) collective-permute-start(bf16[64,1792]{1,0:T(8,128)(2,1)S(1)} %add_convert_fusion), channel_id=1, source_target_pairs={{3,0},{2,1},{1,2},{0,3},{17,16},{16,17},{19,18},{18,19},{7,4},{6,5... | collective-permute-start | bytes 688136 | tf_op jit(solution)/shard_map/ppermute | solution.py:39
  82.5 62.9 %collective-permute-start.13 = (bf16[8960,256]{1,0:T(8,128)(2,1)S(1)}, bf16[8960,256]{1,0:T(8,128)(2,1)S(1)}, u32[]{:S(2)}, u32[]{:S(2)}) collective-permute-start(bf16[8960,256]{1,0:T(8,128)(2,1)S(1)} %copy-done.1), channel_id=1, source_target_pairs={{1,0},{0,1},{3,2},{2,3},{19,16},{18,17},{17,18},{16,19},{5,4},{4,5... | collective-permute-start | bytes 13762568 | tf_op jit(solution)/shard_map/ppermute | solution.py:39
  145.3 5.0 %copy-start.2 = (bf16[3584,512]{1,0:T(8,128)(2,1)S(1)}, bf16[3584,512]{1,0:T(8,128)(2,1)}, u32[]{:S(2)}) copy-start(bf16[3584,512]{1,0:T(8,128)(2,1)} %shard_map.92) | copy-start | bytes 11010052
  148.3 7.1 %collective-permute-start.15 = (f32[640,1]{1,0:T(8,128)S(1)}, f32[640,1]{1,0:T(8,128)S(1)}, u32[]{:S(2)}, u32[]{:S(2)}) collective-permute-start(f32[640,1]{1,0:T(8,128)S(1)} %get-tuple-element.49), channel_id=1, source_target_pairs={{1,0},{0,1},{3,2},{2,3},{19,16},{18,17},{17,18},{16,19},{5,4},{4,5... | collective-permute-start | bytes 7688 | tf_op jit(solution)/shard_map/ppermute | solution.py:39
  148.3 14.1 %collective-permute-start.14 = (bf16[640,512]{1,0:T(8,128)(2,1)S(1)}, bf16[640,512]{1,0:T(8,128)(2,1)S(1)}, u32[]{:S(2)}, u32[]{:S(2)}) collective-permute-start(bf16[640,512]{1,0:T(8,128)(2,1)S(1)} %get-tuple-element.46), channel_id=1, source_target_pairs={{1,0},{0,1},{3,2},{2,3},{19,16},{18,17},{17,18},{16,19},{5,4},{4,5... | collective-permute-start | bytes 1966088 | tf_op jit(solution)/shard_map/ppermute | solution.py:39
  162.8 12.2 %collective-permute-start.18 = (bf16[640,256]{1,0:T(8,128)(2,1)S(1)}, bf16[640,256]{1,0:T(8,128)(2,1)S(1)}, u32[]{:S(2)}, u32[]{:S(2)}) collective-permute-start(bf16[640,256]{1,0:T(8,128)(2,1)S(1)} %fusion.7.refs_0_), channel_id=1, source_target_pairs={{0,2},{1,3},{2,0},{3,1},{4,6},{5,7},{6,4},{7,5},{8,10},{9,11},{10,... | collective-permute-start | bytes 983048 | tf_op jit(solution)/shard_map/ppermute | solution.py:18
  163.0 16.9 %collective-permute-start.17 = (bf16[640,256]{1,0:T(8,128)(2,1)S(1)}, bf16[640,256]{1,0:T(8,128)(2,1)S(1)}, u32[]{:S(2)}, u32[]{:S(2)}) collective-permute-start(bf16[640,256]{1,0:T(8,128)(2,1)S(1)} %fusion.7.refs_0_), channel_id=1, source_target_pairs={{3,0},{2,1},{1,2},{0,3},{17,16},{16,17},{19,18},{18,19},{7,4},{6,5... | collective-permute-start | bytes 983048 | tf_op jit(solution)/shard_map/ppermute | solution.py:39
  165.6 14.3 %collective-permute-start.16 = (bf16[640,256]{1,0:T(8,128)(2,1)S(1)}, bf16[640,256]{1,0:T(8,128)(2,1)S(1)}, u32[]{:S(2)}, u32[]{:S(2)}) collective-permute-start(bf16[640,256]{1,0:T(8,128)(2,1)S(1)} %fusion.7.refs_0_), channel_id=1, source_target_pairs={{1,0},{0,1},{3,2},{2,3},{19,16},{18,17},{17,18},{16,19},{5,4},{4,5... | collective-permute-start | bytes 983048 | tf_op jit(solution)/shard_map/ppermute | solution.py:39
  217.9 1.9 collective-permute-start.19

commit v8 on v7

--- a/solution.py
+++ b/solution.py
@@ -274,7 +274,7 @@
             down_proj[0], (0, at * quarter), (down_proj.shape[1], quarter)
         )
 
-    part = project(context, out_proj, nx)
+    part = project(context, out_proj, nx // 2)
 
     meta = jnp.concatenate([expert_ids.astype(BF16), gates], axis=1)
     meta = jnp.pad(meta, ((0, 0), (0, 128 - meta.shape[1])))

time: 231 us -> 230 us (level)
  no operation moved by 1% of the time
where the time goes in v8:
time: 230 us; the launch traced here: 229 us
  blocking collectives  106 us (46%)
  waiting for transfers between devices  58.3 us (25%)
  starting transfers between devices  28.1 us (12%)
  Pallas kernels  25.1 us (11%)
  local copies, waits for them, and re-layouts  4.53 us (2%)
  matrix products  4.42 us (2%)
  other arithmetic  2.64 us (1%)
    all_to_all x3, blocking collectives, exchange(): return lax.all_to_all(value, axes, split_axis=0, concat_axis=0, tiled=True)  106 us
    ppermute x9, waiting for transfers between devices, shift(): lax.ppermute(value, axis, [(i, (i + amount) % size) for i in range(size)])  34.1 us
    ppermute x11, waiting for transfers between devices, from_places(): return lax.ppermute(value, ('c', 'x'), pairs)  23.1 us
    ppermute x9, starting transfers between devices, shift(): lax.ppermute(value, axis, [(i, (i + amount) % size) for i in range(size)])  12.1 us
    ppermute x11, starting transfers between devices, from_places(): return lax.ppermute(value, ('c', 'x'), pairs)  10.6 us
    pallas_call x1, Pallas kernels, bundle(): pl.pallas_call(bundle_body, out_shape=jax.ShapeDtypeStruct((5 * cut, h),...  6.38 us
    pallas_call x1, Pallas kernels, project(): pl.pallas_call(project_body, out_shape=jax.ShapeDtypeStruct((rows, width)...  5.59 us
    all_to_all x1, starting transfers between devices, exchange(): return lax.all_to_all(value, axes, split_axis=0, concat_axis=0, tiled=True)  5.39 us
  transfers between devices with their start and end apart: 21, of which 14 were waited for; matrix products, arithmetic and copies ran while one was open for 4% of the time, Pallas kernels for 5%

profile of v8, /device:TPU:0, one launch (start us, length us, event | category | flops | bytes accessed | tf_op | source)
XLA Modules:
  0.0 229.0 jit_solution(6505649755978234210)
XLA Ops:
  0.0 5.6 %shard_map.91 = bf16[256,7168]{1,0:T(8,128)(2,1)} custom-call(bf16[256,512]{1,0:T(8,128)(2,1)} %a_ref.1, bf16[512,7168]{1,0:T(8,128)(2,1)} %b_ref.1), custom_call_target="tpu_custom_call" | custom-call | flops 1879048192 | bytes 11272192 | tf_op jit(solution)/shard_map/pallas_call | solution.py:50
  5.6 5.4 %all-to-all-start = ((bf16[4,64,7168]{2,1,0:T(8,128)(2,1)}), bf16[4,64,7168]{2,1,0:T(8,128)(2,1)}, u32[]{:S(2)}, u32[]{:S(2)}) async-start(bf16[4,64,7168]{2,1,0:T(8,128)(2,1)} %bitcast.45), calls=%async_computation | async-start | bytes 7340032 | tf_op jit(solution)/shard_map/all_to_all | solution.py:22
  11.0 2.9 %dynamic-slice_bitcast_fusion = (bf16[256,1792]{1,0:T(8,128)(2,1)S(1)}, bf16[256,1792]{1,0:T(8,128)(2,1)S(1)}, bf16[256,1792]{1,0:T(8,128)(2,1)}) fusion(bf16[1,256,7168]{2,1,0:T(8,128)(2,1)} %d_ref.1, s32[]{:T(128)S(6)} %select_n.53, s32[]{:T(128)S(6)} %select_n.51, s32[]{:T(128)S(6)} %select_n.52), kind=kLoop, calls=%fused_computation.9 | loop fusion | bytes 5505036 | tf_op jit(solution)/shard_map/dynamic_slice | solution.py:273
  13.9 1.5 collective-permute-start.5
  16.0 3.0 %collective-permute-start.1 = (bf16[16,128]{0,1:T(8,128)(2,1)S(1)}, bf16[16,128]{0,1:T(8,128)(2,1)S(1)}, u32[]{:S(2)}, u32[]{:S(2)}) collective-permute-start(bf16[16,128]{0,1:T(8,128)(2,1)S(1)} %fusion.15), channel_id=1, source_target_pairs={{0,2},{1,3},{2,0},{3,1},{4,6},{5,7},{6,4},{7,5},{8,10},{9,11},{10,... | collective-permute-start | bytes 12296 | tf_op jit(solution)/shard_map/ppermute | solution.py:18
  19.0 1.8 collective-permute-start
  21.6 13.0 %collective-permute-done.2 = bf16[16,128]{0,1:T(8,128)(2,1)S(1)} collective-permute-done((bf16[16,128]{0,1:T(8,128)(2,1)S(1)}, bf16[16,128]{0,1:T(8,128)(2,1)S(1)}, u32[]{:S(2)}, u32[]{:S(2)}) %collective-permute-start.2) | collective-permute-done | bytes 4128 | tf_op jit(solution)/shard_map/ppermute | solution.py:18
  34.6 3.9 %collective-permute-done.1 = bf16[16,128]{0,1:T(8,128)(2,1)S(1)} collective-permute-done((bf16[16,128]{0,1:T(8,128)(2,1)S(1)}, bf16[16,128]{0,1:T(8,128)(2,1)S(1)}, u32[]{:S(2)}, u32[]{:S(2)}) %collective-permute-start.1) | collective-permute-done | bytes 4128 | tf_op jit(solution)/shard_map/ppermute | solution.py:18
  39.2 4.1 %shard_map.92 = bf16[3584,512]{1,0:T(8,128)(2,1)} custom-call(s32[2]{0:T(128)} %get-tuple-element.60.at_ref, bf16[1,7168,256]{2,1,0:T(8,128)(2,1)} %g_ref.3, bf16[1,7168,256]{2,1,0:T(8,128)(2,1)} %u_ref.3), custom_call_target="tpu_custom_call" | custom-call | bytes 7340032 | tf_op jit(solution)/shard_map/pallas_call | solution.py:237
  43.4 6.4 %shard_map.93 = bf16[8960,256]{1,0:T(8,128)(2,1)} custom-call(s32[2]{0:T(128)} %get-tuple-element.61.at_ref, bf16[1,7168,256]{2,1,0:T(8,128)(2,1)} %g_ref.3, bf16[1,7168,256]{2,1,0:T(8,128)(2,1)} %u_ref.3, bf16[1,256,7168]{2,1,0:T(8,128)(2,1)} %d_ref.1), custom_call_target="tpu_custom_call" | custom-call | bytes 9175040 | tf_op jit(solution)/shard_map/pallas_call | solution.py:207
  51.4 2.2 collective-permute-done.6.refs_7_
  54.8 3.5 %shard_map.94 = (bf16[64,1792]{1,0:T(8,128)(2,1)S(1)}, bf16[64,1792]{1,0:T(8,128)(2,1)S(1)}, bf16[64,1792]{1,0:T(8,128)(2,1)S(1)}, bf16[64,1792]{1,0:T(8,128)(2,1)S(1)}) custom-call(s32[1]{0:T(128)} %bitcast.at_ref, bf16[4,64,7168]{2,1,0:T(8,128)(2,1)} %all-to-all-done.a_ref, bf16[16,7168]{1,0:T(8,128)(2,1)S(1)} %copy-done), custom_call_target="tpu_custom_call" | custom-call | flops 1835008 | bytes 4587520 | tf_op jit(solution)/shard_map/pallas_call | solution.py:89
  58.3 3.1 %collective-permute-start.7 = (bf16[64,1792]{1,0:T(8,128)(2,1)S(1)}, bf16[64,1792]{1,0:T(8,128)(2,1)S(1)}, u32[]{:S(2)}, u32[]{:S(2)}) collective-permute-start(bf16[64,1792]{1,0:T(8,128)(2,1)S(1)} %get-tuple-element.31), channel_id=1, source_target_pairs={{0,2},{1,3},{2,0},{3,1},{4,6},{5,7},{6,4},{7,5},{8,10},{9,11},{10,... | collective-permute-start | bytes 688136 | tf_op jit(solution)/shard_map/ppermute | solution.py:18
  62.0 2.6 %collective-permute-start.9 = (bf16[64,1792]{1,0:T(8,128)(2,1)S(1)}, bf16[64,1792]{1,0:T(8,128)(2,1)S(1)}, u32[]{:S(2)}, u32[]{:S(2)}) collective-permute-start(bf16[64,1792]{1,0:T(8,128)(2,1)S(1)} %get-tuple-element.33), channel_id=1, source_target_pairs={{0,3},{1,0},{2,1},{3,2},{4,7},{5,4},{6,5},{7,6},{8,11},{9,8},{10,9... | collective-permute-start | bytes 688136 | tf_op jit(solution)/shard_map/ppermute | solution.py:18
  64.7 3.8 %collective-permute-done.7 = bf16[64,1792]{1,0:T(8,128)(2,1)S(1)} collective-permute-done((bf16[64,1792]{1,0:T(8,128)(2,1)S(1)}, bf16[64,1792]{1,0:T(8,128)(2,1)S(1)}, u32[]{:S(2)}, u32[]{:S(2)}) %collective-permute-start.7) | collective-permute-done | bytes 229408 | tf_op jit(solution)/shard_map/ppermute | solution.py:18
  68.4 2.7 %collective-permute-done.8 = bf16[64,1792]{1,0:T(8,128)(2,1)S(1)} collective-permute-done((bf16[64,1792]{1,0:T(8,128)(2,1)S(1)}, bf16[64,1792]{1,0:T(8,128)(2,1)S(1)}, u32[]{:S(2)}, u32[]{:S(2)}) %collective-permute-start.8) | collective-permute-done | bytes 229408 | tf_op jit(solution)/shard_map/ppermute | solution.py:18
  72.5 1.8 collective-permute-start.11
  74.8 3.3 %collective-permute-done.12 = bf16[64,1792]{1,0:T(8,128)(2,1)S(1)} collective-permute-done((bf16[64,1792]{1,0:T(8,128)(2,1)S(1)}, bf16[64,1792]{1,0:T(8,128)(2,1)S(1)}, u32[]{:S(2)}, u32[]{:S(2)}) %collective-permute-start.12) | collective-permute-done | bytes 229408 | tf_op jit(solution)/shard_map/ppermute | solution.py:39
  78.1 3.4 %collective-permute-done.10 = bf16[64,1792]{1,0:T(8,128)(2,1)S(1)} collective-permute-done((bf16[64,1792]{1,0:T(8,128)(2,1)S(1)}, bf16[64,1792]{1,0:T(8,128)(2,1)S(1)}, u32[]{:S(2)}, u32[]{:S(2)}) %collective-permute-start.10) | collective-permute-done | bytes 229408 | tf_op jit(solution)/shard_map/ppermute | solution.py:39
  82.8 61.5 %all_to_all.20 = bf16[16,40,3584]{2,1,0:T(8,128)(2,1)S(1)} all-to-all(bf16[16,40,3584]{2,1,0:T(8,128)(2,1)S(1)} %bitcast.44), channel_id=1, replica_groups=mesh['y'=4,'c'=2,'z'=4,'x'=4] {'y','z'}, dimensions={0} | all-to-all | bytes 9175040 | tf_op jit(solution)/shard_map/all_to_all | solution.py:22
  144.3 3.0 %shard_map.95 = (bf16[640,3584]{1,0:T(8,128)(2,1)S(1)}, f32[640,1]{1,0:T(8,128)S(1)}, bf16[640,512]{1,0:T(8,128)(2,1)S(1)}) custom-call(bf16[640,3584]{1,0:T(8,128)(2,1)S(1)} %bitcast.42, f32[1,3584]{1,0:T(1,128)S(1)} %broadcast_in_dim.50.gain_ref, bf16[8960,256]{1,0:T(8,128)(2,1)S(1)} %collective-permute-done.13.w_ref.refs_5_), custom_call_target="tpu_custom_call" | custom-call | flops 2348810240 | bytes 13500416 | tf_op jit(solution)/shard_map/pallas_call | solution.py:135
  147.5 2.0 collective-permute-start.14
  149.5 2.5 %fusion.24 = f32[640,512]{1,0:T(8,128)S(1)} fusion(bf16[640,3584]{1,0:T(8,128)(2,1)S(1)} %get-tuple-element.44, bf16[3584,512]{1,0:T(8,128)(2,1)S(1)} %copy-done.2), kind=kOutput, calls=%fused_computation.50 | convolution fusion | flops 2348810240 | bytes 9568256 | tf_op jit(solution)/shard_map/dot_general | solution.py:350
  152.1 2.5 %collective-permute-done.15 = f32[640,1]{1,0:T(8,128)S(1)} collective-permute-done((f32[640,1]{1,0:T(8,128)S(1)}, f32[640,1]{1,0:T(8,128)S(1)}, u32[]{:S(2)}, u32[]{:S(2)}) %collective-permute-start.15) | collective-permute-done | bytes 2592 | tf_op jit(solution)/shard_map/ppermute | solution.py:39
  154.8 6.8 %collective-permute-done.14 = bf16[640,512]{1,0:T(8,128)(2,1)S(1)} collective-permute-done((bf16[640,512]{1,0:T(8,128)(2,1)S(1)}, bf16[640,512]{1,0:T(8,128)(2,1)S(1)}, u32[]{:S(2)}, u32[]{:S(2)}) %collective-permute-start.14) | collective-permute-done | bytes 655392 | tf_op jit(solution)/shard_map/ppermute | solution.py:39
  162.2 2.5 %collective-permute-start.17 = (bf16[640,256]{1,0:T(8,128)(2,1)S(1)}, bf16[640,256]{1,0:T(8,128)(2,1)S(1)}, u32[]{:S(2)}, u32[]{:S(2)}) collective-permute-start(bf16[640,256]{1,0:T(8,128)(2,1)S(1)} %fusion.7.refs_0_), channel_id=1, source_target_pairs={{3,0},{2,1},{1,2},{0,3},{17,16},{16,17},{19,18},{18,19},{7,4},{6,5... | collective-permute-start | bytes 983048 | tf_op jit(solution)/shard_map/ppermute | solution.py:39
  165.6 8.7 %collective-permute-done.18.refs_3_ = bf16[640,256]{1,0:T(8,128)(2,1)S(1)} collective-permute-done((bf16[640,256]{1,0:T(8,128)(2,1)S(1)}, bf16[640,256]{1,0:T(8,128)(2,1)S(1)}, u32[]{:S(2)}, u32[]{:S(2)}) %collective-permute-start.18) | collective-permute-done | bytes 327712 | tf_op jit(solution)/shard_map/ppermute | solution.py:18
  174.3 4.8 %collective-permute-done.17.refs_2_ = bf16[640,256]{1,0:T(8,128)(2,1)S(1)} collective-permute-done((bf16[640,256]{1,0:T(8,128)(2,1)S(1)}, bf16[640,256]{1,0:T(8,128)(2,1)S(1)}, u32[]{:S(2)}, u32[]{:S(2)}) %collective-permute-start.17) | collective-permute-done | bytes 327712 | tf_op jit(solution)/shard_map/ppermute | solution.py:39
  179.1 2.5 %shard_map.96 = bf16[640,1792]{1,0:T(8,128)(2,1)S(1)} custom-call(bf16[640,256]{1,0:T(8,128)(2,1)S(1)} %fusion.7.refs_0_, bf16[640,256]{1,0:T(8,128)(2,1)S(1)} %collective-permute-done.16.refs_1_, bf16[640,256]{1,0:T(8,128)(2,1)S(1)} %collective-permute-done.17.refs_2_, bf16[640,256]{1,0:T(8,128)(2,1)S(1)} %collective-permute-done.18.refs_3_, ...), custom_call_target="tpu_custom_call" | custom-call | flops 2348810240 | bytes 7274496 | tf_op jit(solution)/shard_map/pallas_call | solution.py:169
  181.6 34.9 %all_to_all.21 = bf16[16,40,1792]{2,1,0:T(8,128)(2,1)S(1)} all-to-all(bf16[16,40,1792]{2,1,0:T(8,128)(2,1)S(1)} %bitcast.43), channel_id=1, replica_groups=mesh['y'=4,'c'=2,'z'=4,'x'=4] {'y','z'}, dimensions={0} | all-to-all | bytes 4587520 | tf_op jit(solution)/shard_map/all_to_all | solution.py:22
  217.2 1.8 collective-permute-done.19
  219.1 9.3 %all_to_all.22 = bf16[4,16,1792]{2,1,0:T(8,128)(2,1)S(1)} all-to-all(bf16[4,16,1792]{2,1,0:T(8,128)(2,1)S(1)} %bitcast.48), channel_id=1, replica_groups=mesh['y'=4,'c'=2,'z'=4,'x'=4] {'x'}, dimensions={0} | all-to-all | bytes 458752 | tf_op jit(solution)/shard_map/all_to_all | solution.py:22
  (68 shorter events, 11.8 us)
Async XLA Ops:
  5.6 49.2 %all-to-all-start = ((bf16[4,64,7168]{2,1,0:T(8,128)(2,1)}), bf16[4,64,7168]{2,1,0:T(8,128)(2,1)}, u32[]{:S(2)}, u32[]{:S(2)}) async-start(bf16[4,64,7168]{2,1,0:T(8,128)(2,1)} %bitcast.45), calls=%async_computation | async-start | bytes 7340032 | tf_op jit(solution)/shard_map/all_to_all | solution.py:22
  11.0 4.4 %copy-start.4 = (s32[16,8]{0,1:T(8,128)S(1)}, s32[16,8]{0,1:T(8,128)}, u32[]{:S(2)}) copy-start(s32[16,8]{0,1:T(8,128)} %param.13) | copy-start | bytes 1540
  11.0 4.4 %copy-start.5 = (bf16[16,8]{0,1:T(8,128)(2,1)S(1)}, bf16[16,8]{0,1:T(8,128)(2,1)}, u32[]{:S(2)}) copy-start(bf16[16,8]{0,1:T(8,128)(2,1)} %param.14) | copy-start | bytes 772
  11.0 10.5 %copy-start.3 = (f32[7168]{0:T(1024)S(1)}, f32[7168]{0:T(1024)}, u32[]{:S(2)}) copy-start(f32[7168]{0:T(1024)} %param.12) | copy-start | bytes 86020
  13.9 24.9 %collective-permute-start.5 = (bf16[256,1792]{1,0:T(8,128)(2,1)S(1)}, bf16[256,1792]{1,0:T(8,128)(2,1)}, u32[]{:S(2)}, u32[]{:S(2)}) collective-permute-start(bf16[256,1792]{1,0:T(8,128)(2,1)S(1)} %get-tuple-element.53), channel_id=1, source_target_pairs={{1,0},{0,1},{3,2},{2,3},{19,16},{18,17},{17,18},{16,19},{5,4},{4,5... | collective-permute-start | bytes 2752520 | tf_op jit(solution)/shard_map/ppermute | solution.py:39
  15.4 19.2 %collective-permute-start.2 = (bf16[16,128]{0,1:T(8,128)(2,1)S(1)}, bf16[16,128]{0,1:T(8,128)(2,1)S(1)}, u32[]{:S(2)}, u32[]{:S(2)}) collective-permute-start(bf16[16,128]{0,1:T(8,128)(2,1)S(1)} %fusion.15), channel_id=1, source_target_pairs={{0,1},{1,2},{2,3},{3,0},{4,5},{5,6},{6,7},{7,4},{8,9},{9,10},{10,1... | collective-permute-start | bytes 12296 | tf_op jit(solution)/shard_map/ppermute | solution.py:18
  16.0 22.6 %collective-permute-start.1 = (bf16[16,128]{0,1:T(8,128)(2,1)S(1)}, bf16[16,128]{0,1:T(8,128)(2,1)S(1)}, u32[]{:S(2)}, u32[]{:S(2)}) collective-permute-start(bf16[16,128]{0,1:T(8,128)(2,1)S(1)} %fusion.15), channel_id=1, source_target_pairs={{0,2},{1,3},{2,0},{3,1},{4,6},{5,7},{6,4},{7,5},{8,10},{9,11},{10,... | collective-permute-start | bytes 12296 | tf_op jit(solution)/shard_map/ppermute | solution.py:18
  19.0 19.6 %collective-permute-start = (bf16[16,128]{0,1:T(8,128)(2,1)S(1)}, bf16[16,128]{0,1:T(8,128)(2,1)S(1)}, u32[]{:S(2)}, u32[]{:S(2)}) collective-permute-start(bf16[16,128]{0,1:T(8,128)(2,1)S(1)} %fusion.15), channel_id=1, source_target_pairs={{0,3},{1,0},{2,1},{3,2},{4,7},{5,4},{6,5},{7,6},{8,11},{9,8},{10,9... | collective-permute-start | bytes 12296 | tf_op jit(solution)/shard_map/ppermute | solution.py:18
  20.8 30.6 %collective-permute-start.4 = (bf16[256,1792]{1,0:T(8,128)(2,1)}, bf16[256,1792]{1,0:T(8,128)(2,1)S(1)}, u32[]{:S(2)}, u32[]{:S(2)}) collective-permute-start(bf16[256,1792]{1,0:T(8,128)(2,1)} %get-tuple-element.55), channel_id=1, source_target_pairs={{3,0},{2,1},{1,2},{0,3},{17,16},{16,17},{19,18},{18,19},{7,4},{6,5... | collective-permute-start | bytes 2752520 | tf_op jit(solution)/shard_map/ppermute | solution.py:39
  38.7 14.9 %collective-permute-start.6 = (bf16[256,1792]{1,0:T(8,128)(2,1)}, bf16[256,1792]{1,0:T(8,128)(2,1)S(1)}, u32[]{:S(2)}, u32[]{:S(2)}) collective-permute-start(bf16[256,1792]{1,0:T(8,128)(2,1)} %collective-permute-done.5), channel_id=1, source_target_pairs={{3,0},{2,1},{1,2},{0,3},{17,16},{16,17},{19,18},{18,19},{7,4},{6,5... | collective-permute-start | bytes 2752520 | tf_op jit(solution)/shard_map/ppermute | solution.py:39
  38.9 10.8 %collective-permute-start.3 = (bf16[64,128]{0,1:T(8,128)(2,1)S(1)}, bf16[64,128]{0,1:T(8,128)(2,1)S(1)}, u32[]{:S(2)}, u32[]{:S(2)}) collective-permute-start(bf16[64,128]{0,1:T(8,128)(2,1)S(1)} %constant_dynamic-slice_fusion), channel_id=1, source_target_pairs={{0,16},{16,0},{1,17},{17,1},{2,18},{18,2},{3,19},{19,3},{4,20},{20... | collective-permute-start | bytes 49160 | tf_op jit(solution)/shard_map/ppermute | solution.py:18
  43.4 11.4 %copy-start = (bf16[16,7168]{1,0:T(8,128)(2,1)S(1)}, bf16[16,7168]{1,0:T(8,128)(2,1)}, u32[]{:S(2)}) copy-start(bf16[16,7168]{1,0:T(8,128)(2,1)} %r_ref.1) | copy-start | bytes 688132
  54.8 26.7 %copy-start.1 = (bf16[8960,256]{1,0:T(8,128)(2,1)S(1)}, bf16[8960,256]{1,0:T(8,128)(2,1)}, u32[]{:S(2)}) copy-start(bf16[8960,256]{1,0:T(8,128)(2,1)} %shard_map.93) | copy-start | bytes 13762564
  58.3 10.1 %collective-permute-start.7 = (bf16[64,1792]{1,0:T(8,128)(2,1)S(1)}, bf16[64,1792]{1,0:T(8,128)(2,1)S(1)}, u32[]{:S(2)}, u32[]{:S(2)}) collective-permute-start(bf16[64,1792]{1,0:T(8,128)(2,1)S(1)} %get-tuple-element.31), channel_id=1, source_target_pairs={{0,2},{1,3},{2,0},{3,1},{4,6},{5,7},{6,4},{7,5},{8,10},{9,11},{10,... | collective-permute-start | bytes 688136 | tf_op jit(solution)/shard_map/ppermute | solution.py:18
  61.4 9.8 %collective-permute-start.8 = (bf16[64,1792]{1,0:T(8,128)(2,1)S(1)}, bf16[64,1792]{1,0:T(8,128)(2,1)S(1)}, u32[]{:S(2)}, u32[]{:S(2)}) collective-permute-start(bf16[64,1792]{1,0:T(8,128)(2,1)S(1)} %get-tuple-element.32), channel_id=1, source_target_pairs={{0,1},{1,2},{2,3},{3,0},{4,5},{5,6},{6,7},{7,4},{8,9},{9,10},{10,1... | collective-permute-start | bytes 688136 | tf_op jit(solution)/shard_map/ppermute | solution.py:18
  62.0 9.2 %collective-permute-start.9 = (bf16[64,1792]{1,0:T(8,128)(2,1)S(1)}, bf16[64,1792]{1,0:T(8,128)(2,1)S(1)}, u32[]{:S(2)}, u32[]{:S(2)}) collective-permute-start(bf16[64,1792]{1,0:T(8,128)(2,1)S(1)} %get-tuple-element.33), channel_id=1, source_target_pairs={{0,3},{1,0},{2,1},{3,2},{4,7},{5,4},{6,5},{7,6},{8,11},{9,8},{10,9... | collective-permute-start | bytes 688136 | tf_op jit(solution)/shard_map/ppermute | solution.py:18
  71.4 6.7 %collective-permute-start.12 = (bf16[64,1792]{1,0:T(8,128)(2,1)S(1)}, bf16[64,1792]{1,0:T(8,128)(2,1)S(1)}, u32[]{:S(2)}, u32[]{:S(2)}) collective-permute-start(bf16[64,1792]{1,0:T(8,128)(2,1)S(1)} %add_convert_fusion), channel_id=1, source_target_pairs={{19,0},{18,1},{17,2},{16,3},{1,16},{0,17},{3,18},{2,19},{23,4},{22... | collective-permute-start | bytes 688136 | tf_op jit(solution)/shard_map/ppermute | solution.py:39
  72.5 5.6 %collective-permute-start.11 = (bf16[64,1792]{1,0:T(8,128)(2,1)S(1)}, bf16[64,1792]{1,0:T(8,128)(2,1)S(1)}, u32[]{:S(2)}, u32[]{:S(2)}) collective-permute-start(bf16[64,1792]{1,0:T(8,128)(2,1)S(1)} %add_convert_fusion), channel_id=1, source_target_pairs={{16,0},{17,1},{18,2},{19,3},{0,16},{1,17},{2,18},{3,19},{20,4},{21... | collective-permute-start | bytes 688136 | tf_op jit(solution)/shard_map/ppermute | solution.py:39
  74.2 7.2 %collective-permute-start.10 = (bf16[64,1792]{1,0:T(8,128)(2,1)S(1)}, bf16[64,1792]{1,0:T(8,128)(2,1)S(1)}, u32[]{:S(2)}, u32[]{:S(2)}) collective-permute-start(bf16[64,1792]{1,0:T(8,128)(2,1)S(1)} %add_convert_fusion), channel_id=1, source_target_pairs={{3,0},{2,1},{1,2},{0,3},{17,16},{16,17},{19,18},{18,19},{7,4},{6,5... | collective-permute-start | bytes 688136 | tf_op jit(solution)/shard_map/ppermute | solution.py:39
  81.5 62.9 %collective-permute-start.13 = (bf16[8960,256]{1,0:T(8,128)(2,1)S(1)}, bf16[8960,256]{1,0:T(8,128)(2,1)S(1)}, u32[]{:S(2)}, u32[]{:S(2)}) collective-permute-start(bf16[8960,256]{1,0:T(8,128)(2,1)S(1)} %copy-done.1), channel_id=1, source_target_pairs={{1,0},{0,1},{3,2},{2,3},{19,16},{18,17},{17,18},{16,19},{5,4},{4,5... | collective-permute-start | bytes 13762568 | tf_op jit(solution)/shard_map/ppermute | solution.py:39
  144.3 5.2 %copy-start.2 = (bf16[3584,512]{1,0:T(8,128)(2,1)S(1)}, bf16[3584,512]{1,0:T(8,128)(2,1)}, u32[]{:S(2)}) copy-start(bf16[3584,512]{1,0:T(8,128)(2,1)} %shard_map.92) | copy-start | bytes 11010052
  147.3 7.3 %collective-permute-start.15 = (f32[640,1]{1,0:T(8,128)S(1)}, f32[640,1]{1,0:T(8,128)S(1)}, u32[]{:S(2)}, u32[]{:S(2)}) collective-permute-start(f32[640,1]{1,0:T(8,128)S(1)} %get-tuple-element.49), channel_id=1, source_target_pairs={{1,0},{0,1},{3,2},{2,3},{19,16},{18,17},{17,18},{16,19},{5,4},{4,5... | collective-permute-start | bytes 7688 | tf_op jit(solution)/shard_map/ppermute | solution.py:39
  147.5 14.1 %collective-permute-start.14 = (bf16[640,512]{1,0:T(8,128)(2,1)S(1)}, bf16[640,512]{1,0:T(8,128)(2,1)S(1)}, u32[]{:S(2)}, u32[]{:S(2)}) collective-permute-start(bf16[640,512]{1,0:T(8,128)(2,1)S(1)} %get-tuple-element.46), channel_id=1, source_target_pairs={{1,0},{0,1},{3,2},{2,3},{19,16},{18,17},{17,18},{16,19},{5,4},{4,5... | collective-permute-start | bytes 1966088 | tf_op jit(solution)/shard_map/ppermute | solution.py:39
  162.0 12.2 %collective-permute-start.18 = (bf16[640,256]{1,0:T(8,128)(2,1)S(1)}, bf16[640,256]{1,0:T(8,128)(2,1)S(1)}, u32[]{:S(2)}, u32[]{:S(2)}) collective-permute-start(bf16[640,256]{1,0:T(8,128)(2,1)S(1)} %fusion.7.refs_0_), channel_id=1, source_target_pairs={{0,2},{1,3},{2,0},{3,1},{4,6},{5,7},{6,4},{7,5},{8,10},{9,11},{10,... | collective-permute-start | bytes 983048 | tf_op jit(solution)/shard_map/ppermute | solution.py:18
  162.2 16.8 %collective-permute-start.17 = (bf16[640,256]{1,0:T(8,128)(2,1)S(1)}, bf16[640,256]{1,0:T(8,128)(2,1)S(1)}, u32[]{:S(2)}, u32[]{:S(2)}) collective-permute-start(bf16[640,256]{1,0:T(8,128)(2,1)S(1)} %fusion.7.refs_0_), channel_id=1, source_target_pairs={{3,0},{2,1},{1,2},{0,3},{17,16},{16,17},{19,18},{18,19},{7,4},{6,5... | collective-permute-start | bytes 983048 | tf_op jit(solution)/shard_map/ppermute | solution.py:39
  164.8 14.3 %collective-permute-start.16 = (bf16[640,256]{1,0:T(8,128)(2,1)S(1)}, bf16[640,256]{1,0:T(8,128)(2,1)S(1)}, u32[]{:S(2)}, u32[]{:S(2)}) collective-permute-start(bf16[640,256]{1,0:T(8,128)(2,1)S(1)} %fusion.7.refs_0_), channel_id=1, source_target_pairs={{1,0},{0,1},{3,2},{2,3},{19,16},{18,17},{17,18},{16,19},{5,4},{4,5... | collective-permute-start | bytes 983048 | tf_op jit(solution)/shard_map/ppermute | solution.py:39
  217.1 1.9 collective-permute-start.19

commit v9 on v8

--- a/solution.py
+++ b/solution.py
@@ -363,8 +363,14 @@
     )
     mixture = mixture[:tokens_core] + shift(mixture[tokens_core:], "c", 1)
     out = (hidden_wide + mixture).astype(BF16)
-    out = exchange(out.reshape(nx, rows_here, quarter), "x")
-    return out.transpose(1, 0, 2).reshape(rows_here, width)
+    came = []
+    for k in range(nx):
+        at = lax.rem(x + k, nx) * rows_here
+        piece = lax.dynamic_slice(out, (at, jnp.int32(0)), (rows_here, quarter))
+        came.append(piece if k == 0 else shift(piece, "x", k))
+    ring = [came[(nx - m) % nx] for m in range(nx)]
+    ring = jnp.concatenate(ring + ring[:-1], axis=1)
+    return lax.dynamic_slice(ring, (jnp.int32(0), lax.rem(nx - x, nx) * quarter), (rows_here, width))
 
 
 def solution(mesh):

time: 230 us -> 227 us (0.987)
  blocking collectives: 106 us -> 95.4 us
  starting transfers between devices: 28.1 us -> 33 us
  waiting for transfers between devices: 58.3 us -> 61.6 us
    all_to_all x3 -> x2, blocking collectives: 106 us -> 95.4 us  [exchange(): return lax.all_to_all(value, axes, split_axis=0, concat_axis=0, tiled=True)]
    ppermute x9 -> x12, starting transfers between devices: 12.1 us -> 15.5 us  [shift(): lax.ppermute(value, axis, [(i, (i + amount) % size) for i in range(size)])]
    ppermute x9 -> x12, waiting for transfers between devices: 34.1 us -> 36.1 us  [shift(): lax.ppermute(value, axis, [(i, (i + amount) % size) for i in range(size)])]
  transfers between devices with their start and end apart: 21 -> 24, of which waited for: 14 -> 17; matrix products, arithmetic and copies ran while one was open for 4% -> 4% of each run, Pallas kernels for 5% -> 5%
where the time goes in v9:
time: 227 us
  blocking collectives  95.4 us (42%)
  waiting for transfers between devices  61.6 us (27%)
  starting transfers between devices  33 us (15%)
  Pallas kernels  25.1 us (11%)
  local copies, waits for them, and re-layouts  4.59 us (2%)
  matrix products  4.42 us (2%)
  other arithmetic  2.63 us (1%)
    all_to_all x2, blocking collectives, exchange(): return lax.all_to_all(value, axes, split_axis=0, concat_axis=0, tiled=True)  95.4 us
    ppermute x12, waiting for transfers between devices, shift(): lax.ppermute(value, axis, [(i, (i + amount) % size) for i in range(size)])  36.1 us
    ppermute x11, waiting for transfers between devices, from_places(): return lax.ppermute(value, ('c', 'x'), pairs)  23.8 us
    ppermute x12, starting transfers between devices, shift(): lax.ppermute(value, axis, [(i, (i + amount) % size) for i in range(size)])  15.5 us
    ppermute x11, starting transfers between devices, from_places(): return lax.ppermute(value, ('c', 'x'), pairs)  12.1 us
    pallas_call x1, Pallas kernels, bundle(): pl.pallas_call(bundle_body, out_shape=jax.ShapeDtypeStruct((5 * cut, h),...  6.26 us
    pallas_call x1, Pallas kernels, project(): pl.pallas_call(project_body, out_shape=jax.ShapeDtypeStruct((rows, width)...  5.62 us
    all_to_all x1, starting transfers between devices, exchange(): return lax.all_to_all(value, axes, split_axis=0, concat_axis=0, tiled=True)  5.39 us
  transfers between devices with their start and end apart: 24, of which 17 were waited for; matrix products, arithmetic and copies ran while one was open for 4% of the time, Pallas kernels for 5%

profile of v9, /device:TPU:0, one launch (start us, length us, event | category | flops | bytes accessed | tf_op | source)
XLA Modules:
  0.0 227.1 jit_solution(93338756895423604)
XLA Ops:
  0.0 5.6 %shard_map.91 = bf16[256,7168]{1,0:T(8,128)(2,1)} custom-call(bf16[256,512]{1,0:T(8,128)(2,1)} %a_ref.1, bf16[512,7168]{1,0:T(8,128)(2,1)} %b_ref.1), custom_call_target="tpu_custom_call" | custom-call | flops 1879048192 | bytes 11272192 | tf_op jit(solution)/shard_map/pallas_call | solution.py:50
  5.6 5.4 %all-to-all-start = ((bf16[4,64,7168]{2,1,0:T(8,128)(2,1)}), bf16[4,64,7168]{2,1,0:T(8,128)(2,1)}, u32[]{:S(2)}, u32[]{:S(2)}) async-start(bf16[4,64,7168]{2,1,0:T(8,128)(2,1)} %bitcast.41), calls=%async_computation | async-start | bytes 7340032 | tf_op jit(solution)/shard_map/all_to_all | solution.py:22
  11.0 2.9 %dynamic-slice_bitcast_fusion = (bf16[256,1792]{1,0:T(8,128)(2,1)S(1)}, bf16[256,1792]{1,0:T(8,128)(2,1)S(1)}, bf16[256,1792]{1,0:T(8,128)(2,1)}) fusion(bf16[1,256,7168]{2,1,0:T(8,128)(2,1)} %d_ref.1, s32[]{:T(128)S(6)} %select_n.68, s32[]{:T(128)S(6)} %select_n.66, s32[]{:T(128)S(6)} %select_n.67), kind=kLoop, calls=%fused_computation.9 | loop fusion | bytes 5505036 | tf_op jit(solution)/shard_map/dynamic_slice | solution.py:273
  15.4 2.2 collective-permute-start
  19.6 1.9 collective-permute-start.4
  22.3 13.8 %collective-permute-done = bf16[16,128]{0,1:T(8,128)(2,1)S(1)} collective-permute-done((bf16[16,128]{0,1:T(8,128)(2,1)S(1)}, bf16[16,128]{0,1:T(8,128)(2,1)S(1)}, u32[]{:S(2)}, u32[]{:S(2)}) %collective-permute-start) | collective-permute-done | bytes 4128 | tf_op jit(solution)/shard_map/ppermute | solution.py:18
  36.1 2.1 collective-permute-done.1
  40.1 6.3 %shard_map.93 = bf16[8960,256]{1,0:T(8,128)(2,1)} custom-call(s32[2]{0:T(128)} %get-tuple-element.65.at_ref, bf16[1,7168,256]{2,1,0:T(8,128)(2,1)} %g_ref.3, bf16[1,7168,256]{2,1,0:T(8,128)(2,1)} %u_ref.3, bf16[1,256,7168]{2,1,0:T(8,128)(2,1)} %d_ref.1), custom_call_target="tpu_custom_call" | custom-call | bytes 9175040 | tf_op jit(solution)/shard_map/pallas_call | solution.py:207
  46.3 4.2 %shard_map.92 = bf16[3584,512]{1,0:T(8,128)(2,1)} custom-call(s32[2]{0:T(128)} %get-tuple-element.64.at_ref, bf16[1,7168,256]{2,1,0:T(8,128)(2,1)} %g_ref.3, bf16[1,7168,256]{2,1,0:T(8,128)(2,1)} %u_ref.3), custom_call_target="tpu_custom_call" | custom-call | bytes 7340032 | tf_op jit(solution)/shard_map/pallas_call | solution.py:237
  54.8 3.5 %shard_map.94 = (bf16[64,1792]{1,0:T(8,128)(2,1)S(1)}, bf16[64,1792]{1,0:T(8,128)(2,1)S(1)}, bf16[64,1792]{1,0:T(8,128)(2,1)S(1)}, bf16[64,1792]{1,0:T(8,128)(2,1)S(1)}) custom-call(s32[1]{0:T(128)} %bitcast.at_ref, bf16[4,64,7168]{2,1,0:T(8,128)(2,1)} %all-to-all-done.a_ref, bf16[16,7168]{1,0:T(8,128)(2,1)S(1)} %copy-done), custom_call_target="tpu_custom_call" | custom-call | flops 1835008 | bytes 4587520 | tf_op jit(solution)/shard_map/pallas_call | solution.py:89
  58.4 3.1 %collective-permute-start.7 = (bf16[64,1792]{1,0:T(8,128)(2,1)S(1)}, bf16[64,1792]{1,0:T(8,128)(2,1)S(1)}, u32[]{:S(2)}, u32[]{:S(2)}) collective-permute-start(bf16[64,1792]{1,0:T(8,128)(2,1)S(1)} %get-tuple-element.31), channel_id=1, source_target_pairs={{0,2},{1,3},{2,0},{3,1},{4,6},{5,7},{6,4},{7,5},{8,10},{9,11},{10,... | collective-permute-start | bytes 688136 | tf_op jit(solution)/shard_map/ppermute | solution.py:18
  62.1 2.6 %collective-permute-start.9 = (bf16[64,1792]{1,0:T(8,128)(2,1)S(1)}, bf16[64,1792]{1,0:T(8,128)(2,1)S(1)}, u32[]{:S(2)}, u32[]{:S(2)}) collective-permute-start(bf16[64,1792]{1,0:T(8,128)(2,1)S(1)} %get-tuple-element.33), channel_id=1, source_target_pairs={{0,3},{1,0},{2,1},{3,2},{4,7},{5,4},{6,5},{7,6},{8,11},{9,8},{10,9... | collective-permute-start | bytes 688136 | tf_op jit(solution)/shard_map/ppermute | solution.py:18
  64.7 3.8 %collective-permute-done.7 = bf16[64,1792]{1,0:T(8,128)(2,1)S(1)} collective-permute-done((bf16[64,1792]{1,0:T(8,128)(2,1)S(1)}, bf16[64,1792]{1,0:T(8,128)(2,1)S(1)}, u32[]{:S(2)}, u32[]{:S(2)}) %collective-permute-start.7) | collective-permute-done | bytes 229408 | tf_op jit(solution)/shard_map/ppermute | solution.py:18
  68.5 2.7 %collective-permute-done.8 = bf16[64,1792]{1,0:T(8,128)(2,1)S(1)} collective-permute-done((bf16[64,1792]{1,0:T(8,128)(2,1)S(1)}, bf16[64,1792]{1,0:T(8,128)(2,1)S(1)}, u32[]{:S(2)}, u32[]{:S(2)}) %collective-permute-start.8) | collective-permute-done | bytes 229408 | tf_op jit(solution)/shard_map/ppermute | solution.py:18
  71.4 2.8 %collective-permute-start.10 = (bf16[64,1792]{1,0:T(8,128)(2,1)S(1)}, bf16[64,1792]{1,0:T(8,128)(2,1)S(1)}, u32[]{:S(2)}, u32[]{:S(2)}) collective-permute-start(bf16[64,1792]{1,0:T(8,128)(2,1)S(1)} %add_convert_fusion), channel_id=1, source_target_pairs={{3,0},{2,1},{1,2},{0,3},{17,16},{16,17},{19,18},{18,19},{7,4},{6,5... | collective-permute-start | bytes 688136 | tf_op jit(solution)/shard_map/ppermute | solution.py:39
  74.2 6.0 %collective-permute-done.10 = bf16[64,1792]{1,0:T(8,128)(2,1)S(1)} collective-permute-done((bf16[64,1792]{1,0:T(8,128)(2,1)S(1)}, bf16[64,1792]{1,0:T(8,128)(2,1)S(1)}, u32[]{:S(2)}, u32[]{:S(2)}) %collective-permute-start.10) | collective-permute-done | bytes 229408 | tf_op jit(solution)/shard_map/ppermute | solution.py:39
  82.9 60.5 %all_to_all.15 = bf16[16,40,3584]{2,1,0:T(8,128)(2,1)S(1)} all-to-all(bf16[16,40,3584]{2,1,0:T(8,128)(2,1)S(1)} %bitcast.40), channel_id=1, replica_groups=mesh['y'=4,'c'=2,'z'=4,'x'=4] {'y','z'}, dimensions={0} | all-to-all | bytes 9175040 | tf_op jit(solution)/shard_map/all_to_all | solution.py:22
  143.4 3.0 %shard_map.95 = (bf16[640,3584]{1,0:T(8,128)(2,1)S(1)}, f32[640,1]{1,0:T(8,128)S(1)}, bf16[640,512]{1,0:T(8,128)(2,1)S(1)}) custom-call(bf16[640,3584]{1,0:T(8,128)(2,1)S(1)} %bitcast.38, f32[1,3584]{1,0:T(1,128)S(1)} %broadcast_in_dim.50.gain_ref, bf16[8960,256]{1,0:T(8,128)(2,1)S(1)} %collective-permute-done.13.w_ref.refs_5_), custom_call_target="tpu_custom_call" | custom-call | flops 2348810240 | bytes 13500416 | tf_op jit(solution)/shard_map/pallas_call | solution.py:135
  146.5 2.0 collective-permute-start.14
  148.5 2.5 %fusion.24 = f32[640,512]{1,0:T(8,128)S(1)} fusion(bf16[640,3584]{1,0:T(8,128)(2,1)S(1)} %get-tuple-element.44, bf16[3584,512]{1,0:T(8,128)(2,1)S(1)} %copy-done.2), kind=kOutput, calls=%fused_computation.61 | convolution fusion | flops 2348810240 | bytes 9568256 | tf_op jit(solution)/shard_map/dot_general | solution.py:350
  151.1 2.5 %collective-permute-done.15 = f32[640,1]{1,0:T(8,128)S(1)} collective-permute-done((f32[640,1]{1,0:T(8,128)S(1)}, f32[640,1]{1,0:T(8,128)S(1)}, u32[]{:S(2)}, u32[]{:S(2)}) %collective-permute-start.15) | collective-permute-done | bytes 2592 | tf_op jit(solution)/shard_map/ppermute | solution.py:39
  153.8 6.8 %collective-permute-done.14 = bf16[640,512]{1,0:T(8,128)(2,1)S(1)} collective-permute-done((bf16[640,512]{1,0:T(8,128)(2,1)S(1)}, bf16[640,512]{1,0:T(8,128)(2,1)S(1)}, u32[]{:S(2)}, u32[]{:S(2)}) %collective-permute-start.14) | collective-permute-done | bytes 655392 | tf_op jit(solution)/shard_map/ppermute | solution.py:39
  161.1 1.9 collective-permute-start.17
  163.0 2.1 collective-permute-start.18
  165.2 6.5 %collective-permute-done.16.refs_1_ = bf16[640,256]{1,0:T(8,128)(2,1)S(1)} collective-permute-done((bf16[640,256]{1,0:T(8,128)(2,1)S(1)}, bf16[640,256]{1,0:T(8,128)(2,1)S(1)}, u32[]{:S(2)}, u32[]{:S(2)}) %collective-permute-start.16) | collective-permute-done | bytes 327712 | tf_op jit(solution)/shard_map/ppermute | solution.py:39
  171.7 6.6 %collective-permute-done.18.refs_3_ = bf16[640,256]{1,0:T(8,128)(2,1)S(1)} collective-permute-done((bf16[640,256]{1,0:T(8,128)(2,1)S(1)}, bf16[640,256]{1,0:T(8,128)(2,1)S(1)}, u32[]{:S(2)}, u32[]{:S(2)}) %collective-permute-start.18) | collective-permute-done | bytes 327712 | tf_op jit(solution)/shard_map/ppermute | solution.py:18
  178.3 2.5 %shard_map.96 = bf16[640,1792]{1,0:T(8,128)(2,1)S(1)} custom-call(bf16[640,256]{1,0:T(8,128)(2,1)S(1)} %fusion.7.refs_0_, bf16[640,256]{1,0:T(8,128)(2,1)S(1)} %collective-permute-done.16.refs_1_, bf16[640,256]{1,0:T(8,128)(2,1)S(1)} %collective-permute-done.17.refs_2_, bf16[640,256]{1,0:T(8,128)(2,1)S(1)} %collective-permute-done.18.refs_3_, ...), custom_call_target="tpu_custom_call" | custom-call | flops 2348810240 | bytes 7274496 | tf_op jit(solution)/shard_map/pallas_call | solution.py:169
  180.9 34.9 %all_to_all.16 = bf16[16,40,1792]{2,1,0:T(8,128)(2,1)S(1)} all-to-all(bf16[16,40,1792]{2,1,0:T(8,128)(2,1)S(1)} %bitcast.39), channel_id=1, replica_groups=mesh['y'=4,'c'=2,'z'=4,'x'=4] {'y','z'}, dimensions={0} | all-to-all | bytes 4587520 | tf_op jit(solution)/shard_map/all_to_all | solution.py:22
  216.5 1.8 collective-permute-done.19
  218.3 1.7 collective-permute-start.20
  221.0 2.0 collective-permute-done.20
  223.0 3.0 %collective-permute-done.21 = bf16[16,1792]{1,0:T(8,128)(2,1)S(1)} collective-permute-done((bf16[16,1792]{1,0:T(8,128)(2,1)S(1)}, bf16[16,1792]{1,0:T(8,128)(2,1)S(1)}, u32[]{:S(2)}, u32[]{:S(2)}) %collective-permute-start.21) | collective-permute-done | bytes 57376 | tf_op jit(solution)/shard_map/ppermute | solution.py:18
  (80 shorter events, 17.6 us)
Async XLA Ops:
  5.6 49.2 %all-to-all-start = ((bf16[4,64,7168]{2,1,0:T(8,128)(2,1)}), bf16[4,64,7168]{2,1,0:T(8,128)(2,1)}, u32[]{:S(2)}, u32[]{:S(2)}) async-start(bf16[4,64,7168]{2,1,0:T(8,128)(2,1)} %bitcast.41), calls=%async_computation | async-start | bytes 7340032 | tf_op jit(solution)/shard_map/all_to_all | solution.py:22
  11.0 4.4 %copy-start.4 = (s32[16,8]{0,1:T(8,128)S(1)}, s32[16,8]{0,1:T(8,128)}, u32[]{:S(2)}) copy-start(s32[16,8]{0,1:T(8,128)} %param.13) | copy-start | bytes 1540
  11.0 4.4 %copy-start.5 = (bf16[16,8]{0,1:T(8,128)(2,1)S(1)}, bf16[16,8]{0,1:T(8,128)(2,1)}, u32[]{:S(2)}) copy-start(bf16[16,8]{0,1:T(8,128)(2,1)} %param.14) | copy-start | bytes 772
  11.0 11.1 %copy-start.3 = (f32[7168]{0:T(1024)S(1)}, f32[7168]{0:T(1024)}, u32[]{:S(2)}) copy-start(f32[7168]{0:T(1024)} %param.12) | copy-start | bytes 86020
  13.9 24.4 %collective-permute-start.5 = (bf16[256,1792]{1,0:T(8,128)(2,1)S(1)}, bf16[256,1792]{1,0:T(8,128)(2,1)}, u32[]{:S(2)}, u32[]{:S(2)}) collective-permute-start(bf16[256,1792]{1,0:T(8,128)(2,1)S(1)} %get-tuple-element.53), channel_id=1, source_target_pairs={{1,0},{0,1},{3,2},{2,3},{19,16},{18,17},{17,18},{16,19},{5,4},{4,5... | collective-permute-start | bytes 2752520 | tf_op jit(solution)/shard_map/ppermute | solution.py:39
  15.4 20.6 %collective-permute-start = (bf16[16,128]{0,1:T(8,128)(2,1)S(1)}, bf16[16,128]{0,1:T(8,128)(2,1)S(1)}, u32[]{:S(2)}, u32[]{:S(2)}) collective-permute-start(bf16[16,128]{0,1:T(8,128)(2,1)S(1)} %fusion.15), channel_id=1, source_target_pairs={{0,3},{1,0},{2,1},{3,2},{4,7},{5,4},{6,5},{7,6},{8,11},{9,8},{10,9... | collective-permute-start | bytes 12296 | tf_op jit(solution)/shard_map/ppermute | solution.py:18
  17.6 20.5 %collective-permute-start.1 = (bf16[16,128]{0,1:T(8,128)(2,1)S(1)}, bf16[16,128]{0,1:T(8,128)(2,1)S(1)}, u32[]{:S(2)}, u32[]{:S(2)}) collective-permute-start(bf16[16,128]{0,1:T(8,128)(2,1)S(1)} %fusion.15), channel_id=1, source_target_pairs={{0,2},{1,3},{2,0},{3,1},{4,6},{5,7},{6,4},{7,5},{8,10},{9,11},{10,... | collective-permute-start | bytes 12296 | tf_op jit(solution)/shard_map/ppermute | solution.py:18
  18.3 19.8 %collective-permute-start.2 = (bf16[16,128]{0,1:T(8,128)(2,1)S(1)}, bf16[16,128]{0,1:T(8,128)(2,1)S(1)}, u32[]{:S(2)}, u32[]{:S(2)}) collective-permute-start(bf16[16,128]{0,1:T(8,128)(2,1)S(1)} %fusion.15), channel_id=1, source_target_pairs={{0,1},{1,2},{2,3},{3,0},{4,5},{5,6},{6,7},{7,4},{8,9},{9,10},{10,1... | collective-permute-start | bytes 12296 | tf_op jit(solution)/shard_map/ppermute | solution.py:18
  19.6 32.6 %collective-permute-start.4 = (bf16[256,1792]{1,0:T(8,128)(2,1)}, bf16[256,1792]{1,0:T(8,128)(2,1)S(1)}, u32[]{:S(2)}, u32[]{:S(2)}) collective-permute-start(bf16[256,1792]{1,0:T(8,128)(2,1)} %get-tuple-element.55), channel_id=1, source_target_pairs={{3,0},{2,1},{1,2},{0,3},{17,16},{16,17},{19,18},{18,19},{7,4},{6,5... | collective-permute-start | bytes 2752520 | tf_op jit(solution)/shard_map/ppermute | solution.py:39
  38.3 14.9 %collective-permute-start.6 = (bf16[256,1792]{1,0:T(8,128)(2,1)}, bf16[256,1792]{1,0:T(8,128)(2,1)S(1)}, u32[]{:S(2)}, u32[]{:S(2)}) collective-permute-start(bf16[256,1792]{1,0:T(8,128)(2,1)} %collective-permute-done.5), channel_id=1, source_target_pairs={{3,0},{2,1},{1,2},{0,3},{17,16},{16,17},{19,18},{18,19},{7,4},{6,5... | collective-permute-start | bytes 2752520 | tf_op jit(solution)/shard_map/ppermute | solution.py:39
  39.8 10.8 %collective-permute-start.3 = (bf16[64,128]{0,1:T(8,128)(2,1)S(1)}, bf16[64,128]{0,1:T(8,128)(2,1)S(1)}, u32[]{:S(2)}, u32[]{:S(2)}) collective-permute-start(bf16[64,128]{0,1:T(8,128)(2,1)S(1)} %constant_dynamic-slice_fusion.4), channel_id=1, source_target_pairs={{0,16},{16,0},{1,17},{17,1},{2,18},{18,2},{3,19},{19,3},{4,20},{20... | collective-permute-start | bytes 49160 | tf_op jit(solution)/shard_map/ppermute | solution.py:18
  46.3 8.5 %copy-start = (bf16[16,7168]{1,0:T(8,128)(2,1)S(1)}, bf16[16,7168]{1,0:T(8,128)(2,1)}, u32[]{:S(2)}) copy-start(bf16[16,7168]{1,0:T(8,128)(2,1)} %r_ref.1) | copy-start | bytes 688132
  54.8 26.3 %copy-start.1 = (bf16[8960,256]{1,0:T(8,128)(2,1)S(1)}, bf16[8960,256]{1,0:T(8,128)(2,1)}, u32[]{:S(2)}) copy-start(bf16[8960,256]{1,0:T(8,128)(2,1)} %shard_map.93) | copy-start | bytes 13762564
  58.4 10.1 %collective-permute-start.7 = (bf16[64,1792]{1,0:T(8,128)(2,1)S(1)}, bf16[64,1792]{1,0:T(8,128)(2,1)S(1)}, u32[]{:S(2)}, u32[]{:S(2)}) collective-permute-start(bf16[64,1792]{1,0:T(8,128)(2,1)S(1)} %get-tuple-element.31), channel_id=1, source_target_pairs={{0,2},{1,3},{2,0},{3,1},{4,6},{5,7},{6,4},{7,5},{8,10},{9,11},{10,... | collective-permute-start | bytes 688136 | tf_op jit(solution)/shard_map/ppermute | solution.py:18
  61.5 9.7 %collective-permute-start.8 = (bf16[64,1792]{1,0:T(8,128)(2,1)S(1)}, bf16[64,1792]{1,0:T(8,128)(2,1)S(1)}, u32[]{:S(2)}, u32[]{:S(2)}) collective-permute-start(bf16[64,1792]{1,0:T(8,128)(2,1)S(1)} %get-tuple-element.32), channel_id=1, source_target_pairs={{0,1},{1,2},{2,3},{3,0},{4,5},{5,6},{6,7},{7,4},{8,9},{9,10},{10,1... | collective-permute-start | bytes 688136 | tf_op jit(solution)/shard_map/ppermute | solution.py:18
  62.1 9.2 %collective-permute-start.9 = (bf16[64,1792]{1,0:T(8,128)(2,1)S(1)}, bf16[64,1792]{1,0:T(8,128)(2,1)S(1)}, u32[]{:S(2)}, u32[]{:S(2)}) collective-permute-start(bf16[64,1792]{1,0:T(8,128)(2,1)S(1)} %get-tuple-element.33), channel_id=1, source_target_pairs={{0,3},{1,0},{2,1},{3,2},{4,7},{5,4},{6,5},{7,6},{8,11},{9,8},{10,9... | collective-permute-start | bytes 688136 | tf_op jit(solution)/shard_map/ppermute | solution.py:18
  71.4 8.7 %collective-permute-start.10 = (bf16[64,1792]{1,0:T(8,128)(2,1)S(1)}, bf16[64,1792]{1,0:T(8,128)(2,1)S(1)}, u32[]{:S(2)}, u32[]{:S(2)}) collective-permute-start(bf16[64,1792]{1,0:T(8,128)(2,1)S(1)} %add_convert_fusion), channel_id=1, source_target_pairs={{3,0},{2,1},{1,2},{0,3},{17,16},{16,17},{19,18},{18,19},{7,4},{6,5... | collective-permute-start | bytes 688136 | tf_op jit(solution)/shard_map/ppermute | solution.py:39
  74.1 6.0 %collective-permute-start.11 = (bf16[64,1792]{1,0:T(8,128)(2,1)S(1)}, bf16[64,1792]{1,0:T(8,128)(2,1)S(1)}, u32[]{:S(2)}, u32[]{:S(2)}) collective-permute-start(bf16[64,1792]{1,0:T(8,128)(2,1)S(1)} %add_convert_fusion), channel_id=1, source_target_pairs={{16,0},{17,1},{18,2},{19,3},{0,16},{1,17},{2,18},{3,19},{20,4},{21... | collective-permute-start | bytes 688136 | tf_op jit(solution)/shard_map/ppermute | solution.py:39
  74.1 7.0 %collective-permute-start.12 = (bf16[64,1792]{1,0:T(8,128)(2,1)S(1)}, bf16[64,1792]{1,0:T(8,128)(2,1)S(1)}, u32[]{:S(2)}, u32[]{:S(2)}) collective-permute-start(bf16[64,1792]{1,0:T(8,128)(2,1)S(1)} %add_convert_fusion), channel_id=1, source_target_pairs={{19,0},{18,1},{17,2},{16,3},{1,16},{0,17},{3,18},{2,19},{23,4},{22... | collective-permute-start | bytes 688136 | tf_op jit(solution)/shard_map/ppermute | solution.py:39
  81.2 62.2 %collective-permute-start.13 = (bf16[8960,256]{1,0:T(8,128)(2,1)S(1)}, bf16[8960,256]{1,0:T(8,128)(2,1)S(1)}, u32[]{:S(2)}, u32[]{:S(2)}) collective-permute-start(bf16[8960,256]{1,0:T(8,128)(2,1)S(1)} %copy-done.1), channel_id=1, source_target_pairs={{1,0},{0,1},{3,2},{2,3},{19,16},{18,17},{17,18},{16,19},{5,4},{4,5... | collective-permute-start | bytes 13762568 | tf_op jit(solution)/shard_map/ppermute | solution.py:39
  143.4 5.2 %copy-start.2 = (bf16[3584,512]{1,0:T(8,128)(2,1)S(1)}, bf16[3584,512]{1,0:T(8,128)(2,1)}, u32[]{:S(2)}) copy-start(bf16[3584,512]{1,0:T(8,128)(2,1)} %shard_map.92) | copy-start | bytes 11010052
  146.3 7.3 %collective-permute-start.15 = (f32[640,1]{1,0:T(8,128)S(1)}, f32[640,1]{1,0:T(8,128)S(1)}, u32[]{:S(2)}, u32[]{:S(2)}) collective-permute-start(f32[640,1]{1,0:T(8,128)S(1)} %get-tuple-element.49), channel_id=1, source_target_pairs={{1,0},{0,1},{3,2},{2,3},{19,16},{18,17},{17,18},{16,19},{5,4},{4,5... | collective-permute-start | bytes 7688 | tf_op jit(solution)/shard_map/ppermute | solution.py:39
  146.5 14.1 %collective-permute-start.14 = (bf16[640,512]{1,0:T(8,128)(2,1)S(1)}, bf16[640,512]{1,0:T(8,128)(2,1)S(1)}, u32[]{:S(2)}, u32[]{:S(2)}) collective-permute-start(bf16[640,512]{1,0:T(8,128)(2,1)S(1)} %get-tuple-element.46), channel_id=1, source_target_pairs={{1,0},{0,1},{3,2},{2,3},{19,16},{18,17},{17,18},{16,19},{5,4},{4,5... | collective-permute-start | bytes 1966088 | tf_op jit(solution)/shard_map/ppermute | solution.py:39
  161.0 10.7 %collective-permute-start.16 = (bf16[640,256]{1,0:T(8,128)(2,1)S(1)}, bf16[640,256]{1,0:T(8,128)(2,1)S(1)}, u32[]{:S(2)}, u32[]{:S(2)}) collective-permute-start(bf16[640,256]{1,0:T(8,128)(2,1)S(1)} %fusion.7.refs_0_), channel_id=1, source_target_pairs={{1,0},{0,1},{3,2},{2,3},{19,16},{18,17},{17,18},{16,19},{5,4},{4,5... | collective-permute-start | bytes 983048 | tf_op jit(solution)/shard_map/ppermute | solution.py:39
  161.1 10.6 %collective-permute-start.17 = (bf16[640,256]{1,0:T(8,128)(2,1)S(1)}, bf16[640,256]{1,0:T(8,128)(2,1)S(1)}, u32[]{:S(2)}, u32[]{:S(2)}) collective-permute-start(bf16[640,256]{1,0:T(8,128)(2,1)S(1)} %fusion.7.refs_0_), channel_id=1, source_target_pairs={{3,0},{2,1},{1,2},{0,3},{17,16},{16,17},{19,18},{18,19},{7,4},{6,5... | collective-permute-start | bytes 983048 | tf_op jit(solution)/shard_map/ppermute | solution.py:39
  163.0 15.3 %collective-permute-start.18 = (bf16[640,256]{1,0:T(8,128)(2,1)S(1)}, bf16[640,256]{1,0:T(8,128)(2,1)S(1)}, u32[]{:S(2)}, u32[]{:S(2)}) collective-permute-start(bf16[640,256]{1,0:T(8,128)(2,1)S(1)} %fusion.7.refs_0_), channel_id=1, source_target_pairs={{0,2},{1,3},{2,0},{3,1},{4,6},{5,7},{6,4},{7,5},{8,10},{9,11},{10,... | collective-permute-start | bytes 983048 | tf_op jit(solution)/shard_map/ppermute | solution.py:18
  216.3 1.9 collective-permute-start.19
  218.3 4.6 %collective-permute-start.20 = (bf16[16,1792]{1,0:T(8,128)(2,1)S(1)}, bf16[16,1792]{1,0:T(8,128)(2,1)S(1)}, u32[]{:S(2)}, u32[]{:S(2)}) collective-permute-start(bf16[16,1792]{1,0:T(8,128)(2,1)S(1)} %get-tuple-element.59), channel_id=1, source_target_pairs={{0,3},{1,0},{2,1},{3,2},{4,7},{5,4},{6,5},{7,6},{8,11},{9,8},{10,9... | collective-permute-start | bytes 172040 | tf_op jit(solution)/shard_map/ppermute | solution.py:18
  220.1 5.9 %collective-permute-start.21 = (bf16[16,1792]{1,0:T(8,128)(2,1)S(1)}, bf16[16,1792]{1,0:T(8,128)(2,1)S(1)}, u32[]{:S(2)}, u32[]{:S(2)}) collective-permute-start(bf16[16,1792]{1,0:T(8,128)(2,1)S(1)} %get-tuple-element.58), channel_id=1, source_target_pairs={{0,2},{1,3},{2,0},{3,1},{4,6},{5,7},{6,4},{7,5},{8,10},{9,11},{10,... | collective-permute-start | bytes 172040 | tf_op jit(solution)/shard_map/ppermute | solution.py:18
  220.3 6.0 %collective-permute-start.22 = (bf16[16,1792]{1,0:T(8,128)(2,1)S(1)}, bf16[16,1792]{1,0:T(8,128)(2,1)S(1)}, u32[]{:S(2)}, u32[]{:S(2)}) collective-permute-start(bf16[16,1792]{1,0:T(8,128)(2,1)S(1)} %get-tuple-element.56), channel_id=1, source_target_pairs={{0,1},{1,2},{2,3},{3,0},{4,5},{5,6},{6,7},{7,4},{8,9},{9,10},{10,1... | collective-permute-start | bytes 172040 | tf_op jit(solution)/shard_map/ppermute | solution.py:18
